TPU v7x, 32 devices: a whole 2x2x4 slice. The times are simulated.
32 devices in a mesh: dom: 32 (over z, y, x, core).
Axes of the slice: x: 2, y: 2, z: 4, core: 2. Of those that a mesh axis runs over, the one named last changes fastest.
Arguments:
- right_side: float32 [3, 8, 24576], P(None, None, 'dom')
- mass_diag: float32 [24576], P('dom'), may hold values from 0.3 to 3
- precond_blocks: float32 [3, 3, 24576], P(None, None, 'dom'), as said below
- connectivity: int32 [10, 16384], P(None, 'dom'), may hold values from 0 to 1023, as said below
- shape_grads: bfloat16 [4, 3, 10, 16384], P(None, None, None, 'dom'), may hold values from -3 to 3
- quad_weight: float32 [4, 16384], P(None, 'dom'), may hold values from 0.05 to 0.15
- lame_moduli: float32 [2, 16384], P(None, 'dom'), may hold values from 0.2 to 5
- elem_count: int32 [32], P('dom'), may hold values from 64 to 512, as said below
- boundary_ids: int32 [8192], P('dom'), may hold values from 0 to 767, as said below
Outputs:
- solution: float32 [3, 8, 24576], P(None, None, 'dom')
- residual: float32 [3, 8, 24576], P(None, None, 'dom')
Inputs may be any that keep to these rules, and one draw needn't show every extreme that they name: `connectivity`: slots below 768 name the partition's own nodes; slot 768 + j names the partition's j-th ghost node. The ten slots of a live element are distinct. Slots of elements beyond the partition's live count are 0. The first elem_count[p] of partition p's 512 element slots are live; some partition is full. `boundary_ids`: each partition's 256 entries are distinct own-node numbers; entry j of ghost block k lists the node that partition p - o_k holds in its ghost slot j. `precond_blocks`: each node's 3x3 block is symmetric positive definite.
All inputs are finite; a program needn't handle non-finite values.
Results may differ from a plain program's by a relative error of at most 0.00055.
Values sent between devices are 32-bit elements; how exact they have to be, the bound alone decides.
No kernel may reach another device: no remote copies, remote signals or barrier semaphores. Data moves between devices by JAX's collectives and lax.ppermute only.
A program may use at most 64 MiB of HBM per device.

v0:
```python
import jax
import jax.numpy as jnp
from jax import lax
from jax.sharding import PartitionSpec as P

ITERS = 2


NEIGHBOUR_SHIFTS = (1, -1, 4, -4, 16, -16)
NEIGHBOUR_SHARES = (4, 4, 3, 3, 1, 1)


def passed_along(block, axis, distance):
    devices = range(lax.axis_size(axis))
    route = [(i - distance, i) for i in devices if i - distance in devices]
    return lax.ppermute(block, axis, route)


def neighbour_blocks(ghost_count):
    share_unit = ghost_count // 16
    listed = []
    first_slot = 0
    for offset, share in zip(NEIGHBOUR_SHIFTS, NEIGHBOUR_SHARES):
        listed.append((offset, first_slot, share * share_unit))
        first_slot = first_slot + share * share_unit
    return listed


def element_forces(nodal_values, shape_grads, quad_weight, lame_moduli):
    shape_float = shape_grads.astype(jnp.float32)
    gradient = nodal_values[None, :, None, :, 0, :] * shape_float[:, None, :, None, 0, :]
    for node_index in range(1, 10):
        gradient = (
            gradient
            + nodal_values[None, :, None, :, node_index, :]
            * shape_float[:, None, :, None, node_index, :]
        )
    dilation = gradient[:, 0, 0] + gradient[:, 1, 1] + gradient[:, 2, 2]
    identity = jnp.eye(3, dtype=jnp.float32)
    stress = lame_moduli[1] * (gradient + jnp.swapaxes(gradient, 1, 2))
    stress = (
        stress + identity[None, :, :, None, None] * (lame_moduli[0] * dilation)[:, None, None, :, :]
    )
    stress = stress * quad_weight[:, None, None, None, :]
    forces = shape_float[0, 0][None, None, :, :] * stress[0, :, 0][:, :, None, :]
    for quad_point in range(4):
        for deriv_index in range(3):
            if quad_point + deriv_index > 0:
                forces = (
                    forces
                    + shape_float[quad_point, deriv_index][None, None, :, :]
                    * stress[quad_point, :, deriv_index][:, :, None, :]
                )
    return forces


def precondition(blocks, vector):
    case_count = vector.shape[0] // 3
    components = vector.reshape(3, case_count, vector.shape[1])
    result = (
        blocks[:, 0][:, None, :] * components[0][None]
        + blocks[:, 1][:, None, :] * components[1][None]
        + blocks[:, 2][:, None, :] * components[2][None]
    )
    return result.reshape(vector.shape)


def per_row(values):
    return jnp.tile(values, 3)[:, None]


def local(
    right_side,
    mass_diag,
    precond_blocks,
    connectivity,
    shape_grads,
    quad_weight,
    lame_moduli,
    elem_count,
    boundary_ids,
):
    case_count = right_side.shape[1]
    own_nodes = right_side.shape[2]
    row_count = 3 * case_count
    ghost_count = boundary_ids.shape[0]
    slot_count = own_nodes + ghost_count
    layout = neighbour_blocks(ghost_count)
    live_count = elem_count[0]
    block_size = min(512, connectivity.shape[1])
    block_total = connectivity.shape[1] // block_size

    def inner_product(left, right):
        return jnp.sum((left * right).reshape(3, case_count, own_nodes), axis=(0, 2))

    flat_rhs = right_side.reshape(row_count, own_nodes)
    residual = flat_rhs
    solution = jnp.zeros((row_count, own_nodes), jnp.float32)
    search = precondition(precond_blocks, residual)

    def norm_sum(residual_now, search_now):
        return lax.psum(inner_product(residual_now, search_now), "dom")

    direction = search
    energy = norm_sum(residual, search)
    for iteration in range(ITERS):
        pieces = []
        for fetch_offset, fetch_first_slot, fetch_width in layout:
            picked = direction[:, boundary_ids[fetch_first_slot : fetch_first_slot + fetch_width]]
            pieces.append(passed_along(picked, "dom", -fetch_offset))
        vector_ext = jnp.concatenate([direction, jnp.concatenate(pieces, axis=1)], axis=1)

        def visit_block(block_index, accumulated):
            first_slot = block_index * block_size
            nodal_values = jnp.take(vector_ext, connectivity, axis=1).reshape(
                3, case_count, 10, block_size
            )
            forces = element_forces(nodal_values, shape_grads, quad_weight, lame_moduli)
            is_live = first_slot + lax.iota(jnp.int32, block_size) < live_count
            forces = jnp.where(is_live, forces, 0.0).reshape(row_count, 10, block_size)
            return accumulated.at[:, connectivity].add(forces)

        accumulated = lax.fori_loop(
            0, block_total, visit_block, jnp.zeros((row_count, slot_count), jnp.float32)
        )
        result = accumulated[:, :own_nodes] + mass_diag[None, :] * vector_ext[:, :own_nodes]
        for offset, first_slot, width in layout:
            sent = accumulated[:, own_nodes + first_slot : own_nodes + first_slot + width]
            returned = passed_along(sent, "dom", offset)
            result = result.at[:, boundary_ids[first_slot : first_slot + width]].add(returned)
        step_size = energy / lax.psum(inner_product(direction, result), "dom")
        solution = solution + per_row(step_size) * direction
        residual = residual - per_row(step_size) * result
        if iteration + 1 < ITERS:
            search = precondition(precond_blocks, residual)
            fresh_energy = norm_sum(residual, search)
            direction = search + per_row(fresh_energy / energy) * direction
            energy = fresh_energy
    return (solution.reshape(3, case_count, own_nodes), residual.reshape(3, case_count, own_nodes))


def solution(mesh):
    return jax.shard_map(
        local,
        mesh=mesh,
        in_specs=(
            P(None, None, "dom"),
            P("dom"),
            P(None, None, "dom"),
            P(None, "dom"),
            P(None, None, None, "dom"),
            P(None, "dom"),
            P(None, "dom"),
            P("dom"),
            P("dom"),
        ),
        out_specs=(P(None, None, "dom"), P(None, None, "dom")),
        check_vma=False,
    )
```

profile of v0, /device:TPU:0, one launch (start us, length us, event | category | flops | bytes accessed | tf_op | source)
XLA Modules:
  0.0 398.7 jit_solution(11970063024352740400)
XLA Ops:
  1.5 0.9 fusion.44
  3.2 1.6 multiply_reduce_fusion.3
  5.6 1.3 collective-permute-start.4
  7.5 5.9 %collective-permute-start.5 = (f32[24,16]{0,1:T(8,128)S(1)}, f32[24,16]{0,1:T(8,128)S(1)}, u32[]{:S(2)}, u32[]{:S(2)}) collective-permute-start(f32[24,16]{0,1:T(8,128)S(1)} %bitcast.247), channel_id=1, source_target_pairs={{0,16},{1,17},{2,18},{3,19},{4,20},{5,21},{6,22},{7,23},{8,24},{9,... | collective-permute-start | bytes 4616 | tf_op jit(solution)/shard_map/ppermute | solution.py:16
  14.9 1.3 collective-permute-start.2
  16.8 5.0 %collective-permute-start.3 = (f32[24,48]{0,1:T(8,128)S(1)}, f32[24,48]{0,1:T(8,128)S(1)}, u32[]{:S(2)}, u32[]{:S(2)}) collective-permute-start(f32[24,48]{0,1:T(8,128)S(1)} %bitcast.251), channel_id=1, source_target_pairs={{0,4},{1,5},{2,6},{3,7},{4,8},{5,9},{6,10},{7,11},{8,12},{9,13},{1... | collective-permute-start | bytes 13832 | tf_op jit(solution)/shard_map/ppermute | solution.py:16
  23.3 1.3 collective-permute-start
  24.6 1.4 compare_and_fusion
  26.7 0.9 copy_convert_fusion
  35.0 3.0 collective-permute-start.1
  39.0 15.9 %gather_fusion.12 = f32[5120,24]{1,0:T(8,128)S(1)} fusion(f32[24,1024]{0,1:T(8,128)S(1)} %constant_dynamic-update-slice_fusion, s32[5120]{0:T(1024)} %broadcast_clamp_fusion), kind=kCustom, calls=%fused_computation.clone | custom fusion | bytes 1003520 | tf_op jit(solution)/shard_map/while/body/eval_jaxpr/jit(_take)/gather | solution.py:115
  56.6 1.3 multiply_add_fusion.1
  58.0 0.9 add_multiply_fusion.1
  59.2 0.9 copy.387
  60.1 0.9 copy.386
  61.8 0.8 copy.384
  62.6 0.9 copy.383
  66.0 0.9 copy.379
  67.7 9.9 %add_select_fusion.1 = f32[24,10,512]{0,2,1:T(8,128)S(1)} fusion(f32[24,512]{0,1:T(8,128)S(1)} %copy.388, f32[10,512]{1,0:T(8,128)} %get-tuple-element.122, f32[24,512]{0,1:T(8,128)} %copy.387, f32[10,512]{1,0:T(8,128)} %get-tuple-element.123, f32[24,512]{0,1:T(8,128)} %copy.386, f32[10,512]{1,0:T(8,128)} %get-tuple-element.124, f32[24,512]{0,1:T(8,128)} %copy.385, ...), kind=kLoop, calls=%fused_computation.29 | loop fusion | flops 2949120 | bytes 1327616 | tf_op jit(solution)/shard_map/while/body/eval_jaxpr/jit(_where)/select_n | solution.py:120
  77.6 34.7 %scatter_custom_fusion = f32[24,1024]{0,1:T(8,128)S(1)} fusion(s32[5120]{0:T(1024)} %copy-done.48, f32[5120,24]{1,0:T(8,128)S(1)} %bitcast.239, f32[]{:T(128)} %constant.14.clone.1), kind=kCustom, calls=%fused_computation.43 | custom fusion | flops 122880 | bytes 98816 | tf_op jit(solution)/shard_map/while/body/eval_jaxpr/scatter-add | solution.py:121
  112.4 1.7 collective-permute-start.6
  114.1 1.3 collective-permute-start.11
  115.4 9.0 %collective-permute-start.10 = (f32[24,16]{0,1:T(8,128)S(1)}, f32[24,16]{0,1:T(8,128)S(1)}, u32[]{:S(2)}, u32[]{:S(2)}) collective-permute-start(f32[24,16]{0,1:T(8,128)S(1)} %get-tuple-element.96), channel_id=1, source_target_pairs={{0,16},{1,17},{2,18},{3,19},{4,20},{5,21},{6,22},{7,23},{8,24},{9,... | collective-permute-start | bytes 4616 | tf_op jit(solution)/shard_map/ppermute | solution.py:16
  124.5 1.3 collective-permute-start.9
  125.8 4.5 %collective-permute-start.8 = (f32[24,48]{0,1:T(8,128)S(1)}, f32[24,48]{0,1:T(8,128)S(1)}, u32[]{:S(2)}, u32[]{:S(2)}) collective-permute-start(f32[24,48]{0,1:T(8,128)S(1)} %get-tuple-element.98), channel_id=1, source_target_pairs={{0,4},{1,5},{2,6},{3,7},{4,8},{5,9},{6,10},{7,11},{8,12},{9,13},{1... | collective-permute-start | bytes 13832 | tf_op jit(solution)/shard_map/ppermute | solution.py:16
  130.3 1.4 collective-permute-start.7
  131.8 0.9 slice_add_fusion.1
  132.6 1.2 scatter_custom_fusion.1
  133.8 1.2 scatter_custom_fusion.2
  135.1 1.1 scatter_custom_fusion.3
  136.2 1.1 scatter_custom_fusion.4
  137.3 1.0 scatter_custom_fusion.5
  138.3 1.0 scatter_custom_fusion.6
  139.6 44.6 %all-reduce = (f32[8]{0:T(128)S(1)}, f32[8]{0:T(128)S(1)}) all-reduce(f32[8]{0:T(128)S(1)} %copy-done.75, f32[8]{0:T(128)S(1)} %reduce_sum.47), channel_id=1, replica_groups=mesh['dom'=32] {'dom'}, use_global_device_ids=true, to_apply=%region_1.0 | all-reduce | flops 16 | bytes 128 | tf_op jit(solution)/shard_map/psum | solution.py:102
  184.8 40.0 %psum.30 = f32[8]{0:T(128)S(1)} all-reduce(f32[8]{0:T(128)S(1)} %reduce_sum.63), channel_id=1, replica_groups=mesh['dom'=32] {'dom'}, use_global_device_ids=true, to_apply=%region_14.16 | all-reduce | flops 8 | bytes 64 | tf_op jit(solution)/shard_map/psum | solution.py:102
  226.3 1.3 collective-permute-start.12
  231.1 1.3 collective-permute-start.16
  232.4 6.2 %collective-permute-start.17 = (f32[24,16]{0,1:T(8,128)S(1)}, f32[24,16]{0,1:T(8,128)S(1)}, u32[]{:S(2)}, u32[]{:S(2)}) collective-permute-start(f32[24,16]{0,1:T(8,128)S(1)} %bitcast.249), channel_id=1, source_target_pairs={{0,16},{1,17},{2,18},{3,19},{4,20},{5,21},{6,22},{7,23},{8,24},{9,... | collective-permute-start | bytes 4616 | tf_op jit(solution)/shard_map/ppermute | solution.py:16
  238.6 1.3 collective-permute-start.14
  239.9 4.7 %collective-permute-start.15 = (f32[24,48]{0,1:T(8,128)S(1)}, f32[24,48]{0,1:T(8,128)S(1)}, u32[]{:S(2)}, u32[]{:S(2)}) collective-permute-start(f32[24,48]{0,1:T(8,128)S(1)} %bitcast.253), channel_id=1, source_target_pairs={{0,4},{1,5},{2,6},{3,7},{4,8},{5,9},{6,10},{7,11},{8,12},{9,13},{1... | collective-permute-start | bytes 13832 | tf_op jit(solution)/shard_map/ppermute | solution.py:16
  244.6 1.6 collective-permute-start.13
  247.1 17.7 %gather_fusion.13 = f32[5120,24]{1,0:T(8,128)} fusion(f32[24,1024]{0,1:T(8,128)S(1)} %constant_dynamic-update-slice_fusion.7, s32[5120]{0:T(1024)S(1)} %copy-done.21), kind=kCustom, calls=%fused_computation.1.clone | custom fusion | bytes 1003520 | tf_op jit(solution)/shard_map/while/body/eval_jaxpr/jit(_take)/gather | solution.py:115
  265.0 2.5 copy.394
  269.2 0.9 copy.406
  270.1 0.9 copy.405
  271.8 0.8 copy.403
  272.6 0.9 copy.402
  276.0 0.9 copy.398
  278.6 9.9 %add_select_fusion = f32[24,10,512]{0,2,1:T(8,128)S(1)} fusion(f32[24,512]{0,1:T(8,128)} %copy.406, f32[24,512]{0,1:T(8,128)} %copy.405, f32[24,512]{0,1:T(8,128)} %copy.404, f32[24,512]{0,1:T(8,128)} %copy.403, f32[24,512]{0,1:T(8,128)} %copy.402, f32[24,512]{0,1:T(8,128)} %copy.401, f32[24,512]{0,1:T(8,128)} %copy.400, f32[24,512]{0,1:T(8,128)} %copy.399, ...), kind=kLoop, calls=%fused_computation.28 | loop fusion | flops 2949120 | bytes 1327616 | tf_op jit(solution)/shard_map/while/body/eval_jaxpr/jit(_where)/select_n | solution.py:120
  288.5 35.4 %scatter_custom_fusion.7 = f32[24,1024]{0,1:T(8,128)} fusion(s32[5120]{0:T(1024)} %copy-done.48, f32[5120,24]{1,0:T(8,128)S(1)} %bitcast.238, f32[]{:T(128)} %constant.14.clone.1), kind=kCustom, calls=%fused_computation.41 | custom fusion | flops 122880 | bytes 98816 | tf_op jit(solution)/shard_map/while/body/eval_jaxpr/scatter-add | solution.py:121
  325.6 2.6 collective-permute-start.18
  328.9 1.3 collective-permute-start.23
  330.2 7.1 %collective-permute-start.22 = (f32[24,16]{0,1:T(8,128)S(1)}, f32[24,16]{0,1:T(8,128)S(1)}, u32[]{:S(2)}, u32[]{:S(2)}) collective-permute-start(f32[24,16]{0,1:T(8,128)S(1)} %get-tuple-element.90), channel_id=1, source_target_pairs={{0,16},{1,17},{2,18},{3,19},{4,20},{5,21},{6,22},{7,23},{8,24},{9,... | collective-permute-start | bytes 4616 | tf_op jit(solution)/shard_map/ppermute | solution.py:16
  337.4 1.3 collective-permute-start.21
  338.7 5.4 %collective-permute-start.20 = (f32[24,48]{0,1:T(8,128)S(1)}, f32[24,48]{0,1:T(8,128)S(1)}, u32[]{:S(2)}, u32[]{:S(2)}) collective-permute-start(f32[24,48]{0,1:T(8,128)S(1)} %get-tuple-element.92), channel_id=1, source_target_pairs={{0,4},{1,5},{2,6},{3,7},{4,8},{5,9},{6,10},{7,11},{8,12},{9,13},{1... | collective-permute-start | bytes 13832 | tf_op jit(solution)/shard_map/ppermute | solution.py:16
  344.1 1.3 collective-permute-start.19
  345.4 1.2 slice_add_fusion
  346.6 1.2 scatter_custom_fusion.8
  347.8 1.2 scatter_custom_fusion.9
  349.0 1.1 scatter_custom_fusion.10
  350.1 1.1 scatter_custom_fusion.11
  351.3 1.0 scatter_custom_fusion.12
  352.3 1.0 scatter_custom_fusion.13
  353.6 43.5 %psum.31 = f32[8]{0:T(128)S(1)} all-reduce(f32[8]{0:T(128)S(1)} %reduce_sum.66), channel_id=1, replica_groups=mesh['dom'=32] {'dom'}, use_global_device_ids=true, to_apply=%region_24.26 | all-reduce | flops 8 | bytes 64 | tf_op jit(solution)/shard_map/psum | solution.py:131
  (285 shorter events, 38.3 us)
Async XLA Ops:
  0.6 28.8 %copy-start.63 = (f32[2,512]{1,0:T(2,128)S(1)}, f32[2,512]{1,0:T(2,128)}, u32[]{:S(2)}) copy-start(f32[2,512]{1,0:T(2,128)} %param.17) | copy-start | bytes 12292
  1.5 27.9 %copy-start.69 = (s32[16]{0:T(128)}, s32[16]{0:T(128)S(1)}, u32[]{:S(2)}) copy-start(s32[16]{0:T(128)S(1)} %get-tuple-element.156) | copy-start | bytes 196
  1.5 27.9 %copy-start.70 = (s32[16]{0:T(128)}, s32[16]{0:T(128)S(1)}, u32[]{:S(2)}) copy-start(s32[16]{0:T(128)S(1)} %get-tuple-element.157) | copy-start | bytes 196
  2.4 182.1 %copy-start.40 = (f32[3,1,768]{2,0,1:T(4,128)}, f32[3,1,768]{2,0,1:T(4,128)S(1)}, u32[]{:S(2)}) copy-start(f32[3,1,768]{2,0,1:T(4,128)S(1)} %copy.435) | copy-start | bytes 27652
  5.1 22.8 %copy-start.57 = (s32[1024]{0:T(1024)}, s32[1024]{0:T(1024)S(1)}, u32[]{:S(2)}) copy-start(s32[1024]{0:T(1024)S(1)} %get-tuple-element.177) | copy-start | bytes 12292
  5.6 33.3 %collective-permute-start.4 = (f32[24,16]{0,1:T(8,128)S(1)}, f32[24,16]{0,1:T(8,128)S(1)}, u32[]{:S(2)}, u32[]{:S(2)}) collective-permute-start(f32[24,16]{0,1:T(8,128)S(1)} %bitcast.248), channel_id=1, source_target_pairs={{16,0},{17,1},{18,2},{19,3},{20,4},{21,5},{22,6},{23,7},{24,8},{25... | collective-permute-start | bytes 4616 | tf_op jit(solution)/shard_map/ppermute | solution.py:16
  7.5 31.4 %collective-permute-start.5 = (f32[24,16]{0,1:T(8,128)S(1)}, f32[24,16]{0,1:T(8,128)S(1)}, u32[]{:S(2)}, u32[]{:S(2)}) collective-permute-start(f32[24,16]{0,1:T(8,128)S(1)} %bitcast.247), channel_id=1, source_target_pairs={{0,16},{1,17},{2,18},{3,19},{4,20},{5,21},{6,22},{7,23},{8,24},{9,... | collective-permute-start | bytes 4616 | tf_op jit(solution)/shard_map/ppermute | solution.py:16
  14.3 15.1 %copy-start.71 = (s32[48]{0:T(128)}, s32[48]{0:T(128)S(1)}, u32[]{:S(2)}) copy-start(s32[48]{0:T(128)S(1)} %get-tuple-element.158) | copy-start | bytes 580
  14.3 15.1 %copy-start.72 = (s32[48]{0:T(128)}, s32[48]{0:T(128)S(1)}, u32[]{:S(2)}) copy-start(s32[48]{0:T(128)S(1)} %get-tuple-element.159) | copy-start | bytes 580
  14.3 13.6 %copy-start.59 = (s32[1024]{0:T(1024)}, s32[1024]{0:T(1024)S(1)}, u32[]{:S(2)}) copy-start(s32[1024]{0:T(1024)S(1)} %get-tuple-element.179) | copy-start | bytes 12292
  14.3 13.6 %copy-start.60 = (s32[1024]{0:T(1024)}, s32[1024]{0:T(1024)S(1)}, u32[]{:S(2)}) copy-start(s32[1024]{0:T(1024)S(1)} %get-tuple-element.178) | copy-start | bytes 12292
  14.9 24.0 %collective-permute-start.2 = (f32[24,48]{0,1:T(8,128)S(1)}, f32[24,48]{0,1:T(8,128)S(1)}, u32[]{:S(2)}, u32[]{:S(2)}) collective-permute-start(f32[24,48]{0,1:T(8,128)S(1)} %bitcast.252), channel_id=1, source_target_pairs={{4,0},{5,1},{6,2},{7,3},{8,4},{9,5},{10,6},{11,7},{12,8},{13,9},{1... | collective-permute-start | bytes 13832 | tf_op jit(solution)/shard_map/ppermute | solution.py:16
  16.8 22.1 %collective-permute-start.3 = (f32[24,48]{0,1:T(8,128)S(1)}, f32[24,48]{0,1:T(8,128)S(1)}, u32[]{:S(2)}, u32[]{:S(2)}) collective-permute-start(f32[24,48]{0,1:T(8,128)S(1)} %bitcast.251), channel_id=1, source_target_pairs={{0,4},{1,5},{2,6},{3,7},{4,8},{5,9},{6,10},{7,11},{8,12},{9,13},{1... | collective-permute-start | bytes 13832 | tf_op jit(solution)/shard_map/ppermute | solution.py:16
  22.7 16.3 %copy-start.61 = (s32[1024]{0:T(1024)}, s32[1024]{0:T(1024)S(1)}, u32[]{:S(2)}) copy-start(s32[1024]{0:T(1024)S(1)} %get-tuple-element.174) | copy-start | bytes 12292
  23.3 11.7 %collective-permute-start = (f32[24,64]{0,1:T(8,128)S(1)}, f32[24,64]{0,1:T(8,128)S(1)}, u32[]{:S(2)}, u32[]{:S(2)}) collective-permute-start(f32[24,64]{0,1:T(8,128)S(1)} %bitcast.255), channel_id=1, source_target_pairs={{1,0},{2,1},{3,2},{4,3},{5,4},{6,5},{7,6},{8,7},{9,8},{10,9},{11,1... | collective-permute-start | bytes 18440 | tf_op jit(solution)/shard_map/ppermute | solution.py:16
  30.0 9.0 %copy-start.48 = (s32[5120]{0:T(1024)}, s32[5120]{0:T(1024)S(1)}, u32[]{:S(2)}) copy-start(s32[5120]{0:T(1024)S(1)} %reshape.319) | copy-start | bytes 61444
  35.0 3.9 collective-permute-start.1
  112.3 27.3 %copy-start.75 = (f32[8]{0:T(128)S(1)}, f32[8]{0:T(128)}, u32[]{:S(2)}) copy-start(f32[8]{0:T(128)} %get-tuple-element.143) | copy-start | bytes 100
  112.4 72.0 %copy-start.20 = (f32[3,8,768]{2,1,0:T(8,128)S(1)}, f32[3,8,768]{2,1,0:T(8,128)}, u32[]{:S(2)}) copy-start(f32[3,8,768]{2,1,0:T(8,128)} %param.11) | copy-start | bytes 221188
  112.4 17.9 %collective-permute-start.6 = (f32[24,64]{0,1:T(8,128)S(1)}, f32[24,64]{0,1:T(8,128)S(1)}, u32[]{:S(2)}, u32[]{:S(2)}) collective-permute-start(f32[24,64]{0,1:T(8,128)S(1)} %get-tuple-element.100), channel_id=1, source_target_pairs={{0,1},{1,2},{2,3},{3,4},{4,5},{5,6},{6,7},{7,8},{8,9},{9,10},{10,1... | collective-permute-start | bytes 18440 | tf_op jit(solution)/shard_map/ppermute | solution.py:16
  114.1 24.2 %collective-permute-start.11 = (f32[24,16]{0,1:T(8,128)S(1)}, f32[24,16]{0,1:T(8,128)S(1)}, u32[]{:S(2)}, u32[]{:S(2)}) collective-permute-start(f32[24,16]{0,1:T(8,128)S(1)} %get-tuple-element.95), channel_id=1, source_target_pairs={{16,0},{17,1},{18,2},{19,3},{20,4},{21,5},{22,6},{23,7},{24,8},{25... | collective-permute-start | bytes 4616 | tf_op jit(solution)/shard_map/ppermute | solution.py:16
  115.4 21.9 %collective-permute-start.10 = (f32[24,16]{0,1:T(8,128)S(1)}, f32[24,16]{0,1:T(8,128)S(1)}, u32[]{:S(2)}, u32[]{:S(2)}) collective-permute-start(f32[24,16]{0,1:T(8,128)S(1)} %get-tuple-element.96), channel_id=1, source_target_pairs={{0,16},{1,17},{2,18},{3,19},{4,20},{5,21},{6,22},{7,23},{8,24},{9,... | collective-permute-start | bytes 4616 | tf_op jit(solution)/shard_map/ppermute | solution.py:16
  124.5 11.7 %collective-permute-start.9 = (f32[24,48]{0,1:T(8,128)S(1)}, f32[24,48]{0,1:T(8,128)S(1)}, u32[]{:S(2)}, u32[]{:S(2)}) collective-permute-start(f32[24,48]{0,1:T(8,128)S(1)} %get-tuple-element.97), channel_id=1, source_target_pairs={{4,0},{5,1},{6,2},{7,3},{8,4},{9,5},{10,6},{11,7},{12,8},{13,9},{1... | collective-permute-start | bytes 13832 | tf_op jit(solution)/shard_map/ppermute | solution.py:16
  125.8 9.3 %collective-permute-start.8 = (f32[24,48]{0,1:T(8,128)S(1)}, f32[24,48]{0,1:T(8,128)S(1)}, u32[]{:S(2)}, u32[]{:S(2)}) collective-permute-start(f32[24,48]{0,1:T(8,128)S(1)} %get-tuple-element.98), channel_id=1, source_target_pairs={{0,4},{1,5},{2,6},{3,7},{4,8},{5,9},{6,10},{7,11},{8,12},{9,13},{1... | collective-permute-start | bytes 13832 | tf_op jit(solution)/shard_map/ppermute | solution.py:16
  130.3 54.2 %copy-start.43 = (f32[3,768]{1,0:T(4,128)S(1)}, f32[3,768]{1,0:T(4,128)}, u32[]{:S(2)}) copy-start(f32[3,768]{1,0:T(4,128)} %copy-done.42) | copy-start | bytes 27652
  130.3 54.2 %copy-start.46 = (f32[3,768]{1,0:T(4,128)S(1)}, f32[3,768]{1,0:T(4,128)}, u32[]{:S(2)}) copy-start(f32[3,768]{1,0:T(4,128)} %copy-done.45) | copy-start | bytes 27652
  130.3 3.5 collective-permute-start.7
  138.3 108.8 %copy-start.21 = (s32[5120]{0:T(1024)S(1)}, s32[5120]{0:T(1024)}, u32[]{:S(2)}) copy-start(s32[5120]{0:T(1024)} %broadcast_clamp_fusion) | copy-start | bytes 61444
  184.3 46.8 %copy-start.65 = (f32[8]{0:T(128)}, f32[8]{0:T(128)S(1)}, u32[]{:S(2)}) copy-start(f32[8]{0:T(128)S(1)} %div.9) | copy-start | bytes 100
  184.5 40.9 %copy-start.34 = (f32[8,768]{1,0:T(8,128)}, f32[8,768]{1,0:T(8,128)S(1)}, u32[]{:S(2)}) copy-start(f32[8,768]{1,0:T(8,128)S(1)} %get-tuple-element.145) | copy-start | bytes 73732
  184.5 40.9 %copy-start.36 = (f32[8,768]{1,0:T(8,128)}, f32[8,768]{1,0:T(8,128)S(1)}, u32[]{:S(2)}) copy-start(f32[8,768]{1,0:T(8,128)S(1)} %get-tuple-element.146) | copy-start | bytes 73732
  184.5 40.8 %copy-start.38 = (f32[8,768]{1,0:T(8,128)}, f32[8,768]{1,0:T(8,128)S(1)}, u32[]{:S(2)}) copy-start(f32[8,768]{1,0:T(8,128)S(1)} %get-tuple-element.147) | copy-start | bytes 73732
  226.3 18.3 %collective-permute-start.12 = (f32[24,64]{0,1:T(8,128)S(1)}, f32[24,64]{0,1:T(8,128)S(1)}, u32[]{:S(2)}, u32[]{:S(2)}) collective-permute-start(f32[24,64]{0,1:T(8,128)S(1)} %bitcast.256), channel_id=1, source_target_pairs={{1,0},{2,1},{3,2},{4,3},{5,4},{6,5},{7,6},{8,7},{9,8},{10,9},{11,1... | collective-permute-start | bytes 18440 | tf_op jit(solution)/shard_map/ppermute | solution.py:16
  231.1 15.9 %collective-permute-start.16 = (f32[24,16]{0,1:T(8,128)S(1)}, f32[24,16]{0,1:T(8,128)S(1)}, u32[]{:S(2)}, u32[]{:S(2)}) collective-permute-start(f32[24,16]{0,1:T(8,128)S(1)} %bitcast.250), channel_id=1, source_target_pairs={{16,0},{17,1},{18,2},{19,3},{20,4},{21,5},{22,6},{23,7},{24,8},{25... | collective-permute-start | bytes 4616 | tf_op jit(solution)/shard_map/ppermute | solution.py:16
  232.4 14.7 %collective-permute-start.17 = (f32[24,16]{0,1:T(8,128)S(1)}, f32[24,16]{0,1:T(8,128)S(1)}, u32[]{:S(2)}, u32[]{:S(2)}) collective-permute-start(f32[24,16]{0,1:T(8,128)S(1)} %bitcast.249), channel_id=1, source_target_pairs={{0,16},{1,17},{2,18},{3,19},{4,20},{5,21},{6,22},{7,23},{8,24},{9,... | collective-permute-start | bytes 4616 | tf_op jit(solution)/shard_map/ppermute | solution.py:16
  238.6 8.4 %collective-permute-start.14 = (f32[24,48]{0,1:T(8,128)S(1)}, f32[24,48]{0,1:T(8,128)S(1)}, u32[]{:S(2)}, u32[]{:S(2)}) collective-permute-start(f32[24,48]{0,1:T(8,128)S(1)} %bitcast.254), channel_id=1, source_target_pairs={{4,0},{5,1},{6,2},{7,3},{8,4},{9,5},{10,6},{11,7},{12,8},{13,9},{1... | collective-permute-start | bytes 13832 | tf_op jit(solution)/shard_map/ppermute | solution.py:16
  239.9 7.1 %collective-permute-start.15 = (f32[24,48]{0,1:T(8,128)S(1)}, f32[24,48]{0,1:T(8,128)S(1)}, u32[]{:S(2)}, u32[]{:S(2)}) collective-permute-start(f32[24,48]{0,1:T(8,128)S(1)} %bitcast.253), channel_id=1, source_target_pairs={{0,4},{1,5},{2,6},{3,7},{4,8},{5,9},{6,10},{7,11},{8,12},{9,13},{1... | collective-permute-start | bytes 13832 | tf_op jit(solution)/shard_map/ppermute | solution.py:16
  244.6 2.4 collective-permute-start.13
  269.0 9.6 %copy-start.22 = (f32[10,512]{1,0:T(8,128)S(1)}, f32[10,512]{1,0:T(8,128)}, u32[]{:S(2)}) copy-start(f32[10,512]{1,0:T(8,128)} %get-tuple-element.121) | copy-start | bytes 61444
  269.0 9.6 %copy-start.23 = (f32[10,512]{1,0:T(8,128)S(1)}, f32[10,512]{1,0:T(8,128)}, u32[]{:S(2)}) copy-start(f32[10,512]{1,0:T(8,128)} %get-tuple-element.122) | copy-start | bytes 61444
  269.0 9.5 %copy-start.24 = (f32[10,512]{1,0:T(8,128)S(1)}, f32[10,512]{1,0:T(8,128)}, u32[]{:S(2)}) copy-start(f32[10,512]{1,0:T(8,128)} %get-tuple-element.123) | copy-start | bytes 61444
  269.0 9.5 %copy-start.25 = (f32[10,512]{1,0:T(8,128)S(1)}, f32[10,512]{1,0:T(8,128)}, u32[]{:S(2)}) copy-start(f32[10,512]{1,0:T(8,128)} %get-tuple-element.124) | copy-start | bytes 61444
  269.0 9.5 %copy-start.26 = (f32[10,512]{1,0:T(8,128)S(1)}, f32[10,512]{1,0:T(8,128)}, u32[]{:S(2)}) copy-start(f32[10,512]{1,0:T(8,128)} %get-tuple-element.125) | copy-start | bytes 61444
  269.0 9.5 %copy-start.27 = (f32[10,512]{1,0:T(8,128)S(1)}, f32[10,512]{1,0:T(8,128)}, u32[]{:S(2)}) copy-start(f32[10,512]{1,0:T(8,128)} %get-tuple-element.126) | copy-start | bytes 61444
  269.0 9.5 %copy-start.64 = (pred[512]{0:T(512)(128)(4,1)S(1)}, pred[512]{0:T(512)(128)(4,1)}, u32[]{:S(2)}) copy-start(pred[512]{0:T(512)(128)(4,1)} %iota_compare_fusion.1) | copy-start | bytes 1540
  278.6 66.8 %copy-start.56 = (f32[768]{0:T(1024)S(1)}, f32[768]{0:T(1024)}, u32[]{:S(2)}) copy-start(f32[768]{0:T(1024)} %param.12) | copy-start | bytes 9220
  323.9 73.2 %copy-start.77 = (f32[8]{0:T(128)S(1)}, f32[8]{0:T(128)}, u32[]{:S(2)}) copy-start(f32[8]{0:T(128)} %copy-done.76) | copy-start | bytes 100
  323.9 73.2 %copy-start.29 = (f32[8,768]{1,0:T(8,128)S(1)}, f32[8,768]{1,0:T(8,128)}, u32[]{:S(2)}) copy-start(f32[8,768]{1,0:T(8,128)} %copy-done.28) | copy-start | bytes 73732
  323.9 73.2 %copy-start.31 = (f32[8,768]{1,0:T(8,128)S(1)}, f32[8,768]{1,0:T(8,128)}, u32[]{:S(2)}) copy-start(f32[8,768]{1,0:T(8,128)} %copy-done.30) | copy-start | bytes 73732
  323.9 73.2 %copy-start.33 = (f32[8,768]{1,0:T(8,128)S(1)}, f32[8,768]{1,0:T(8,128)}, u32[]{:S(2)}) copy-start(f32[8,768]{1,0:T(8,128)} %copy-done.32) | copy-start | bytes 73732
  323.9 73.2 %copy-start.35 = (f32[8,768]{1,0:T(8,128)S(1)}, f32[8,768]{1,0:T(8,128)}, u32[]{:S(2)}) copy-start(f32[8,768]{1,0:T(8,128)} %copy-done.34) | copy-start | bytes 73732
  323.9 73.2 %copy-start.37 = (f32[8,768]{1,0:T(8,128)S(1)}, f32[8,768]{1,0:T(8,128)}, u32[]{:S(2)}) copy-start(f32[8,768]{1,0:T(8,128)} %copy-done.36) | copy-start | bytes 73732
  323.9 73.2 %copy-start.39 = (f32[8,768]{1,0:T(8,128)S(1)}, f32[8,768]{1,0:T(8,128)}, u32[]{:S(2)}) copy-start(f32[8,768]{1,0:T(8,128)} %copy-done.38) | copy-start | bytes 73732
  324.0 73.2 %copy-start.41 = (f32[3,1,768]{2,0,1:T(4,128)S(1)}, f32[3,1,768]{2,0,1:T(4,128)}, u32[]{:S(2)}) copy-start(f32[3,1,768]{2,0,1:T(4,128)} %copy-done.40) | copy-start | bytes 27652
  324.0 73.2 %copy-start.44 = (f32[3,768]{1,0:T(4,128)S(1)}, f32[3,768]{1,0:T(4,128)}, u32[]{:S(2)}) copy-start(f32[3,768]{1,0:T(4,128)} %copy-done.42) | copy-start | bytes 27652
  324.0 73.2 %copy-start.47 = (f32[3,768]{1,0:T(4,128)S(1)}, f32[3,768]{1,0:T(4,128)}, u32[]{:S(2)}) copy-start(f32[3,768]{1,0:T(4,128)} %copy-done.45) | copy-start | bytes 27652
  324.0 73.2 %copy-start.66 = (f32[8]{0:T(128)S(1)}, f32[8]{0:T(128)}, u32[]{:S(2)}) copy-start(f32[8]{0:T(128)} %copy-done.65) | copy-start | bytes 100
  324.0 73.2 %copy-start.68 = (f32[8]{0:T(128)S(1)}, f32[8]{0:T(128)}, u32[]{:S(2)}) copy-start(f32[8]{0:T(128)} %copy-done.67) | copy-start | bytes 100
  325.6 18.5 %collective-permute-start.18 = (f32[24,64]{0,1:T(8,128)S(1)}, f32[24,64]{0,1:T(8,128)S(1)}, u32[]{:S(2)}, u32[]{:S(2)}) collective-permute-start(f32[24,64]{0,1:T(8,128)S(1)} %get-tuple-element.94), channel_id=1, source_target_pairs={{0,1},{1,2},{2,3},{3,4},{4,5},{5,6},{6,7},{7,8},{8,9},{9,10},{10,1... | collective-permute-start | bytes 18440 | tf_op jit(solution)/shard_map/ppermute | solution.py:16
  328.9 23.3 %collective-permute-start.23 = (f32[24,16]{0,1:T(8,128)S(1)}, f32[24,16]{0,1:T(8,128)S(1)}, u32[]{:S(2)}, u32[]{:S(2)}) collective-permute-start(f32[24,16]{0,1:T(8,128)S(1)} %get-tuple-element.89), channel_id=1, source_target_pairs={{16,0},{17,1},{18,2},{19,3},{20,4},{21,5},{22,6},{23,7},{24,8},{25... | collective-permute-start | bytes 4616 | tf_op jit(solution)/shard_map/ppermute | solution.py:16
  330.2 21.1 %collective-permute-start.22 = (f32[24,16]{0,1:T(8,128)S(1)}, f32[24,16]{0,1:T(8,128)S(1)}, u32[]{:S(2)}, u32[]{:S(2)}) collective-permute-start(f32[24,16]{0,1:T(8,128)S(1)} %get-tuple-element.90), channel_id=1, source_target_pairs={{0,16},{1,17},{2,18},{3,19},{4,20},{5,21},{6,22},{7,23},{8,24},{9,... | collective-permute-start | bytes 4616 | tf_op jit(solution)/shard_map/ppermute | solution.py:16
  337.4 12.8 %collective-permute-start.21 = (f32[24,48]{0,1:T(8,128)S(1)}, f32[24,48]{0,1:T(8,128)S(1)}, u32[]{:S(2)}, u32[]{:S(2)}) collective-permute-start(f32[24,48]{0,1:T(8,128)S(1)} %get-tuple-element.91), channel_id=1, source_target_pairs={{4,0},{5,1},{6,2},{7,3},{8,4},{9,5},{10,6},{11,7},{12,8},{13,9},{1... | collective-permute-start | bytes 13832 | tf_op jit(solution)/shard_map/ppermute | solution.py:16
  338.7 10.4 %collective-permute-start.20 = (f32[24,48]{0,1:T(8,128)S(1)}, f32[24,48]{0,1:T(8,128)S(1)}, u32[]{:S(2)}, u32[]{:S(2)}) collective-permute-start(f32[24,48]{0,1:T(8,128)S(1)} %get-tuple-element.92), channel_id=1, source_target_pairs={{0,4},{1,5},{2,6},{3,7},{4,8},{5,9},{6,10},{7,11},{8,12},{9,13},{1... | collective-permute-start | bytes 13832 | tf_op jit(solution)/shard_map/ppermute | solution.py:16
  344.1 3.7 collective-permute-start.19
  (38 other events, 88.6 us)
where the time goes:
time: 401 us; the launch traced here: 399 us
  blocking collectives  128 us (32%)
  other arithmetic  120 us (30%)
  local copies, waits for them, and re-layouts  73.6 us (18%)
  starting transfers between devices  72.5 us (18%)
    psum x2, blocking collectives, norm_sum(): return lax.psum(inner_product(residual_now, search_now), 'dom')  84.6 us
    ppermute x24, starting transfers between devices, passed_along(): return lax.ppermute(block, axis, route)  72.5 us
    scatter-add x2, other arithmetic, visit_block(): return accumulated.at[:, connectivity].add(forces)  70.1 us
    psum x1, blocking collectives, local(): step_size = energy / lax.psum(inner_product(direction, result), 'dom')  43.5 us
    gather x4, local copies, waits for them, and re-layouts, visit_block(): jnp.take(vector_ext, connectivity, axis=1)  36.8 us
    select_n x2, other arithmetic, visit_block(): forces = jnp.where(is_live, forces, 0.0).reshape(row_count, 10, block_size)  19.9 us
    mul x22, local copies, waits for them, and re-layouts, element_forces(): shape_float[quad_point, deriv_index][None, None, :, :]  17.9 us
    scatter-add x12, other arithmetic, local(): result.at[:, boundary_ids[first_slot:first_slot + width]].add(returned)  13.1 us
  transfers between devices with their start and end apart: 24, of which 2 were waited for; matrix products, arithmetic and copies ran while one was open for 8% of the time, Pallas kernels for 0%

commit v1 on v0

v1 whole, which is shorter than its diff:
```python
import functools

import jax
import jax.numpy as jnp
from jax import lax
from jax.experimental import pallas as pl
from jax.experimental.pallas import tpu as pltpu
from jax.sharding import PartitionSpec as P

F32 = jnp.float32
BF16 = jnp.bfloat16
AXIS = "dom"
CASES = 8
LANES = 128
DISTANCES = (1, 4, 16)
SHARES = {1: 4, 4: 3, 16: 1}


def matchings(devices):
    listed = []
    for distance in DISTANCES:
        for parity in (0, 1):
            pairs = []
            for i in range(devices - distance):
                if (i // distance) % 2 == parity:
                    pairs += [(i, i + distance), (i + distance, i)]
            if pairs:
                listed.append((distance, parity, pairs))
    return listed


def take_lanes(chunks, index):
    lane = index & (LANES - 1)
    which = index >> 7
    rows = len(chunks)
    picked = [None] * rows
    for c in range(len(chunks[0])):
        mask = which == c
        for r in range(rows):
            moved = jnp.take_along_axis(chunks[r][c], lane, axis=1)
            picked[r] = moved if c == 0 else jnp.where(mask, moved, picked[r])
    return picked


def row8(ref, row, start=0, width=LANES):
    return jnp.broadcast_to(ref[row : row + 1, start : start + width], (8, width))


def split_lanes(value):
    return [value[:, c * LANES : (c + 1) * LANES] for c in range(value.shape[1] // LANES)]


def in_two(value):
    head = value.astype(BF16)
    tail = (value - head.astype(F32)).astype(BF16)
    return head, tail


def pick_sides(p, distance, even, odd):
    first = lax.rem(lax.div(p, distance), 2) == 0
    zero = jnp.zeros_like(even)
    odd = zero if odd is None else odd
    return jnp.where(first, even, odd), jnp.where(first, odd, even)


def ghost_bounds(unit):
    return 4 * unit, 8 * unit, 11 * unit, 14 * unit, 15 * unit, 16 * unit


def joined(p, received, rows, lane, opposite):
    sides = {}
    for distance in DISTANCES:
        even = received.get((distance, 0))
        odd = received.get((distance, 1))
        even = even[rows, :]
        odd = None if odd is None else odd[rows, :]
        plus, minus = pick_sides(p, distance, even, odd)
        sides[distance] = (minus, plus) if opposite else (plus, minus)
    tile0 = jnp.where(lane < 64, sides[1][0], sides[1][1])
    tile1 = jnp.where(
        lane < 48,
        sides[4][0],
        jnp.where(lane < 96, sides[4][1], jnp.where(lane < 112, sides[16][0], sides[16][1])),
    )
    return [tile0, tile1]


def spread(tiles, bids_ref, own):
    width = bids_ref.shape[1]
    stacked = jnp.concatenate([jnp.concatenate(t, axis=1) for t in tiles], axis=0)
    head, tail = in_two(stacked)
    left = jnp.concatenate([head, tail], axis=0)
    nodes = lax.broadcasted_iota(jnp.int32, (own, width), 0)
    right = jnp.where(nodes == bids_ref[0:1, :], 1.0, 0.0).astype(BF16)
    out = lax.dot_general(left, right, (((1,), (1,)), ((), ())), preferred_element_type=F32)
    return out[:24] + out[24:]


def boundary_values(chunks, bids_ref):
    return [take_lanes(chunks, row8(bids_ref, 0, t * LANES)) for t in range(2)]


def operate(chunks, conn_ref, grads, qw_ref, lame_ref, live, left_ref, right_ref):
    elems = conn_ref.shape[1]
    lows = lax.broadcasted_iota(jnp.int32, (256, LANES), 0)
    lane = lax.broadcasted_iota(jnp.int32, (1, LANES), 1)

    def block(e):
        e0 = e * LANES
        is_live = (e0 + lane) < live
        nodal = []
        for a in range(10):
            index = conn_ref[a : a + 1, e0 : e0 + LANES]
            nodal.append(take_lanes(chunks, jnp.broadcast_to(index, (8, LANES))))
            hot = jnp.where(lows == (index & 255), 1.0, 0.0).astype(BF16)
            right_ref[:, a * elems + e0 : a * elems + e0 + LANES] = hot

        forces = [[None] * 10 for _ in range(3)]
        lam = lame_ref[0:1, e0 : e0 + LANES]
        mu = lame_ref[1:2, e0 : e0 + LANES]
        for q in range(4):
            grad = [[None] * 3 for _ in range(3)]
            for k in range(3):
                for a in range(10):
                    g = grads(q, k, a, e0)
                    for i in range(3):
                        term = nodal[a][i] * g
                        grad[i][k] = term if a == 0 else grad[i][k] + term
            w = qw_ref[q : q + 1, e0 : e0 + LANES]
            wmu = jnp.broadcast_to(w * mu, (8, LANES))
            wlam = jnp.broadcast_to(w * lam, (8, LANES))
            swell = wlam * (grad[0][0] + grad[1][1] + grad[2][2])
            stress = [[None] * 3 for _ in range(3)]
            for i in range(3):
                stress[i][i] = wmu * (grad[i][i] + grad[i][i]) + swell
                for k in range(i):
                    stress[i][k] = wmu * (grad[i][k] + grad[k][i])
                    stress[k][i] = stress[i][k]
            for k in range(3):
                for a in range(10):
                    g = grads(q, k, a, e0)
                    for i in range(3):
                        term = stress[i][k] * g
                        forces[i][a] = term if q + k == 0 else forces[i][a] + term
        for a in range(10):
            index = conn_ref[a : a + 1, e0 : e0 + LANES]
            high = jnp.broadcast_to(jnp.where(is_live, index >> 8, -1), (8, LANES))
            parts = [in_two(forces[i][a]) for i in range(3)]
            for h in range(4):
                mask = high == h
                kept = [jnp.where(mask, parts[i][s].astype(F32), 0.0) for s in range(2) for i in range(3)]
                left_ref[h * 48 : h * 48 + 48, a * elems + e0 : a * elems + e0 + LANES] = jnp.concatenate(
                    kept, axis=0
                ).astype(BF16)

    for e in range(elems // LANES):
        block(e)
    out = lax.dot_general(
        left_ref[...], right_ref[...], (((1,), (1,)), ((), ())), preferred_element_type=F32
    )
    return [
        [
            (out[h * 48 + i * 8 : h * 48 + i * 8 + 8] + out[h * 48 + 24 + i * 8 : h * 48 + 32 + i * 8])[
                :, c * LANES : (c + 1) * LANES
            ]
            for h in range(4)
            for c in range(2)
        ]
        for i in range(3)
    ]


def widen_grads(grads_ref, wide_ref):
    for q in range(4):
        for k in range(3):
            wide_ref[q * 3 + k, 0:10, :] = grads_ref[q, k].astype(F32)

    def grads(q, k, a, e0):
        return jnp.broadcast_to(wide_ref[q * 3 + k, a : a + 1, e0 : e0 + LANES], (8, LANES))

    return grads


def lane_sum(values):
    total = values[0]
    for value in values[1:]:
        total = total + value
    return jnp.sum(total, axis=1, keepdims=True)


def begin_kernel(rhs_ref, prec_ref, bids_ref, d_ref, t0_ref, t1_ref, blocks_ref):
    own = rhs_ref.shape[1]
    blocks_ref[...] = jnp.zeros_like(blocks_ref)
    for i in range(3):
        d_ref[8 * i : 8 * i + 8, :] = (
            prec_ref[i, 0:1, :] * rhs_ref[0:8, :]
            + prec_ref[i, 1:2, :] * rhs_ref[8:16, :]
            + prec_ref[i, 2:3, :] * rhs_ref[16:24, :]
        )
        for j in range(3):
            blocks_ref[3 * i + j : 3 * i + j + 1, :] = prec_ref[i, j : j + 1, :]
    rows = [split_lanes(d_ref[8 * i : 8 * i + 8, :]) for i in range(3)]
    rows += [split_lanes(blocks_ref[8 * i : 8 * i + 8, :]) for i in range(2)]
    picked = boundary_values(rows, bids_ref)
    for t, ref in enumerate((t0_ref, t1_ref)):
        for r in range(5):
            ref[8 * r : 8 * r + 8, :] = picked[t][r]


def first_kernel(
    keys,
    p_ref,
    count_ref,
    d_ref,
    bids_ref,
    conn_ref,
    grads_ref,
    qw_ref,
    lame_ref,
    mass_ref,
    *rest,
):
    received = dict(zip(keys, rest[: len(keys)]))
    q_ref, s0_ref, s1_ref, gprec_ref, dot_ref, wide_ref, left_ref, right_ref = rest[len(keys) :]
    p = p_ref[0]
    lane = lax.broadcasted_iota(jnp.int32, (8, LANES), 1)
    chunks = []
    for i in range(3):
        ghost = joined(p, received, slice(8 * i, 8 * i + 8), lane, False)
        chunks.append(split_lanes(d_ref[8 * i : 8 * i + 8, :]) + ghost)
    for r in range(2):
        tiles = joined(p, received, slice(24 + 8 * r, 32 + 8 * r), lane, False)
        for t in range(2):
            gprec_ref[8 * r : 8 * r + 8, t * LANES : (t + 1) * LANES] = tiles[t]
    grads = widen_grads(grads_ref, wide_ref)
    acc = operate(chunks, conn_ref, grads, qw_ref, lame_ref, count_ref[0], left_ref, right_ref)
    own_chunks = d_ref.shape[1] // LANES
    dots = []
    partial = []
    for i in range(3):
        partial.append([])
        for c in range(own_chunks):
            value = acc[i][c] + mass_ref[0:1, c * LANES : (c + 1) * LANES] * chunks[i][c]
            q_ref[8 * i : 8 * i + 8, c * LANES : (c + 1) * LANES] = value
            partial[i].append(value)
            dots.append(value * chunks[i][c])
        for c in range(2):
            dots.append(acc[i][own_chunks + c] * chunks[i][own_chunks + c])
    picked = boundary_values(partial, bids_ref)
    for t, ref in enumerate((s0_ref, s1_ref)):
        for i in range(3):
            ref[8 * i : 8 * i + 8, :] = acc[i][own_chunks + t]
            ref[24 + 8 * i : 32 + 8 * i, :] = picked[t][i]
    dot_ref[...] = jnp.broadcast_to(lane_sum(dots), (8, LANES))


def second_kernel(
    keys,
    p_ref,
    count_ref,
    rhs_ref,
    d_ref,
    qpart_ref,
    s0_ref,
    s1_ref,
    prec_ref,
    gprec_ref,
    dot_ref,
    bids_ref,
    conn_ref,
    grads_ref,
    qw_ref,
    lame_ref,
    mass_ref,
    *rest,
):
    received = dict(zip(keys, rest[: len(keys)]))
    q_ref, s_ref, w_ref, out_ref, wide_ref, left_ref, right_ref = rest[len(keys) :]
    p = p_ref[0]
    devices = out_ref.shape[0]
    own = d_ref.shape[1]
    own_chunks = own // LANES
    lane = lax.broadcasted_iota(jnp.int32, (8, LANES), 1)
    back = [joined(p, received, slice(8 * i, 8 * i + 8), lane, True) for i in range(3)]
    q_ref[...] = qpart_ref[...] + spread(back, bids_ref, own)
    largest = jnp.maximum(jnp.max(jnp.abs(prec_ref[...])), jnp.max(jnp.abs(gprec_ref[...])))
    inverse = 1.0 / largest
    ghost_q = []
    for i in range(3):
        tiles = joined(p, received, slice(24 + 8 * i, 32 + 8 * i), lane, False)
        ghost_q.append([s0_ref[8 * i : 8 * i + 8, :] + tiles[0], s1_ref[8 * i : 8 * i + 8, :] + tiles[1]])
    chunks = []
    for i in range(3):
        value = (
            (prec_ref[i, 0:1, :] * inverse) * q_ref[0:8, :]
            + (prec_ref[i, 1:2, :] * inverse) * q_ref[8:16, :]
            + (prec_ref[i, 2:3, :] * inverse) * q_ref[16:24, :]
        )
        s_ref[8 * i : 8 * i + 8, :] = value
        chunks.append(split_lanes(value))
        for t in range(2):
            total = None
            for j in range(3):
                term = (gprec_ref[3 * i + j : 3 * i + j + 1, t * LANES : (t + 1) * LANES] * inverse) * ghost_q[j][t]
                total = term if j == 0 else total + term
            chunks[i].append(total)
    grads = widen_grads(grads_ref, wide_ref)
    acc = operate(chunks, conn_ref, grads, qw_ref, lame_ref, count_ref[0], left_ref, right_ref)
    start = []
    cross = []
    square = []
    for i in range(3):
        for c in range(own_chunks):
            here = slice(8 * i, 8 * i + 8), slice(c * LANES, (c + 1) * LANES)
            value = acc[i][c] + mass_ref[0:1, here[1]] * chunks[i][c]
            w_ref[here] = value
            square.append(value * chunks[i][c])
            cross.append(q_ref[here] * chunks[i][c])
            start.append(rhs_ref[here] * d_ref[here])
        for t in range(2):
            square.append(acc[i][own_chunks + t] * chunks[i][own_chunks + t])
    scalars = [lane_sum(start), dot_ref[:, 0:1], lane_sum(cross), lane_sum(square)]
    scalars.append(jnp.broadcast_to(jnp.reshape(largest, (1, 1)), (8, 1)))
    tail = jnp.zeros((8, LANES), F32)
    for k, value in enumerate(scalars):
        tail = jnp.where(lane == 64 + k, value, tail)

    def clear(j, unused):
        out_ref[j, 0:8, :] = jnp.zeros((8, LANES), F32)
        out_ref[j, 8:16, :] = tail
        return unused

    lax.fori_loop(0, devices, clear, 0)
    for distance, shift_plus, shift_minus, tile in WINDOWS:
        for sign, shift in ((1, shift_plus), (-1, shift_minus)):
            moved = [acc[i][own_chunks + tile] for i in range(3)]
            if shift:
                moved = [pltpu.roll(m, LANES - shift, 1) for m in moved]
            target = p + sign * distance

            @pl.when((target >= 0) & (target < devices))
            def _():
                out_ref[target, 0:8, :] = jnp.where(lane < 64, moved[0], pltpu.roll(moved[1], 64, 1))
                out_ref[target, 8:16, :] = jnp.where(lane < 64, moved[2], tail)


WINDOWS = ((1, 0, 64, 0), (4, 0, 48, 1), (16, 96, 112, 1))
WIDTHS = {1: 64, 4: 48, 16: 16}


def final_kernel(p_ref, in_ref, rhs_ref, d_ref, q_ref, s_ref, wpart_ref, bids_ref, x_ref, r_ref):
    p = p_ref[0]
    devices = in_ref.shape[0]
    own = rhs_ref.shape[1]
    lane = lax.broadcasted_iota(jnp.int32, (8, LANES), 1)
    mine = in_ref[p, 8:16, 68:69]
    inv_mine = 1.0 / mine

    def add_up(j, sums):
        values = in_ref[j, 8:16, 64:68]
        ratio = in_ref[j, 8:16, 68:69] * inv_mine
        column = lax.broadcasted_iota(jnp.int32, (8, 4), 1)
        factor = jnp.where(column < 2, 1.0, jnp.where(column == 2, ratio, ratio * ratio))
        return sums + values * factor

    sums = lax.fori_loop(0, devices, add_up, jnp.zeros((8, 4), F32))
    e0, d0, cross, square = (sums[:, k : k + 1] for k in range(4))
    step = e0 / d0
    scaled = step * mine
    fresh = scaled * (step * cross) - e0
    beta = fresh / e0
    more = 1.0 + beta
    bend = more * more * d0 - 2.0 * more * (scaled * cross) + scaled * (scaled * square)
    step1 = fresh / bend

    zero = jnp.zeros((8, LANES), F32)
    back = [[zero, zero] for _ in range(3)]
    for distance, shift_plus, shift_minus, tile in WINDOWS:
        for sign, shift in ((1, shift_plus), (-1, shift_minus)):
            source = p - sign * distance
            valid = (source >= 0) & (source < devices)
            source = jnp.clip(source, 0, devices - 1)
            ratio = jnp.where(valid, in_ref[source, 8:16, 68:69] * inv_mine, 0.0)
            pair = in_ref[source, 0:8, :]
            last = in_ref[source, 8:16, :]
            blocks = [pair, pltpu.roll(pair, 64, 1), last]
            inside = (lane >= shift) & (lane < shift + WIDTHS[distance])
            for i in range(3):
                moved = blocks[i] if shift == 0 else pltpu.roll(blocks[i], shift, 1)
                back[i][tile] = jnp.where(inside & valid, moved * ratio, back[i][tile])
    w = wpart_ref[...] + spread(back, bids_ref, own)
    for i in range(3):
        here = slice(8 * i, 8 * i + 8)
        d = d_ref[here, :]
        q = q_ref[here, :]
        x_ref[here, :] = step * d + step1 * (more * d - scaled * s_ref[here, :])
        r_ref[here, :] = rhs_ref[here, :] - step * q - step1 * (more * q - scaled * w[here])


def local(
    devices,
    right_side,
    mass_diag,
    precond_blocks,
    connectivity,
    shape_grads,
    quad_weight,
    lame_moduli,
    elem_count,
    boundary_ids,
):
    own = right_side.shape[2]
    elems = connectivity.shape[1]
    p = lax.axis_index(AXIS).astype(jnp.int32).reshape(1)
    rhs = right_side.reshape(24, own)
    mass = mass_diag.reshape(1, own)
    bids = boundary_ids.reshape(1, boundary_ids.shape[0])
    vmem = pl.BlockSpec(memory_space=pltpu.VMEM)
    smem = pl.BlockSpec(memory_space=pltpu.SMEM)
    moves = matchings(devices)
    keys = [(distance, parity) for distance, parity, _ in moves]

    def shape(*dims):
        return jax.ShapeDtypeStruct(dims, F32)

    def call(kernel, out_shape, in_specs, scratch=()):
        return pl.pallas_call(
            kernel,
            out_shape=out_shape,
            in_specs=in_specs,
            out_specs=[vmem] * len(out_shape),
            scratch_shapes=list(scratch),
            compiler_params=pltpu.CompilerParams(vmem_limit_bytes=32 << 20),
        )

    def exchange(tile0, tile1):
        return [
            lax.ppermute(tile0 if distance == 1 else tile1, AXIS, pairs) for distance, _, pairs in moves
        ]

    work = (
        pltpu.VMEM((12, 16, elems), F32),
        pltpu.VMEM((192, 10 * elems), BF16),
        pltpu.VMEM((256, 10 * elems), BF16),
    )
    d, t0, t1 = call(
        begin_kernel,
        [shape(24, own), shape(40, LANES), shape(40, LANES)],
        [vmem] * 3,
        [pltpu.VMEM((16, own), F32)],
    )(rhs, precond_blocks, bids)
    got = exchange(t0, t1)
    mesh_args = (bids, connectivity, shape_grads, quad_weight, lame_moduli, mass)
    qpart, s0, s1, gprec, dot = call(
        functools.partial(first_kernel, keys),
        [shape(24, own), shape(48, LANES), shape(48, LANES), shape(16, 2 * LANES), shape(8, LANES)],
        [smem, smem] + [vmem] * (7 + len(keys)),
        work,
    )(p, elem_count, d, *mesh_args, *got)
    got = exchange(s0, s1)
    q, s, wpart, message = call(
        functools.partial(second_kernel, keys),
        [shape(24, own), shape(24, own), shape(24, own), shape(devices, 16, LANES)],
        [smem, smem] + [vmem] * (14 + len(keys)),
        work,
    )(p, elem_count, rhs, d, qpart, s0, s1, precond_blocks, gprec, dot, *mesh_args, *got)
    message = lax.all_to_all(message, AXIS, 0, 0, tiled=True)
    x, r = call(final_kernel, [shape(24, own), shape(24, own)], [smem] + [vmem] * 7)(
        p, message, rhs, d, q, s, wpart, bids
    )
    return x.reshape(3, CASES, own), r.reshape(3, CASES, own)


def solution(mesh):
    return jax.shard_map(
        functools.partial(local, mesh.shape[AXIS]),
        mesh=mesh,
        in_specs=(
            P(None, None, AXIS),
            P(AXIS),
            P(None, None, AXIS),
            P(None, AXIS),
            P(None, None, None, AXIS),
            P(None, AXIS),
            P(None, AXIS),
            P(AXIS),
            P(AXIS),
        ),
        out_specs=(P(None, None, AXIS), P(None, None, AXIS)),
        check_vma=False,
    )
```

time: 401 us -> 58.9 us (0.15)
  other arithmetic: 120 us -> 0 us
  blocking collectives: 128 us -> 16 us
  local copies, waits for them, and re-layouts: 73.6 us -> 3.41 us
  starting transfers between devices: 72.5 us -> 21.6 us
  Pallas kernels: 0 us -> 13.9 us
    psum x3 -> x0, blocking collectives: 128 us -> none  [the longest x2 84.6 us: norm_sum(): return lax.psum(inner_product(residual_now, search_now), 'dom')]
    scatter-add x14 -> x0, other arithmetic: 83.2 us -> none  [the longest x2 70.1 us: visit_block(): return accumulated.at[:, connectivity].add(forces)]
    ppermute x24 -> x10, starting transfers between devices: 72.5 us -> 21.6 us  [exchange(): lax.ppermute(tile0 if distance == 1 else tile1, AXIS, pairs)]
    gather x16 -> x0, local copies, waits for them, and re-layouts: 44.5 us -> none  [the longest x4 36.8 us: visit_block(): jnp.take(vector_ext, connectivity, axis=1)]
    mul x38 -> x0, local copies, waits for them, and re-layouts: 23.3 us -> none  [the longest x22 17.9 us: element_forces(): shape_float[quad_point, deriv_index][None, None, :, :]]
    select_n x6 -> x0, other arithmetic: 23.1 us -> none  [the longest x2 19.9 us: visit_block(): forces = jnp.where(is_live, forces, 0.0).reshape(row_count, 10, block_size)]
    all_to_all x0 -> x1, blocking collectives: none -> 16 us  [local(): message = lax.all_to_all(message, AXIS, 0, 0, tiled=True)]
    pallas_call x0 -> x4, Pallas kernels: none -> 13.9 us  [the longest x1 5.59 us: local(): call(final_kernel, [shape(24, own), shape(24, own)], [smem] + [vmem] * 7)]
  transfers between devices with their start and end apart: 24 -> 10, of which waited for: 2 -> 2; matrix products, arithmetic and copies ran while one was open for 8% -> 1% of each run, Pallas kernels for 0% -> 0%
where the time goes in v1:
time: 58.9 us; the launch traced here: 58.5 us
  starting transfers between devices  21.6 us (37%)
  blocking collectives  16 us (27%)
  Pallas kernels  13.9 us (24%)
  local copies, waits for them, and re-layouts  3.41 us (6%)
  waiting for transfers between devices  2.12 us (4%)
  between operations  1.43 us (2%)
    ppermute x10, starting transfers between devices, exchange(): lax.ppermute(tile0 if distance == 1 else tile1, AXIS, pairs)  21.6 us
    all_to_all x1, blocking collectives, local(): message = lax.all_to_all(message, AXIS, 0, 0, tiled=True)  16 us
    pallas_call x1, Pallas kernels, local(): call(final_kernel, [shape(24, own), shape(24, own)], [smem] + [vmem] * 7)  5.59 us
    pallas_call x1, Pallas kernels, local(): call(functools.partial(second_kernel, keys), [shape(24, own), shape(24, o...  4.65 us
    pallas_call x1, Pallas kernels, local(): call(functools.partial(first_kernel, keys), [shape(24, own), shape(48, LA...  3.56 us
    unnamed x19, local copies, waits for them, and re-layouts  2.72 us
    ppermute x10, waiting for transfers between devices, exchange(): lax.ppermute(tile0 if distance == 1 else tile1, AXIS, pairs)  2.12 us
  transfers between devices with their start and end apart: 10, of which 2 were waited for; matrix products, arithmetic and copies ran while one was open for 1% of the time, Pallas kernels for 0%

profile of v1, /device:TPU:0, one launch (start us, length us, event | category | flops | bytes accessed | tf_op | source)
XLA Modules:
  0.0 58.5 jit_solution(13275359699143004807)
XLA Ops:
  0.6 0.0 copy-start.7
  0.6 0.7 %copy-done.7 = s32[256]{0:T(256)S(1)} copy-done((s32[256]{0:T(256)S(1)}, s32[256]{0:T(256)}, u32[]{:S(2)}) %copy-start.7) | copy-done | bytes 1048
  1.3 0.0 copy-start
  1.3 0.9 %copy-done = f32[3,8,768]{2,1,0:T(8,128)S(1)} copy-done((f32[3,8,768]{2,1,0:T(8,128)S(1)}, f32[3,8,768]{2,1,0:T(8,128)}, u32[]{:S(2)}) %copy-start) | copy-done | bytes 73752
  2.2 0.0 copy-start.2
  2.2 0.8 %copy-done.2 = f32[3,3,768]{2,1,0:T(4,128)S(1)} copy-done((f32[3,3,768]{2,1,0:T(4,128)S(1)}, f32[3,3,768]{2,1,0:T(4,128)}, u32[]{:S(2)}) %copy-start.2) | copy-done | bytes 27672
  3.0 0.0 copy-start.8
  3.0 0.1 shard_map.104
  3.1 0.7 %collective-permute-start.1 = (f32[40,128]{1,0:T(8,128)S(1)}, f32[40,128]{1,0:T(8,128)S(1)}, u32[]{:S(2)}, u32[]{:S(2)}) collective-permute-start(f32[40,128]{1,0:T(8,128)S(1)} %get-tuple-element.17), channel_id=1, source_target_pairs={{1,2},{2,1},{3,4},{4,3},{5,6},{6,5},{7,8},{8,7},{9,10},{10,9},{11,... | collective-permute-start | bytes 61448 | tf_op jit(solution)/shard_map/ppermute | solution.py:438
  3.8 4.4 %collective-permute-start = (f32[40,128]{1,0:T(8,128)S(1)}, f32[40,128]{1,0:T(8,128)S(1)}, u32[]{:S(2)}, u32[]{:S(2)}) collective-permute-start(f32[40,128]{1,0:T(8,128)S(1)} %get-tuple-element.17), channel_id=1, source_target_pairs={{0,1},{1,0},{2,3},{3,2},{4,5},{5,4},{6,7},{7,6},{8,9},{9,8},{10,11... | collective-permute-start | bytes 61448 | tf_op jit(solution)/shard_map/ppermute | solution.py:438
  8.1 2.8 %collective-permute-start.4 = (f32[40,128]{1,0:T(8,128)S(1)}, f32[40,128]{1,0:T(8,128)S(1)}, u32[]{:S(2)}, u32[]{:S(2)}) collective-permute-start(f32[40,128]{1,0:T(8,128)S(1)} %get-tuple-element.18), channel_id=1, source_target_pairs={{0,16},{16,0},{1,17},{17,1},{2,18},{18,2},{3,19},{19,3},{4,20},{20... | collective-permute-start | bytes 61448 | tf_op jit(solution)/shard_map/ppermute | solution.py:438
  11.0 0.7 %collective-permute-start.3 = (f32[40,128]{1,0:T(8,128)S(1)}, f32[40,128]{1,0:T(8,128)S(1)}, u32[]{:S(2)}, u32[]{:S(2)}) collective-permute-start(f32[40,128]{1,0:T(8,128)S(1)} %get-tuple-element.18), channel_id=1, source_target_pairs={{4,8},{8,4},{5,9},{9,5},{6,10},{10,6},{7,11},{11,7},{12,16},{16,12... | collective-permute-start | bytes 61448 | tf_op jit(solution)/shard_map/ppermute | solution.py:438
  11.6 4.3 %collective-permute-start.2 = (f32[40,128]{1,0:T(8,128)S(1)}, f32[40,128]{1,0:T(8,128)S(1)}, u32[]{:S(2)}, u32[]{:S(2)}) collective-permute-start(f32[40,128]{1,0:T(8,128)S(1)} %get-tuple-element.18), channel_id=1, source_target_pairs={{0,4},{4,0},{1,5},{5,1},{2,6},{6,2},{3,7},{7,3},{8,12},{12,8},{9,1... | collective-permute-start | bytes 61448 | tf_op jit(solution)/shard_map/ppermute | solution.py:438
  16.6 0.7 %reshape.25.mass_ref = f32[1,768]{1,0:T(1,128)S(1)} reshape(f32[768]{0:T(1024)} %param.10) | data formatting | bytes 6144 | tf_op jit(solution)/shard_map/reshape | solution.py:416
  17.3 0.0 copy-done.8
  17.3 0.0 copy-start.4
  17.3 0.0 copy-start.5
  17.3 0.0 copy-start.6
  17.4 0.0 collective-permute-done.1.rest_1_
  17.4 0.0 collective-permute-done.rest_0_
  17.4 0.0 collective-permute-done.4.rest_4_
  17.4 0.0 collective-permute-done.3.rest_3_
  17.4 0.3 collective-permute-done.2.rest_2_
  17.8 0.3 copy-done.4
  18.1 0.0 copy-done.5
  18.1 0.0 copy-done.6
  18.1 0.0 copy-start.1
  18.1 0.0 copy-start.3
  18.1 3.6 %shard_map.105 = (f32[24,768]{1,0:T(8,128)S(1)}, f32[48,128]{1,0:T(8,128)S(1)}, f32[48,128]{1,0:T(8,128)S(1)}, f32[16,256]{1,0:T(8,128)S(1)}, f32[8,128]{1,0:T(8,128)S(1)}) custom-call(s32[1]{0:T(128)} %bitcast.p_ref, s32[1]{0:T(128)S(6)} %copy.13.count_ref, f32[24,768]{1,0:T(8,128)S(1)} %get-tuple-element.16.d_ref, s32[1,256]{1,0:T(1,128)S(1)} %bitcast.9, ...), custom_call_target="tpu_custom_call" | custom-call | tf_op jit(solution)/shard_map/pallas_call | solution.py:454
  21.7 0.7 %collective-permute-start.6 = (f32[48,128]{1,0:T(8,128)S(1)}, f32[48,128]{1,0:T(8,128)S(1)}, u32[]{:S(2)}, u32[]{:S(2)}) collective-permute-start(f32[48,128]{1,0:T(8,128)S(1)} %get-tuple-element.20.s0_ref), channel_id=1, source_target_pairs={{1,2},{2,1},{3,4},{4,3},{5,6},{6,5},{7,8},{8,7},{9,10},{10,9},{11,... | collective-permute-start | bytes 73736 | tf_op jit(solution)/shard_map/ppermute | solution.py:438
  22.3 2.7 %collective-permute-start.5 = (f32[48,128]{1,0:T(8,128)S(1)}, f32[48,128]{1,0:T(8,128)S(1)}, u32[]{:S(2)}, u32[]{:S(2)}) collective-permute-start(f32[48,128]{1,0:T(8,128)S(1)} %get-tuple-element.20.s0_ref), channel_id=1, source_target_pairs={{0,1},{1,0},{2,3},{3,2},{4,5},{5,4},{6,7},{7,6},{8,9},{9,8},{10,11... | collective-permute-start | bytes 73736 | tf_op jit(solution)/shard_map/ppermute | solution.py:438
  25.0 1.1 %collective-permute-start.9 = (f32[48,128]{1,0:T(8,128)S(1)}, f32[48,128]{1,0:T(8,128)S(1)}, u32[]{:S(2)}, u32[]{:S(2)}) collective-permute-start(f32[48,128]{1,0:T(8,128)S(1)} %get-tuple-element.21.s1_ref), channel_id=1, source_target_pairs={{0,16},{16,0},{1,17},{17,1},{2,18},{18,2},{3,19},{19,3},{4,20},{20... | collective-permute-start | bytes 73736 | tf_op jit(solution)/shard_map/ppermute | solution.py:438
  26.2 0.7 %collective-permute-start.8 = (f32[48,128]{1,0:T(8,128)S(1)}, f32[48,128]{1,0:T(8,128)S(1)}, u32[]{:S(2)}, u32[]{:S(2)}) collective-permute-start(f32[48,128]{1,0:T(8,128)S(1)} %get-tuple-element.21.s1_ref), channel_id=1, source_target_pairs={{4,8},{8,4},{5,9},{9,5},{6,10},{10,6},{7,11},{11,7},{12,16},{16,12... | collective-permute-start | bytes 73736 | tf_op jit(solution)/shard_map/ppermute | solution.py:438
  26.8 3.6 %collective-permute-start.7 = (f32[48,128]{1,0:T(8,128)S(1)}, f32[48,128]{1,0:T(8,128)S(1)}, u32[]{:S(2)}, u32[]{:S(2)}) collective-permute-start(f32[48,128]{1,0:T(8,128)S(1)} %get-tuple-element.21.s1_ref), channel_id=1, source_target_pairs={{0,4},{4,0},{1,5},{5,1},{2,6},{6,2},{3,7},{7,3},{8,12},{12,8},{9,1... | collective-permute-start | bytes 73736 | tf_op jit(solution)/shard_map/ppermute | solution.py:438
  30.4 0.0 collective-permute-done.6.rest_1_
  30.4 0.0 collective-permute-done.5.rest_0_
  30.4 0.0 collective-permute-done.9.rest_4_
  30.4 0.0 collective-permute-done.8.rest_3_
  30.5 1.8 %collective-permute-done.7.rest_2_ = f32[48,128]{1,0:T(8,128)S(1)} collective-permute-done((f32[48,128]{1,0:T(8,128)S(1)}, f32[48,128]{1,0:T(8,128)S(1)}, u32[]{:S(2)}, u32[]{:S(2)}) %collective-permute-start.7) | collective-permute-done | bytes 24608 | tf_op jit(solution)/shard_map/ppermute | solution.py:438
  32.2 0.0 copy-done.1
  32.2 0.0 copy-done.3
  32.2 4.6 %shard_map.106 = (f32[24,768]{1,0:T(8,128)S(1)}, f32[24,768]{1,0:T(8,128)S(1)}, f32[24,768]{1,0:T(8,128)S(1)}, f32[32,16,128]{2,1,0:T(8,128)S(1)}) custom-call(s32[1]{0:T(128)} %bitcast.p_ref, s32[1]{0:T(128)S(6)} %copy.13.count_ref, f32[24,768]{1,0:T(8,128)S(1)} %bitcast.6, f32[24,768]{1,0:T(8,128)S(1)} %get-tuple-element.16.d_ref, ...), custom_call_target="tpu_custom_call" | custom-call | tf_op jit(solution)/shard_map/pallas_call | solution.py:461
  36.9 16.0 %all_to_all.5.in_ref = f32[32,16,128]{2,1,0:T(8,128)S(1)} all-to-all(f32[32,16,128]{2,1,0:T(8,128)S(1)} %get-tuple-element.24), channel_id=1, replica_groups=mesh['dom'=32] {'dom'}, dimensions={0} | all-to-all | bytes 524288 | tf_op jit(solution)/shard_map/all_to_all | solution.py:467
  52.9 5.6 %shard_map.107 = (f32[24,768]{1,0:T(8,128)}, f32[24,768]{1,0:T(8,128)}) custom-call(s32[1]{0:T(128)} %bitcast.p_ref, f32[32,16,128]{2,1,0:T(8,128)S(1)} %all_to_all.5.in_ref, f32[24,768]{1,0:T(8,128)S(1)} %bitcast.7, f32[24,768]{1,0:T(8,128)S(1)} %get-tuple-element.16.d_ref, f32[24,768]{1,0:T(8,128)S(1)} %get-tuple-element.25.q_ref, ...), custom_call_target="tpu_custom_call" | custom-call | tf_op jit(solution)/shard_map/pallas_call | solution.py:468
  (1 shorter events, 0.0 us)
Async XLA Ops:
  0.6 0.7 %copy-start.7 = (s32[256]{0:T(256)S(1)}, s32[256]{0:T(256)}, u32[]{:S(2)}) copy-start(s32[256]{0:T(256)} %param.17) | copy-start | bytes 3076
  1.3 0.9 %copy-start = (f32[3,8,768]{2,1,0:T(8,128)S(1)}, f32[3,8,768]{2,1,0:T(8,128)}, u32[]{:S(2)}) copy-start(f32[3,8,768]{2,1,0:T(8,128)} %param.9) | copy-start | bytes 221188
  2.2 0.8 %copy-start.2 = (f32[3,3,768]{2,1,0:T(4,128)S(1)}, f32[3,3,768]{2,1,0:T(4,128)}, u32[]{:S(2)}) copy-start(f32[3,3,768]{2,1,0:T(4,128)} %prec_ref.3) | copy-start | bytes 82948
  3.0 14.4 %copy-start.8 = (bf16[4,3,10,512]{3,0,2,1:T(4,128)(2,1)S(1)}, bf16[4,3,10,512]{3,0,2,1:T(4,128)(2,1)}, u32[]{:S(2)}) copy-start(bf16[4,3,10,512]{3,0,2,1:T(4,128)(2,1)} %param.13) | copy-start | bytes 368644
  3.1 14.3 %collective-permute-start.1 = (f32[40,128]{1,0:T(8,128)S(1)}, f32[40,128]{1,0:T(8,128)S(1)}, u32[]{:S(2)}, u32[]{:S(2)}) collective-permute-start(f32[40,128]{1,0:T(8,128)S(1)} %get-tuple-element.17), channel_id=1, source_target_pairs={{1,2},{2,1},{3,4},{4,3},{5,6},{6,5},{7,8},{8,7},{9,10},{10,9},{11,... | collective-permute-start | bytes 61448 | tf_op jit(solution)/shard_map/ppermute | solution.py:438
  3.8 13.6 %collective-permute-start = (f32[40,128]{1,0:T(8,128)S(1)}, f32[40,128]{1,0:T(8,128)S(1)}, u32[]{:S(2)}, u32[]{:S(2)}) collective-permute-start(f32[40,128]{1,0:T(8,128)S(1)} %get-tuple-element.17), channel_id=1, source_target_pairs={{0,1},{1,0},{2,3},{3,2},{4,5},{5,4},{6,7},{7,6},{8,9},{9,8},{10,11... | collective-permute-start | bytes 61448 | tf_op jit(solution)/shard_map/ppermute | solution.py:438
  8.1 9.3 %collective-permute-start.4 = (f32[40,128]{1,0:T(8,128)S(1)}, f32[40,128]{1,0:T(8,128)S(1)}, u32[]{:S(2)}, u32[]{:S(2)}) collective-permute-start(f32[40,128]{1,0:T(8,128)S(1)} %get-tuple-element.18), channel_id=1, source_target_pairs={{0,16},{16,0},{1,17},{17,1},{2,18},{18,2},{3,19},{19,3},{4,20},{20... | collective-permute-start | bytes 61448 | tf_op jit(solution)/shard_map/ppermute | solution.py:438
  11.0 6.4 %collective-permute-start.3 = (f32[40,128]{1,0:T(8,128)S(1)}, f32[40,128]{1,0:T(8,128)S(1)}, u32[]{:S(2)}, u32[]{:S(2)}) collective-permute-start(f32[40,128]{1,0:T(8,128)S(1)} %get-tuple-element.18), channel_id=1, source_target_pairs={{4,8},{8,4},{5,9},{9,5},{6,10},{10,6},{7,11},{11,7},{12,16},{16,12... | collective-permute-start | bytes 61448 | tf_op jit(solution)/shard_map/ppermute | solution.py:438
  11.6 6.1 %collective-permute-start.2 = (f32[40,128]{1,0:T(8,128)S(1)}, f32[40,128]{1,0:T(8,128)S(1)}, u32[]{:S(2)}, u32[]{:S(2)}) collective-permute-start(f32[40,128]{1,0:T(8,128)S(1)} %get-tuple-element.18), channel_id=1, source_target_pairs={{0,4},{4,0},{1,5},{5,1},{2,6},{6,2},{3,7},{7,3},{8,12},{12,8},{9,1... | collective-permute-start | bytes 61448 | tf_op jit(solution)/shard_map/ppermute | solution.py:438
  17.3 0.8 %copy-start.4 = (s32[10,512]{1,0:T(8,128)S(1)}, s32[10,512]{1,0:T(8,128)}, u32[]{:S(2)}) copy-start(s32[10,512]{1,0:T(8,128)} %conn_ref.3) | copy-start | bytes 61444
  17.3 0.8 %copy-start.5 = (f32[4,512]{1,0:T(4,128)S(1)}, f32[4,512]{1,0:T(4,128)}, u32[]{:S(2)}) copy-start(f32[4,512]{1,0:T(4,128)} %qw_ref.3) | copy-start | bytes 24580
  17.3 0.8 %copy-start.6 = (f32[2,512]{1,0:T(2,128)S(1)}, f32[2,512]{1,0:T(2,128)}, u32[]{:S(2)}) copy-start(f32[2,512]{1,0:T(2,128)} %lame_ref.3) | copy-start | bytes 12292
  18.1 14.1 %copy-start.1 = (f32[3,8,768]{2,1,0:T(8,128)S(1)}, f32[3,8,768]{2,1,0:T(8,128)}, u32[]{:S(2)}) copy-start(f32[3,8,768]{2,1,0:T(8,128)} %param.9) | copy-start | bytes 221188
  18.1 14.1 %copy-start.3 = (f32[3,3,768]{2,1,0:T(4,128)S(1)}, f32[3,3,768]{2,1,0:T(4,128)}, u32[]{:S(2)}) copy-start(f32[3,3,768]{2,1,0:T(4,128)} %prec_ref.3) | copy-start | bytes 82948
  21.7 8.8 %collective-permute-start.6 = (f32[48,128]{1,0:T(8,128)S(1)}, f32[48,128]{1,0:T(8,128)S(1)}, u32[]{:S(2)}, u32[]{:S(2)}) collective-permute-start(f32[48,128]{1,0:T(8,128)S(1)} %get-tuple-element.20.s0_ref), channel_id=1, source_target_pairs={{1,2},{2,1},{3,4},{4,3},{5,6},{6,5},{7,8},{8,7},{9,10},{10,9},{11,... | collective-permute-start | bytes 73736 | tf_op jit(solution)/shard_map/ppermute | solution.py:438
  22.3 8.1 %collective-permute-start.5 = (f32[48,128]{1,0:T(8,128)S(1)}, f32[48,128]{1,0:T(8,128)S(1)}, u32[]{:S(2)}, u32[]{:S(2)}) collective-permute-start(f32[48,128]{1,0:T(8,128)S(1)} %get-tuple-element.20.s0_ref), channel_id=1, source_target_pairs={{0,1},{1,0},{2,3},{3,2},{4,5},{5,4},{6,7},{7,6},{8,9},{9,8},{10,11... | collective-permute-start | bytes 73736 | tf_op jit(solution)/shard_map/ppermute | solution.py:438
  25.0 5.4 %collective-permute-start.9 = (f32[48,128]{1,0:T(8,128)S(1)}, f32[48,128]{1,0:T(8,128)S(1)}, u32[]{:S(2)}, u32[]{:S(2)}) collective-permute-start(f32[48,128]{1,0:T(8,128)S(1)} %get-tuple-element.21.s1_ref), channel_id=1, source_target_pairs={{0,16},{16,0},{1,17},{17,1},{2,18},{18,2},{3,19},{19,3},{4,20},{20... | collective-permute-start | bytes 73736 | tf_op jit(solution)/shard_map/ppermute | solution.py:438
  26.2 4.3 %collective-permute-start.8 = (f32[48,128]{1,0:T(8,128)S(1)}, f32[48,128]{1,0:T(8,128)S(1)}, u32[]{:S(2)}, u32[]{:S(2)}) collective-permute-start(f32[48,128]{1,0:T(8,128)S(1)} %get-tuple-element.21.s1_ref), channel_id=1, source_target_pairs={{4,8},{8,4},{5,9},{9,5},{6,10},{10,6},{7,11},{11,7},{12,16},{16,12... | collective-permute-start | bytes 73736 | tf_op jit(solution)/shard_map/ppermute | solution.py:438
  26.8 5.4 %collective-permute-start.7 = (f32[48,128]{1,0:T(8,128)S(1)}, f32[48,128]{1,0:T(8,128)S(1)}, u32[]{:S(2)}, u32[]{:S(2)}) collective-permute-start(f32[48,128]{1,0:T(8,128)S(1)} %get-tuple-element.21.s1_ref), channel_id=1, source_target_pairs={{0,4},{4,0},{1,5},{5,1},{2,6},{6,2},{3,7},{7,3},{8,12},{12,8},{9,1... | collective-permute-start | bytes 73736 | tf_op jit(solution)/shard_map/ppermute | solution.py:438

commit v2 on v1

v2 whole, which is shorter than its diff:
```python
import functools

import jax
import jax.numpy as jnp
from jax import lax
from jax.experimental import pallas as pl
from jax.experimental.pallas import tpu as pltpu
from jax.sharding import PartitionSpec as P

F32 = jnp.float32
BF16 = jnp.bfloat16
AXIS = "dom"
CASES = 8
LANES = 128
DISTANCES = (1, 4, 16)


def routes(devices):
    listed = {}
    for distance in DISTANCES:
        for parity in (0, 1):
            route = {}
            for i in range(devices - distance):
                if (i // distance) % 2 == parity:
                    route[i], route[i + distance] = i + distance, i
            if route:
                for i in range(devices):
                    route.setdefault(i, i ^ 1)
                listed[distance, parity] = route
    last = devices - 1
    listed[1, 1].update({0: 1, 1: 2, 2: 0, last: last - 1, last - 1: last - 2, last - 2: last})
    listed[4, 1].update({2: 1, 1: 0, 0: 3, 3: 2})
    listed[4, 1].update({last - 2: last - 1, last - 1: last, last: last - 3, last - 3: last - 2})
    for route in listed.values():
        assert sorted(route.values()) == list(range(devices))
    return listed


def take_lanes(chunks, index):
    lane = index & (LANES - 1)
    which = index >> 7
    rows = len(chunks)
    picked = [None] * rows
    for c in range(len(chunks[0])):
        mask = which == c
        for r in range(rows):
            moved = jnp.take_along_axis(chunks[r][c], lane, axis=1)
            picked[r] = moved if c == 0 else jnp.where(mask, moved, picked[r])
    return picked


def row8(ref, row, start=0, width=LANES):
    return jnp.broadcast_to(ref[row : row + 1, start : start + width], (8, width))


def split_lanes(value):
    return [value[:, c * LANES : (c + 1) * LANES] for c in range(value.shape[1] // LANES)]


def in_two(value):
    head = value.astype(BF16)
    tail = (value - head.astype(F32)).astype(BF16)
    return head, tail


def joined(p, devices, received, rows, lane, opposite):
    sides = {}
    detour = (p == 1) | (p == devices - 2)
    for distance in DISTANCES:
        even = received[distance, 0][rows, :]
        first = lax.rem(lax.div(p, distance), 2) == 0
        if (distance, 1) in received:
            odd = received[distance, 1][rows, :]
            if distance == 1:
                odd = jnp.where(detour, received[4, 1][rows, :], odd)
        else:
            odd = jnp.zeros_like(even)
        plus = jnp.where(p + distance < devices, jnp.where(first, even, odd), 0.0)
        minus = jnp.where(p - distance >= 0, jnp.where(first, odd, even), 0.0)
        sides[distance] = (minus, plus) if opposite else (plus, minus)
    tile0 = jnp.where(lane < 64, sides[1][0], sides[1][1])
    tile1 = jnp.where(
        lane < 48,
        sides[4][0],
        jnp.where(lane < 96, sides[4][1], jnp.where(lane < 112, sides[16][0], sides[16][1])),
    )
    return [tile0, tile1]


def send_mixed(p, devices, tile0, tile1):
    return jnp.where((p == 2) | (p == devices - 3), tile0, tile1)


def spread(tiles, spot_ref):
    stacked = jnp.concatenate([jnp.concatenate(t, axis=1) for t in tiles], axis=0)
    head, tail = in_two(stacked)
    left = jnp.concatenate([head, tail], axis=0)
    out = lax.dot_general(left, spot_ref[...], (((1,), (1,)), ((), ())), preferred_element_type=F32)
    return out[:24] + out[24:]


def boundary_values(chunks, bids_ref):
    return [take_lanes(chunks, row8(bids_ref, 0, t * LANES)) for t in range(2)]


def operate(chunks, conn_ref, high_ref, wide_ref, qw_ref, lame_ref, hot_ref, left_ref):
    elems = conn_ref.shape[1]

    def wide(k, a, q, e0):
        return jnp.broadcast_to(wide_ref[k * 10 + a, q : q + 1, e0 : e0 + LANES], (8, LANES))

    for e0 in range(0, elems, LANES):
        nodal = [take_lanes(chunks, row8(conn_ref, a, e0)) for a in range(10)]
        forces = [[None] * 10 for _ in range(3)]
        lam = lame_ref[0:1, e0 : e0 + LANES]
        mu = lame_ref[1:2, e0 : e0 + LANES]
        for q in range(4):
            grad = [[None] * 3 for _ in range(3)]
            for k in range(3):
                for a in range(10):
                    g = wide(k, a, q, e0)
                    for i in range(3):
                        term = nodal[a][i] * g
                        grad[i][k] = term if a == 0 else grad[i][k] + term
            w = qw_ref[q : q + 1, e0 : e0 + LANES]
            wmu = jnp.broadcast_to(w * mu, (8, LANES))
            wlam = jnp.broadcast_to(w * lam, (8, LANES))
            swell = wlam * (grad[0][0] + grad[1][1] + grad[2][2])
            stress = [[None] * 3 for _ in range(3)]
            for i in range(3):
                stress[i][i] = wmu * (grad[i][i] + grad[i][i]) + swell
                for k in range(i):
                    stress[i][k] = wmu * (grad[i][k] + grad[k][i])
                    stress[k][i] = stress[i][k]
            for k in range(3):
                for a in range(10):
                    g = wide(k, a, q, e0)
                    for i in range(3):
                        term = stress[i][k] * g
                        forces[i][a] = term if q + k == 0 else forces[i][a] + term
        for a in range(10):
            high = row8(high_ref, a, e0)
            parts = [in_two(forces[i][a]) for i in range(3)]
            for h in range(4):
                mask = high == h
                kept = [jnp.where(mask, parts[i][s].astype(F32), 0.0) for s in range(2) for i in range(3)]
                left_ref[h * 48 : h * 48 + 48, a * elems + e0 : a * elems + e0 + LANES] = jnp.concatenate(
                    kept, axis=0
                ).astype(BF16)
    out = lax.dot_general(
        left_ref[...], hot_ref[...], (((1,), (1,)), ((), ())), preferred_element_type=F32
    )
    return [
        [
            (out[h * 48 + i * 8 : h * 48 + i * 8 + 8] + out[h * 48 + 24 + i * 8 : h * 48 + 32 + i * 8])[
                :, c * LANES : (c + 1) * LANES
            ]
            for h in range(4)
            for c in range(2)
        ]
        for i in range(3)
    ]


def lane_sum(values):
    total = values[0]
    for value in values[1:]:
        total = total + value
    return jnp.sum(total, axis=1, keepdims=True)


def setup_kernel(count_ref, conn_ref, bids_ref, grads_ref, hot_ref, high_ref, wide_ref, spot_ref):
    elems = conn_ref.shape[1]
    lows = lax.broadcasted_iota(jnp.int32, (256, LANES), 0)
    element = lax.broadcasted_iota(jnp.int32, (10, elems), 1)
    is_live = element < count_ref[0]
    high_ref[...] = jnp.where(is_live, conn_ref[...] >> 8, -1)
    for a in range(10):
        for e0 in range(0, elems, LANES):
            index = conn_ref[a : a + 1, e0 : e0 + LANES] & 255
            hot_ref[:, a * elems + e0 : a * elems + e0 + LANES] = jnp.where(lows == index, 1.0, 0.0).astype(BF16)
    for k in range(3):
        for a in range(10):
            wide_ref[k * 10 + a] = grads_ref[k, a].astype(F32)
    nodes = lax.broadcasted_iota(jnp.int32, spot_ref.shape, 0)
    spot_ref[...] = jnp.where(nodes == bids_ref[0:1, :], 1.0, 0.0).astype(BF16)


def begin_kernel(devices, inputs, p_ref, *rest):
    hbm = rest[:inputs]
    held = rest[inputs : 2 * inputs]
    d_ref, t0_ref, t1_ref, mixed_ref, blocks_ref, sems = rest[2 * inputs :]
    copies = [pltpu.make_async_copy(hbm[k], held[k], sems.at[k]) for k in range(inputs)]
    for copy in copies:
        copy.start()
    for copy in copies[:3]:
        copy.wait()
    rhs_ref, prec_ref, bids_ref = held[:3]
    p = p_ref[0]
    blocks_ref[...] = jnp.zeros_like(blocks_ref)
    for i in range(3):
        d_ref[8 * i : 8 * i + 8, :] = (
            prec_ref[i, 0:1, :] * rhs_ref[0:8, :]
            + prec_ref[i, 1:2, :] * rhs_ref[8:16, :]
            + prec_ref[i, 2:3, :] * rhs_ref[16:24, :]
        )
        for j in range(3):
            blocks_ref[3 * i + j : 3 * i + j + 1, :] = prec_ref[i, j : j + 1, :]
    rows = [split_lanes(d_ref[8 * i : 8 * i + 8, :]) for i in range(3)]
    rows += [split_lanes(blocks_ref[8 * i : 8 * i + 8, :]) for i in range(2)]
    tiles = boundary_values(rows, bids_ref)
    for r in range(5):
        here = slice(8 * r, 8 * r + 8)
        t0_ref[here, :] = tiles[0][r]
        t1_ref[here, :] = tiles[1][r]
        mixed_ref[here, :] = send_mixed(p, devices, tiles[0][r], tiles[1][r])
    for copy in copies[3:]:
        copy.wait()


def first_kernel(keys, devices, p_ref, d_ref, bids_ref, conn_ref, high_ref, wide_ref, qw_ref, lame_ref, hot_ref, mass_ref, *rest):
    received = dict(zip(keys, rest[: len(keys)]))
    q_ref, s0_ref, s1_ref, mixed_ref, gprec_ref, dot_ref, left_ref = rest[len(keys) :]
    p = p_ref[0]
    lane = lax.broadcasted_iota(jnp.int32, (8, LANES), 1)
    chunks = []
    for i in range(3):
        ghost = joined(p, devices, received, slice(8 * i, 8 * i + 8), lane, False)
        chunks.append(split_lanes(d_ref[8 * i : 8 * i + 8, :]) + ghost)
    for r in range(2):
        tiles = joined(p, devices, received, slice(24 + 8 * r, 32 + 8 * r), lane, False)
        for t in range(2):
            gprec_ref[8 * r : 8 * r + 8, t * LANES : (t + 1) * LANES] = tiles[t]
    acc = operate(chunks, conn_ref, high_ref, wide_ref, qw_ref, lame_ref, hot_ref, left_ref)
    own_chunks = d_ref.shape[1] // LANES
    mass = mass_rows(mass_ref)
    partial = [[acc[i][c] + mass[c] * chunks[i][c] for c in range(own_chunks)] for i in range(3)]
    tiles = boundary_values(partial, bids_ref)
    for i in range(3):
        send = [acc[i][own_chunks], acc[i][own_chunks + 1]], [tiles[0][i], tiles[1][i]]
        for part, (tile0, tile1) in enumerate(send):
            here = slice(24 * part + 8 * i, 24 * part + 8 * i + 8)
            s0_ref[here, :] = tile0
            s1_ref[here, :] = tile1
            mixed_ref[here, :] = send_mixed(p, devices, tile0, tile1)
    dots = []
    for i in range(3):
        for c in range(own_chunks):
            q_ref[8 * i : 8 * i + 8, c * LANES : (c + 1) * LANES] = partial[i][c]
            dots.append(partial[i][c] * chunks[i][c])
        for c in range(2):
            dots.append(acc[i][own_chunks + c] * chunks[i][own_chunks + c])
    dot_ref[...] = jnp.broadcast_to(lane_sum(dots), (8, LANES))


def mass_rows(mass_ref):
    count = mass_ref.shape[0] // LANES
    return [jnp.broadcast_to(mass_ref[c * LANES : (c + 1) * LANES].reshape(1, LANES), (8, LANES)) for c in range(count)]


WINDOWS = ((1, 0, 64, 0), (4, 0, 48, 1), (16, 96, 112, 1))
WIDTHS = {1: 64, 4: 48, 16: 16}


def second_kernel(
    keys,
    devices,
    p_ref,
    rhs_ref,
    d_ref,
    qpart_ref,
    s0_ref,
    s1_ref,
    prec_ref,
    gprec_ref,
    dot_ref,
    spot_ref,
    conn_ref,
    high_ref,
    wide_ref,
    qw_ref,
    lame_ref,
    hot_ref,
    mass_ref,
    *rest,
):
    received = dict(zip(keys, rest[: len(keys)]))
    q_ref, s_ref, w_ref, out_ref, left_ref = rest[len(keys) :]
    p = p_ref[0]
    own_chunks = d_ref.shape[1] // LANES
    lane = lax.broadcasted_iota(jnp.int32, (8, LANES), 1)
    back = [joined(p, devices, received, slice(8 * i, 8 * i + 8), lane, True) for i in range(3)]
    q_ref[...] = qpart_ref[...] + spread(back, spot_ref)
    largest = jnp.maximum(jnp.max(jnp.abs(prec_ref[...])), jnp.max(jnp.abs(gprec_ref[...])))
    inverse = 1.0 / largest
    ghost_q = []
    for i in range(3):
        tiles = joined(p, devices, received, slice(24 + 8 * i, 32 + 8 * i), lane, False)
        ghost_q.append([s0_ref[8 * i : 8 * i + 8, :] + tiles[0], s1_ref[8 * i : 8 * i + 8, :] + tiles[1]])
    chunks = []
    for i in range(3):
        value = (
            (prec_ref[i, 0:1, :] * inverse) * q_ref[0:8, :]
            + (prec_ref[i, 1:2, :] * inverse) * q_ref[8:16, :]
            + (prec_ref[i, 2:3, :] * inverse) * q_ref[16:24, :]
        )
        s_ref[8 * i : 8 * i + 8, :] = value
        chunks.append(split_lanes(value))
        for t in range(2):
            total = None
            for j in range(3):
                term = (gprec_ref[3 * i + j : 3 * i + j + 1, t * LANES : (t + 1) * LANES] * inverse) * ghost_q[j][t]
                total = term if j == 0 else total + term
            chunks[i].append(total)
    acc = operate(chunks, conn_ref, high_ref, wide_ref, qw_ref, lame_ref, hot_ref, left_ref)
    start = []
    cross = []
    square = []
    mass = mass_rows(mass_ref)
    for i in range(3):
        for c in range(own_chunks):
            here = slice(8 * i, 8 * i + 8), slice(c * LANES, (c + 1) * LANES)
            value = acc[i][c] + mass[c] * chunks[i][c]
            w_ref[here] = value
            square.append(value * chunks[i][c])
            cross.append(q_ref[here] * chunks[i][c])
            start.append(rhs_ref[here] * d_ref[here])
        for t in range(2):
            square.append(acc[i][own_chunks + t] * chunks[i][own_chunks + t])
    scalars = [lane_sum(start), dot_ref[:, 0:1], lane_sum(cross), lane_sum(square)]
    tail = jnp.broadcast_to(jnp.reshape(largest, (1, 1)), (8, LANES))
    for k, value in enumerate(scalars):
        tail = jnp.where(lane == 64 + k, value, tail)
    zero = jnp.zeros((8, LANES), F32)

    def clear(j, unused):
        for k in range(8):
            out_ref[8 * j + k, 0:8, :] = zero
            out_ref[8 * j + k, 8:16, :] = tail
        return unused

    lax.fori_loop(0, devices // 8, clear, 0)
    for distance, shift_plus, shift_minus, tile in WINDOWS:
        for sign, shift in ((1, shift_plus), (-1, shift_minus)):
            moved = [acc[i][own_chunks + tile] for i in range(3)]
            if shift:
                moved = [pltpu.roll(m, LANES - shift, 1) for m in moved]
            target = p + sign * distance

            @pl.when((target >= 0) & (target < devices))
            def _():
                out_ref[target, 0:8, :] = jnp.where(lane < 64, moved[0], pltpu.roll(moved[1], 64, 1))
                out_ref[target, 8:16, :] = jnp.where(lane < 64, moved[2], tail)


def final_kernel(p_ref, in_ref, rhs_ref, d_ref, q_ref, s_ref, wpart_ref, spot_ref, x_ref, r_ref):
    p = p_ref[0]
    devices = in_ref.shape[0]
    lane = lax.broadcasted_iota(jnp.int32, (8, LANES), 1)
    mine = jnp.broadcast_to(in_ref[p, 8:16, 68:69], (8, LANES))
    inv_mine = 1.0 / mine

    def term(j):
        tile = in_ref[j, 8:16, :]
        ratio = pltpu.roll(tile, LANES - 4, 1) * inv_mine
        return tile * jnp.where(lane == 66, ratio, jnp.where(lane == 67, ratio * ratio, 1.0))

    def add_up(j, sums):
        values = [term(8 * j + k) for k in range(8)]
        while len(values) > 1:
            values = [a + b for a, b in zip(values[::2], values[1::2])]
        return sums + values[0]

    sums = lax.fori_loop(0, devices // 8, add_up, jnp.zeros((8, LANES), F32), unroll=devices <= 64)
    e0, d0, cross, square = (jnp.broadcast_to(sums[:, k : k + 1], (8, LANES)) for k in range(64, 68))
    step = e0 / d0
    scaled = step * mine
    fresh = scaled * (step * cross) - e0
    beta = fresh / e0
    more = 1.0 + beta
    bend = more * more * d0 - 2.0 * more * (scaled * cross) + scaled * (scaled * square)
    step1 = fresh / bend
    for_d = step + step1 * more
    for_s = step1 * scaled

    zero = jnp.zeros((8, LANES), F32)
    back = [[zero, zero] for _ in range(3)]
    for distance, shift_plus, shift_minus, tile in WINDOWS:
        for sign, shift in ((1, shift_plus), (-1, shift_minus)):
            source = p - sign * distance
            valid = (source >= 0) & (source < devices)
            source = jnp.clip(source, 0, devices - 1)
            pair = in_ref[source, 0:8, :]
            last = in_ref[source, 8:16, :]
            ratio = jnp.broadcast_to(last[:, 68:69], (8, LANES)) * inv_mine
            blocks = [pair, pltpu.roll(pair, 64, 1), last]
            inside = (lane >= shift) & (lane < shift + WIDTHS[distance]) & valid
            for i in range(3):
                moved = blocks[i] if shift == 0 else pltpu.roll(blocks[i], shift, 1)
                back[i][tile] = jnp.where(inside, moved * ratio, back[i][tile])
    w = spread(back, spot_ref)
    for i in range(3):
        for c in range(rhs_ref.shape[1] // LANES):
            here = slice(8 * i, 8 * i + 8), slice(c * LANES, (c + 1) * LANES)
            x_ref[here] = for_d * d_ref[here] - for_s * s_ref[here]
            r_ref[here] = rhs_ref[here] - for_d * q_ref[here] + for_s * (wpart_ref[here] + w[here])


def local(
    devices,
    right_side,
    mass_diag,
    precond_blocks,
    connectivity,
    shape_grads,
    quad_weight,
    lame_moduli,
    elem_count,
    boundary_ids,
):
    own = right_side.shape[2]
    elems = connectivity.shape[1]
    ghosts = boundary_ids.shape[0]
    p = lax.axis_index(AXIS).astype(jnp.int32).reshape(1)
    rhs = right_side.reshape(24, own)
    bids = boundary_ids.reshape(1, ghosts)
    grads = jnp.transpose(shape_grads, (1, 2, 0, 3))
    vmem = pl.BlockSpec(memory_space=pltpu.VMEM)
    smem = pl.BlockSpec(memory_space=pltpu.SMEM)
    hbm = pl.BlockSpec(memory_space=pltpu.HBM)
    moves = routes(devices)
    keys = list(moves)

    def shape(*dims, dtype=F32):
        return jax.ShapeDtypeStruct(dims, dtype)

    def call(kernel, out_shape, in_specs, scratch=(), cost=None):
        return pl.pallas_call(
            kernel,
            out_shape=out_shape,
            in_specs=in_specs,
            out_specs=[vmem] * len(out_shape),
            scratch_shapes=list(scratch),
            cost_estimate=cost,
            compiler_params=pltpu.CompilerParams(vmem_limit_bytes=24 << 20),
        )

    def exchange(tile0, tile1, mixed):
        tiles = {1: tile0, 4: tile1, 16: tile1}
        return [
            lax.ppermute(mixed if key == (4, 1) else tiles[key[0]], AXIS, sorted(moves[key].items())) for key in keys
        ]

    tile = shape(40, LANES)
    inputs = [
        pltpu.with_memory_space_constraint(value, pltpu.HBM)
        for value in (rhs, precond_blocks, bids, connectivity, grads, quad_weight, lame_moduli, mass_diag)
    ]
    *held, d, t0, t1, mixed = call(
        functools.partial(begin_kernel, devices, len(inputs)),
        [shape(*value.shape, dtype=value.dtype) for value in inputs] + [shape(24, own), tile, tile, tile],
        [smem] + [hbm] * len(inputs),
        [pltpu.VMEM((16, own), F32), pltpu.SemaphoreType.DMA((len(inputs),))],
    )(pltpu.with_memory_space_constraint(p, pltpu.SMEM), *inputs)
    rhs, precond_blocks, bids, connectivity, grads, quad_weight, lame_moduli, mass_diag = held
    got = exchange(t0, t1, mixed)
    hot, high, wide, spot = call(
        setup_kernel,
        [
            shape(256, 10 * elems, dtype=BF16),
            shape(10, elems, dtype=jnp.int32),
            shape(30, 4, elems),
            shape(own, ghosts, dtype=BF16),
        ],
        [smem] + [vmem] * 3,
        cost=pl.CostEstimate(flops=20_000_000, bytes_accessed=4_000_000, transcendentals=0),
    )(elem_count, connectivity, bids, grads)
    mesh_args = (connectivity, high, wide, quad_weight, lame_moduli, hot, mass_diag)
    left = [pltpu.VMEM((192, 10 * elems), BF16)]
    tile = shape(48, LANES)
    qpart, s0, s1, mixed, gprec, dot = call(
        functools.partial(first_kernel, keys, devices),
        [shape(24, own), tile, tile, tile, shape(16, 2 * LANES), shape(8, LANES)],
        [smem] + [vmem] * (9 + len(keys)),
        left,
    )(p, d, bids, *mesh_args, *got)
    got = exchange(s0, s1, mixed)
    q, s, wpart, message = call(
        functools.partial(second_kernel, keys, devices),
        [shape(24, own), shape(24, own), shape(24, own), shape(devices, 16, LANES)],
        [smem] + [vmem] * (16 + len(keys)),
        left,
    )(p, rhs, d, qpart, s0, s1, precond_blocks, gprec, dot, spot, *mesh_args, *got)
    message = lax.all_to_all(message, AXIS, 0, 0, tiled=True)
    x, r = call(final_kernel, [shape(24, own), shape(24, own)], [smem] + [vmem] * 7)(
        p, message, rhs, d, q, s, wpart, spot
    )
    return x.reshape(3, CASES, own), r.reshape(3, CASES, own)


def solution(mesh):
    return jax.shard_map(
        functools.partial(local, mesh.shape[AXIS]),
        mesh=mesh,
        in_specs=(
            P(None, None, AXIS),
            P(AXIS),
            P(None, None, AXIS),
            P(None, AXIS),
            P(None, None, None, AXIS),
            P(None, AXIS),
            P(None, AXIS),
            P(AXIS),
            P(AXIS),
        ),
        out_specs=(P(None, None, AXIS), P(None, None, AXIS)),
        check_vma=False,
    )
```

time: 58.9 us -> 43.5 us (0.74)
  starting transfers between devices: 21.6 us -> 13.9 us
  Pallas kernels: 13.9 us -> 9.62 us
  local copies, waits for them, and re-layouts: 3.41 us -> 0 us
  waiting for transfers between devices: 2.12 us -> 3.79 us
  blocking collectives: 16 us -> 14.7 us
    ppermute x10, starting transfers between devices: 21.6 us -> 13.9 us  [exchange(): lax.ppermute(mixed if key == (4, 1) else tiles[key[0]], AXIS, sorted(move...]
    pallas_call x1, Pallas kernels: 5.59 us -> 0.99 us  [local(): call(final_kernel, [shape(24, own), shape(24, own)], [smem] + [vmem] * 7)]
    unnamed x19 -> x0, local copies, waits for them, and re-layouts: 2.72 us -> none
    ppermute x10, waiting for transfers between devices: 2.12 us -> 3.79 us  [exchange(): lax.ppermute(mixed if key == (4, 1) else tiles[key[0]], AXIS, sorted(move...]
    all_to_all x1, blocking collectives: 16 us -> 14.7 us  [local(): message = lax.all_to_all(message, AXIS, 0, 0, tiled=True)]
    reshape x1 -> x0, local copies, waits for them, and re-layouts: 0.69 us -> none  [local(): mass = mass_diag.reshape(1, own)]
    pallas_call x3 -> x4, Pallas kernels: 8.35 us -> 8.63 us  [the longest x1 3.87 us: local(): call(functools.partial(second_kernel, keys, devices), [shape(24, own), sh...]
  transfers between devices with their start and end apart: 10 -> 10, of which waited for: 2 -> 3; matrix products, arithmetic and copies ran while one was open for 1% -> 0% of each run, Pallas kernels for 0% -> 2%
where the time goes in v2:
time: 43.5 us; the launch traced here: 43.3 us
  blocking collectives  14.7 us (34%)
  starting transfers between devices  13.9 us (32%)
  Pallas kernels  9.62 us (22%)
  waiting for transfers between devices  3.79 us (9%)
  between operations  1.37 us (3%)
    all_to_all x1, blocking collectives, local(): message = lax.all_to_all(message, AXIS, 0, 0, tiled=True)  14.7 us
    ppermute x10, starting transfers between devices, exchange(): lax.ppermute(mixed if key == (4, 1) else tiles[key[0]], AXIS, sorted(move...  13.9 us
    pallas_call x1, Pallas kernels, local(): call(functools.partial(second_kernel, keys, devices), [shape(24, own), sh...  3.87 us
    ppermute x10, waiting for transfers between devices, exchange(): lax.ppermute(mixed if key == (4, 1) else tiles[key[0]], AXIS, sorted(move...  3.79 us
    pallas_call x1, Pallas kernels, local(): call(functools.partial(first_kernel, keys, devices), [shape(24, own), til...  2.9 us
    pallas_call x1, Pallas kernels, local(): call(functools.partial(begin_kernel, devices, len(inputs)), [shape(*value...  1.13 us
    pallas_call x1, Pallas kernels, local(): call(final_kernel, [shape(24, own), shape(24, own)], [smem] + [vmem] * 7)  0.99 us
  transfers between devices with their start and end apart: 10, of which 3 were waited for; matrix products, arithmetic and copies ran while one was open for 0% of the time, Pallas kernels for 2%

profile of v2, /device:TPU:0, one launch (start us, length us, event | category | flops | bytes accessed | tf_op | source)
XLA Modules:
  0.0 43.3 jit_solution(17627064099179108896)
XLA Ops:
  0.6 1.1 %shard_map.104 = (f32[24,768]{1,0:T(8,128)S(1)}, f32[3,3,768]{2,1,0:T(4,128)S(1)}, s32[1,256]{1,0:T(1,128)S(1)}, s32[10,512]{1,0:T(8,128)S(1)}, bf16[3,10,4,512]...) custom-call(s32[1]{0:T(128)} %bitcast.p_ref, ...), custom_call_target="tpu_custom_call" | custom-call | tf_op jit(solution)/shard_map/pallas_call | solution.py:459
  1.8 2.4 %collective-permute-start.3 = (f32[40,128]{1,0:T(8,128)S(1)}, f32[40,128]{1,0:T(8,128)S(1)}, u32[]{:S(2)}, u32[]{:S(2)}) collective-permute-start(f32[40,128]{1,0:T(8,128)S(1)} %get-tuple-element.43), channel_id=1, source_target_pairs={{0,3},{1,0},{2,1},{3,2},{4,8},{5,9},{6,10},{7,11},{8,4},{9,5},{10,... | collective-permute-start | bytes 61448 | tf_op jit(solution)/shard_map/ppermute | solution.py:451
  4.2 0.0 collective-permute-start.1
  4.2 0.7 %collective-permute-start = (f32[40,128]{1,0:T(8,128)S(1)}, f32[40,128]{1,0:T(8,128)S(1)}, u32[]{:S(2)}, u32[]{:S(2)}) collective-permute-start(f32[40,128]{1,0:T(8,128)S(1)} %get-tuple-element.41), channel_id=1, source_target_pairs={{0,1},{1,0},{2,3},{3,2},{4,5},{5,4},{6,7},{7,6},{8,9},{9,8},{10,11... | collective-permute-start | bytes 61448 | tf_op jit(solution)/shard_map/ppermute | solution.py:451
  4.9 3.9 %collective-permute-start.4 = (f32[40,128]{1,0:T(8,128)S(1)}, f32[40,128]{1,0:T(8,128)S(1)}, u32[]{:S(2)}, u32[]{:S(2)}) collective-permute-start(f32[40,128]{1,0:T(8,128)S(1)} %get-tuple-element.42), channel_id=1, source_target_pairs={{0,16},{1,17},{2,18},{3,19},{4,20},{5,21},{6,22},{7,23},{8,24},{9,... | collective-permute-start | bytes 61448 | tf_op jit(solution)/shard_map/ppermute | solution.py:451
  8.9 1.6 %collective-permute-start.2 = (f32[40,128]{1,0:T(8,128)S(1)}, f32[40,128]{1,0:T(8,128)S(1)}, u32[]{:S(2)}, u32[]{:S(2)}) collective-permute-start(f32[40,128]{1,0:T(8,128)S(1)} %get-tuple-element.42), channel_id=1, source_target_pairs={{0,4},{1,5},{2,6},{3,7},{4,0},{5,1},{6,2},{7,3},{8,12},{9,13},{10,... | collective-permute-start | bytes 61448 | tf_op jit(solution)/shard_map/ppermute | solution.py:451
  11.2 0.7 %shard_map.105 = (bf16[256,5120]{1,0:T(8,128)(2,1)S(1)}, s32[10,512]{1,0:T(8,128)S(1)}, f32[30,4,512]{2,1,0:T(4,128)S(1)}, bf16[768,256]{1,0:T(8,128)(2,1)S(1)}) custom-call(s32[1]{0:T(128)S(6)} %copy.11.count_ref, s32[10,512]{1,0:T(8,128)S(1)} %get-tuple-element.33.conn_ref, s32[1,256]{1,0:T(1,128)S(1)} %get-tuple-element.32.bids_ref, ...), custom_call_target="tpu_custom_call" | custom-call | flops 20000000 | bytes 4000000 | tf_op jit(solution)/shard_map/pallas_call | solution.py:467
  11.9 0.0 collective-permute-done.3.rest_3_
  11.9 0.0 collective-permute-done.1.rest_1_
  11.9 0.0 collective-permute-done.rest_0_
  11.9 0.0 collective-permute-done.4.rest_4_
  11.9 0.7 %collective-permute-done.2.rest_2_ = f32[40,128]{1,0:T(8,128)S(1)} collective-permute-done((f32[40,128]{1,0:T(8,128)S(1)}, f32[40,128]{1,0:T(8,128)S(1)}, u32[]{:S(2)}, u32[]{:S(2)}) %collective-permute-start.2) | collective-permute-done | bytes 20512 | tf_op jit(solution)/shard_map/ppermute | solution.py:451
  12.7 2.9 %shard_map.106 = (f32[24,768]{1,0:T(8,128)S(1)}, f32[48,128]{1,0:T(8,128)S(1)}, f32[48,128]{1,0:T(8,128)S(1)}, f32[48,128]{1,0:T(8,128)S(1)}, f32[16,256]{1,0:T(8,128)S(1)}, /*index=5*/f32[8,128]{1,0:T(8,128)S(1)}) custom-call(s32[1]{0:T(128)} %bitcast.p_ref, f32[24,768]{1,0:T(8,128)S(1)} %get-tuple-element.31.d_ref, ...), custom_call_target="tpu_custom_call" | custom-call | tf_op jit(solution)/shard_map/pallas_call | solution.py:481
  15.6 0.1 collective-permute-start.8
  15.6 0.5 %collective-permute-start.6 = (f32[48,128]{1,0:T(8,128)S(1)}, f32[48,128]{1,0:T(8,128)S(1)}, u32[]{:S(2)}, u32[]{:S(2)}) collective-permute-start(f32[48,128]{1,0:T(8,128)S(1)} %get-tuple-element.45.s0_ref), channel_id=1, source_target_pairs={{0,1},{1,2},{2,0},{3,4},{4,3},{5,6},{6,5},{7,8},{8,7},{9,10},{10,9... | collective-permute-start | bytes 73736 | tf_op jit(solution)/shard_map/ppermute | solution.py:451
  16.1 1.3 %collective-permute-start.5 = (f32[48,128]{1,0:T(8,128)S(1)}, f32[48,128]{1,0:T(8,128)S(1)}, u32[]{:S(2)}, u32[]{:S(2)}) collective-permute-start(f32[48,128]{1,0:T(8,128)S(1)} %get-tuple-element.45.s0_ref), channel_id=1, source_target_pairs={{0,1},{1,0},{2,3},{3,2},{4,5},{5,4},{6,7},{7,6},{8,9},{9,8},{10,11... | collective-permute-start | bytes 73736 | tf_op jit(solution)/shard_map/ppermute | solution.py:451
  17.4 2.5 %collective-permute-start.9 = (f32[48,128]{1,0:T(8,128)S(1)}, f32[48,128]{1,0:T(8,128)S(1)}, u32[]{:S(2)}, u32[]{:S(2)}) collective-permute-start(f32[48,128]{1,0:T(8,128)S(1)} %get-tuple-element.46.s1_ref), channel_id=1, source_target_pairs={{0,16},{1,17},{2,18},{3,19},{4,20},{5,21},{6,22},{7,23},{8,24},{9,... | collective-permute-start | bytes 73736 | tf_op jit(solution)/shard_map/ppermute | solution.py:451
  19.9 0.8 %collective-permute-start.7 = (f32[48,128]{1,0:T(8,128)S(1)}, f32[48,128]{1,0:T(8,128)S(1)}, u32[]{:S(2)}, u32[]{:S(2)}) collective-permute-start(f32[48,128]{1,0:T(8,128)S(1)} %get-tuple-element.46.s1_ref), channel_id=1, source_target_pairs={{0,4},{1,5},{2,6},{3,7},{4,0},{5,1},{6,2},{7,3},{8,12},{9,13},{10,... | collective-permute-start | bytes 73736 | tf_op jit(solution)/shard_map/ppermute | solution.py:451
  20.7 0.0 collective-permute-done.8.rest_3_
  20.7 0.0 collective-permute-done.6.rest_1_
  20.7 0.0 collective-permute-done.5.rest_0_
  20.7 1.4 %collective-permute-done.9.rest_4_ = f32[48,128]{1,0:T(8,128)S(1)} collective-permute-done((f32[48,128]{1,0:T(8,128)S(1)}, f32[48,128]{1,0:T(8,128)S(1)}, u32[]{:S(2)}, u32[]{:S(2)}) %collective-permute-start.9) | collective-permute-done | bytes 24608 | tf_op jit(solution)/shard_map/ppermute | solution.py:451
  22.1 1.6 %collective-permute-done.7.rest_2_ = f32[48,128]{1,0:T(8,128)S(1)} collective-permute-done((f32[48,128]{1,0:T(8,128)S(1)}, f32[48,128]{1,0:T(8,128)S(1)}, u32[]{:S(2)}, u32[]{:S(2)}) %collective-permute-start.7) | collective-permute-done | bytes 24608 | tf_op jit(solution)/shard_map/ppermute | solution.py:451
  23.8 3.9 %shard_map.107 = (f32[24,768]{1,0:T(8,128)S(1)}, f32[24,768]{1,0:T(8,128)S(1)}, f32[24,768]{1,0:T(8,128)S(1)}, f32[32,16,128]{2,1,0:T(8,128)S(1)}) custom-call(s32[1]{0:T(128)} %bitcast.p_ref, f32[24,768]{1,0:T(8,128)S(1)} %get-tuple-element.30.rhs_ref, f32[24,768]{1,0:T(8,128)S(1)} %get-tuple-element.31.d_ref, f32[24,768]{1,0:T(8,128)S(1)} %get-tuple-element.44.qpart_ref, ...), custom_call_target="tpu_custom_call" | custom-call | tf_op jit(solution)/shard_map/pallas_call | solution.py:488
  27.7 14.7 %all_to_all.5.in_ref = f32[32,16,128]{2,1,0:T(8,128)S(1)} all-to-all(f32[32,16,128]{2,1,0:T(8,128)S(1)} %get-tuple-element.52), channel_id=1, replica_groups=mesh['dom'=32] {'dom'}, dimensions={0} | all-to-all | bytes 524288 | tf_op jit(solution)/shard_map/all_to_all | solution.py:494
  42.4 1.0 %shard_map.108 = (f32[24,768]{1,0:T(8,128)}, f32[24,768]{1,0:T(8,128)}) custom-call(s32[1]{0:T(128)} %bitcast.p_ref, f32[32,16,128]{2,1,0:T(8,128)S(1)} %all_to_all.5.in_ref, f32[24,768]{1,0:T(8,128)S(1)} %get-tuple-element.30.rhs_ref, f32[24,768]{1,0:T(8,128)S(1)} %get-tuple-element.31.d_ref, f32[24,768]{1,0:T(8,128)S(1)} %get-tuple-element.53.q_ref, ...), custom_call_target="tpu_custom_call" | custom-call | tf_op jit(solution)/shard_map/pallas_call | solution.py:495
Async XLA Ops:
  1.8 10.1 %collective-permute-start.3 = (f32[40,128]{1,0:T(8,128)S(1)}, f32[40,128]{1,0:T(8,128)S(1)}, u32[]{:S(2)}, u32[]{:S(2)}) collective-permute-start(f32[40,128]{1,0:T(8,128)S(1)} %get-tuple-element.43), channel_id=1, source_target_pairs={{0,3},{1,0},{2,1},{3,2},{4,8},{5,9},{6,10},{7,11},{8,4},{9,5},{10,... | collective-permute-start | bytes 61448 | tf_op jit(solution)/shard_map/ppermute | solution.py:451
  4.2 7.7 %collective-permute-start.1 = (f32[40,128]{1,0:T(8,128)S(1)}, f32[40,128]{1,0:T(8,128)S(1)}, u32[]{:S(2)}, u32[]{:S(2)}) collective-permute-start(f32[40,128]{1,0:T(8,128)S(1)} %get-tuple-element.41), channel_id=1, source_target_pairs={{0,1},{1,2},{2,0},{3,4},{4,3},{5,6},{6,5},{7,8},{8,7},{9,10},{10,9... | collective-permute-start | bytes 61448 | tf_op jit(solution)/shard_map/ppermute | solution.py:451
  4.2 7.7 %collective-permute-start = (f32[40,128]{1,0:T(8,128)S(1)}, f32[40,128]{1,0:T(8,128)S(1)}, u32[]{:S(2)}, u32[]{:S(2)}) collective-permute-start(f32[40,128]{1,0:T(8,128)S(1)} %get-tuple-element.41), channel_id=1, source_target_pairs={{0,1},{1,0},{2,3},{3,2},{4,5},{5,4},{6,7},{7,6},{8,9},{9,8},{10,11... | collective-permute-start | bytes 61448 | tf_op jit(solution)/shard_map/ppermute | solution.py:451
  4.9 7.0 %collective-permute-start.4 = (f32[40,128]{1,0:T(8,128)S(1)}, f32[40,128]{1,0:T(8,128)S(1)}, u32[]{:S(2)}, u32[]{:S(2)}) collective-permute-start(f32[40,128]{1,0:T(8,128)S(1)} %get-tuple-element.42), channel_id=1, source_target_pairs={{0,16},{1,17},{2,18},{3,19},{4,20},{5,21},{6,22},{7,23},{8,24},{9,... | collective-permute-start | bytes 61448 | tf_op jit(solution)/shard_map/ppermute | solution.py:451
  8.9 3.8 %collective-permute-start.2 = (f32[40,128]{1,0:T(8,128)S(1)}, f32[40,128]{1,0:T(8,128)S(1)}, u32[]{:S(2)}, u32[]{:S(2)}) collective-permute-start(f32[40,128]{1,0:T(8,128)S(1)} %get-tuple-element.42), channel_id=1, source_target_pairs={{0,4},{1,5},{2,6},{3,7},{4,0},{5,1},{6,2},{7,3},{8,12},{9,13},{10,... | collective-permute-start | bytes 61448 | tf_op jit(solution)/shard_map/ppermute | solution.py:451
  15.6 5.1 %collective-permute-start.8 = (f32[48,128]{1,0:T(8,128)S(1)}, f32[48,128]{1,0:T(8,128)S(1)}, u32[]{:S(2)}, u32[]{:S(2)}) collective-permute-start(f32[48,128]{1,0:T(8,128)S(1)} %get-tuple-element.51), channel_id=1, source_target_pairs={{0,3},{1,0},{2,1},{3,2},{4,8},{5,9},{6,10},{7,11},{8,4},{9,5},{10,... | collective-permute-start | bytes 73736 | tf_op jit(solution)/shard_map/ppermute | solution.py:451
  15.6 5.1 %collective-permute-start.6 = (f32[48,128]{1,0:T(8,128)S(1)}, f32[48,128]{1,0:T(8,128)S(1)}, u32[]{:S(2)}, u32[]{:S(2)}) collective-permute-start(f32[48,128]{1,0:T(8,128)S(1)} %get-tuple-element.45.s0_ref), channel_id=1, source_target_pairs={{0,1},{1,2},{2,0},{3,4},{4,3},{5,6},{6,5},{7,8},{8,7},{9,10},{10,9... | collective-permute-start | bytes 73736 | tf_op jit(solution)/shard_map/ppermute | solution.py:451
  16.1 4.6 %collective-permute-start.5 = (f32[48,128]{1,0:T(8,128)S(1)}, f32[48,128]{1,0:T(8,128)S(1)}, u32[]{:S(2)}, u32[]{:S(2)}) collective-permute-start(f32[48,128]{1,0:T(8,128)S(1)} %get-tuple-element.45.s0_ref), channel_id=1, source_target_pairs={{0,1},{1,0},{2,3},{3,2},{4,5},{5,4},{6,7},{7,6},{8,9},{9,8},{10,11... | collective-permute-start | bytes 73736 | tf_op jit(solution)/shard_map/ppermute | solution.py:451
  17.4 4.7 %collective-permute-start.9 = (f32[48,128]{1,0:T(8,128)S(1)}, f32[48,128]{1,0:T(8,128)S(1)}, u32[]{:S(2)}, u32[]{:S(2)}) collective-permute-start(f32[48,128]{1,0:T(8,128)S(1)} %get-tuple-element.46.s1_ref), channel_id=1, source_target_pairs={{0,16},{1,17},{2,18},{3,19},{4,20},{5,21},{6,22},{7,23},{8,24},{9,... | collective-permute-start | bytes 73736 | tf_op jit(solution)/shard_map/ppermute | solution.py:451
  19.9 3.8 %collective-permute-start.7 = (f32[48,128]{1,0:T(8,128)S(1)}, f32[48,128]{1,0:T(8,128)S(1)}, u32[]{:S(2)}, u32[]{:S(2)}) collective-permute-start(f32[48,128]{1,0:T(8,128)S(1)} %get-tuple-element.46.s1_ref), channel_id=1, source_target_pairs={{0,4},{1,5},{2,6},{3,7},{4,0},{5,1},{6,2},{7,3},{8,12},{9,13},{10,... | collective-permute-start | bytes 73736 | tf_op jit(solution)/shard_map/ppermute | solution.py:451

commit v3 on v2

--- a/solution.py
+++ b/solution.py
@@ -103,8 +103,9 @@
     return [take_lanes(chunks, row8(bids_ref, 0, t * LANES)) for t in range(2)]
 
 
-def operate(chunks, conn_ref, high_ref, wide_ref, qw_ref, lame_ref, hot_ref, left_ref):
+def elements(chunks, conn_ref, high_ref, wide_ref, qw_ref, lame_ref, left_ref):
     elems = conn_ref.shape[1]
+    work = jnp.zeros((8, LANES), F32)
 
     def wide(k, a, q, e0):
         return jnp.broadcast_to(wide_ref[k * 10 + a, q : q + 1, e0 : e0 + LANES], (8, LANES))
@@ -138,28 +139,38 @@
                     for i in range(3):
                         term = stress[i][k] * g
                         forces[i][a] = term if q + k == 0 else forces[i][a] + term
+        done = forces[0][0] * nodal[0][0]
+        for a in range(10):
+            for i in range(3):
+                if a + i > 0:
+                    done = done + forces[i][a] * nodal[a][i]
+        work = work + jnp.where(row8(high_ref, 0, e0) >= 0, done, 0.0)
         for a in range(10):
             high = row8(high_ref, a, e0)
             parts = [in_two(forces[i][a]) for i in range(3)]
             for h in range(4):
                 mask = high == h
                 kept = [jnp.where(mask, parts[i][s].astype(F32), 0.0) for s in range(2) for i in range(3)]
-                left_ref[h * 48 : h * 48 + 48, a * elems + e0 : a * elems + e0 + LANES] = jnp.concatenate(
-                    kept, axis=0
-                ).astype(BF16)
+                at = e0 * 10 + a * LANES
+                left_ref[h * 48 : h * 48 + 48, at : at + LANES] = jnp.concatenate(kept, axis=0).astype(BF16)
+    return work
+
+
+def scatter(left_ref, hot_ref, first, last):
     out = lax.dot_general(
-        left_ref[...], hot_ref[...], (((1,), (1,)), ((), ())), preferred_element_type=F32
+        left_ref[48 * first : 48 * last, :], hot_ref[...], (((1,), (0,)), ((), ())), preferred_element_type=F32
     )
-    return [
-        [
-            (out[h * 48 + i * 8 : h * 48 + i * 8 + 8] + out[h * 48 + 24 + i * 8 : h * 48 + 32 + i * 8])[
-                :, c * LANES : (c + 1) * LANES
-            ]
-            for h in range(4)
-            for c in range(2)
-        ]
-        for i in range(3)
-    ]
+    blocks = []
+    for i in range(3):
+        blocks.append([])
+        for h in range(last - first):
+            at = h * 48 + i * 8
+            blocks[i] += split_lanes(out[at : at + 8] + out[at + 24 : at + 32])
+    return blocks
+
+
+def splat(value):
+    return jnp.broadcast_to(value, (8, LANES))
 
 
 def lane_sum(values):
@@ -169,21 +180,31 @@
     return jnp.sum(total, axis=1, keepdims=True)
 
 
-def setup_kernel(count_ref, conn_ref, bids_ref, grads_ref, hot_ref, high_ref, wide_ref, spot_ref):
+def setup_kernel(
+    count_ref, conn_ref, bids_ref, grads_ref, rhs_ref, d_ref, prec_ref, hot_ref, high_ref, wide_ref, spot_ref, start_ref, size_ref
+):
     elems = conn_ref.shape[1]
-    lows = lax.broadcasted_iota(jnp.int32, (256, LANES), 0)
     element = lax.broadcasted_iota(jnp.int32, (10, elems), 1)
     is_live = element < count_ref[0]
     high_ref[...] = jnp.where(is_live, conn_ref[...] >> 8, -1)
-    for a in range(10):
-        for e0 in range(0, elems, LANES):
-            index = conn_ref[a : a + 1, e0 : e0 + LANES] & 255
-            hot_ref[:, a * elems + e0 : a * elems + e0 + LANES] = jnp.where(lows == index, 1.0, 0.0).astype(BF16)
+    lows = lax.broadcasted_iota(jnp.int32, (LANES, 256), 1)
+    padding = jnp.zeros((6, LANES), jnp.int32)
+    for e0 in range(0, elems, LANES):
+        index = jnp.concatenate([conn_ref[:, e0 : e0 + LANES] & 255, padding], axis=0).T
+        for a in range(10):
+            at = e0 * 10 + a * LANES
+            hot_ref[at : at + LANES, :] = jnp.where(lows == index[:, a : a + 1], 1.0, 0.0).astype(BF16)
     for k in range(3):
         for a in range(10):
             wide_ref[k * 10 + a] = grads_ref[k, a].astype(F32)
     nodes = lax.broadcasted_iota(jnp.int32, spot_ref.shape, 0)
     spot_ref[...] = jnp.where(nodes == bids_ref[0:1, :], 1.0, 0.0).astype(BF16)
+    blocks = [slice(8 * i, 8 * i + 8) for i in range(3)]
+    start_ref[...] = splat(lane_sum([p for b in blocks for p in split_lanes(rhs_ref[b, :] * d_ref[b, :])]))
+    largest = jnp.abs(prec_ref[0])
+    for i in range(1, 3):
+        largest = jnp.maximum(largest, jnp.abs(prec_ref[i]))
+    size_ref[...] = splat(jnp.max(jnp.max(largest, axis=1, keepdims=True), axis=0, keepdims=True))
 
 
 def begin_kernel(devices, inputs, p_ref, *rest):
@@ -218,23 +239,36 @@
         copy.wait()
 
 
-def first_kernel(keys, devices, p_ref, d_ref, bids_ref, conn_ref, high_ref, wide_ref, qw_ref, lame_ref, hot_ref, mass_ref, *rest):
+def first_kernel(
+    keys, devices, p_ref, d_ref, bids_ref, size_ref, conn_ref, high_ref, wide_ref, qw_ref, lame_ref, hot_ref, mass_ref, *rest
+):
     received = dict(zip(keys, rest[: len(keys)]))
-    q_ref, s0_ref, s1_ref, mixed_ref, gprec_ref, dot_ref, left_ref = rest[len(keys) :]
+    q_ref, s0_ref, s1_ref, mixed_ref, gprec_ref, scale_ref, dot_ref, left_ref = rest[len(keys) :]
     p = p_ref[0]
     lane = lax.broadcasted_iota(jnp.int32, (8, LANES), 1)
     chunks = []
     for i in range(3):
         ghost = joined(p, devices, received, slice(8 * i, 8 * i + 8), lane, False)
         chunks.append(split_lanes(d_ref[8 * i : 8 * i + 8, :]) + ghost)
+    largest = size_ref[...]
     for r in range(2):
         tiles = joined(p, devices, received, slice(24 + 8 * r, 32 + 8 * r), lane, False)
         for t in range(2):
             gprec_ref[8 * r : 8 * r + 8, t * LANES : (t + 1) * LANES] = tiles[t]
-    acc = operate(chunks, conn_ref, high_ref, wide_ref, qw_ref, lame_ref, hot_ref, left_ref)
+            largest = jnp.maximum(largest, jnp.abs(tiles[t]))
+    scale_ref[...] = splat(jnp.max(jnp.max(largest, axis=1, keepdims=True), axis=0, keepdims=True))
+    work = elements(chunks, conn_ref, high_ref, wide_ref, qw_ref, lame_ref, left_ref)
+    acc = scatter(left_ref, hot_ref, 0, 4)
     own_chunks = d_ref.shape[1] // LANES
     mass = mass_rows(mass_ref)
-    partial = [[acc[i][c] + mass[c] * chunks[i][c] for c in range(own_chunks)] for i in range(3)]
+    dots = [work]
+    partial = []
+    for i in range(3):
+        partial.append([])
+        for c in range(own_chunks):
+            heavy = mass[c] * chunks[i][c]
+            partial[i].append(acc[i][c] + heavy)
+            dots.append(heavy * chunks[i][c])
     tiles = boundary_values(partial, bids_ref)
     for i in range(3):
         send = [acc[i][own_chunks], acc[i][own_chunks + 1]], [tiles[0][i], tiles[1][i]]
@@ -243,14 +277,9 @@
             s0_ref[here, :] = tile0
             s1_ref[here, :] = tile1
             mixed_ref[here, :] = send_mixed(p, devices, tile0, tile1)
-    dots = []
-    for i in range(3):
         for c in range(own_chunks):
             q_ref[8 * i : 8 * i + 8, c * LANES : (c + 1) * LANES] = partial[i][c]
-            dots.append(partial[i][c] * chunks[i][c])
-        for c in range(2):
-            dots.append(acc[i][own_chunks + c] * chunks[i][own_chunks + c])
-    dot_ref[...] = jnp.broadcast_to(lane_sum(dots), (8, LANES))
+    dot_ref[...] = splat(lane_sum(dots))
 
 
 def mass_rows(mass_ref):
@@ -266,13 +295,13 @@
     keys,
     devices,
     p_ref,
-    rhs_ref,
-    d_ref,
     qpart_ref,
     s0_ref,
     s1_ref,
     prec_ref,
     gprec_ref,
+    scale_ref,
+    start_ref,
     dot_ref,
     spot_ref,
     conn_ref,
@@ -287,12 +316,13 @@
     received = dict(zip(keys, rest[: len(keys)]))
     q_ref, s_ref, w_ref, out_ref, left_ref = rest[len(keys) :]
     p = p_ref[0]
-    own_chunks = d_ref.shape[1] // LANES
+    own_chunks = q_ref.shape[1] // LANES
     lane = lax.broadcasted_iota(jnp.int32, (8, LANES), 1)
+    case = lax.broadcasted_iota(jnp.int32, (8, LANES), 0)
     back = [joined(p, devices, received, slice(8 * i, 8 * i + 8), lane, True) for i in range(3)]
     q_ref[...] = qpart_ref[...] + spread(back, spot_ref)
-    largest = jnp.maximum(jnp.max(jnp.abs(prec_ref[...])), jnp.max(jnp.abs(gprec_ref[...])))
-    inverse = 1.0 / largest
+    scale = scale_ref[...]
+    inverse = (1.0 / scale)[0:1, 0:1]
     ghost_q = []
     for i in range(3):
         tiles = joined(p, devices, received, slice(24 + 8 * i, 32 + 8 * i), lane, False)
@@ -312,67 +342,62 @@
                 term = (gprec_ref[3 * i + j : 3 * i + j + 1, t * LANES : (t + 1) * LANES] * inverse) * ghost_q[j][t]
                 total = term if j == 0 else total + term
             chunks[i].append(total)
-    acc = operate(chunks, conn_ref, high_ref, wide_ref, qw_ref, lame_ref, hot_ref, left_ref)
-    start = []
+    work = elements(chunks, conn_ref, high_ref, wide_ref, qw_ref, lame_ref, left_ref)
+    acc = scatter(left_ref, hot_ref, 0, 4)
+    ghost = [acc[i][own_chunks:] for i in range(3)]
+    mass = mass_rows(mass_ref)
     cross = []
-    square = []
-    mass = mass_rows(mass_ref)
+    square = [work]
     for i in range(3):
         for c in range(own_chunks):
             here = slice(8 * i, 8 * i + 8), slice(c * LANES, (c + 1) * LANES)
-            value = acc[i][c] + mass[c] * chunks[i][c]
-            w_ref[here] = value
-            square.append(value * chunks[i][c])
+            heavy = mass[c] * chunks[i][c]
+            w_ref[here] = acc[i][c] + heavy
             cross.append(q_ref[here] * chunks[i][c])
-            start.append(rhs_ref[here] * d_ref[here])
-        for t in range(2):
-            square.append(acc[i][own_chunks + t] * chunks[i][own_chunks + t])
-    scalars = [lane_sum(start), dot_ref[:, 0:1], lane_sum(cross), lane_sum(square)]
-    tail = jnp.broadcast_to(jnp.reshape(largest, (1, 1)), (8, LANES))
-    for k, value in enumerate(scalars):
-        tail = jnp.where(lane == 64 + k, value, tail)
-    zero = jnp.zeros((8, LANES), F32)
-
-    def clear(j, unused):
+            square.append(heavy * chunks[i][c])
+    tail = jnp.zeros((8, LANES), F32)
+    for k, value in enumerate((start_ref[...], dot_ref[...], splat(lane_sum(cross)), splat(lane_sum(square)))):
+        tail = jnp.where(lane == 8 * k + case, value, tail)
+    tail = jnp.where(lane[0:1] < 32, jnp.sum(tail, axis=0, keepdims=True), scale[0:1])
+
+    def fill(j, unused):
         for k in range(8):
-            out_ref[8 * j + k, 0:8, :] = zero
-            out_ref[8 * j + k, 8:16, :] = tail
+            out_ref[8 * j + k, 12, :, :] = tail
         return unused
 
-    lax.fori_loop(0, devices // 8, clear, 0)
+    lax.fori_loop(0, devices // 8, fill, 0)
     for distance, shift_plus, shift_minus, tile in WINDOWS:
         for sign, shift in ((1, shift_plus), (-1, shift_minus)):
-            moved = [acc[i][own_chunks + tile] for i in range(3)]
+            moved = [ghost[i][tile] for i in range(3)]
             if shift:
                 moved = [pltpu.roll(m, LANES - shift, 1) for m in moved]
+            pair = jnp.where(lane < 64, moved[0], pltpu.roll(moved[1], 64, 1))
+            rest = jnp.where(lane < 64, moved[2], pltpu.roll(pltpu.roll(moved[2], 4, 0), 64, 1))
             target = p + sign * distance
 
             @pl.when((target >= 0) & (target < devices))
             def _():
-                out_ref[target, 0:8, :] = jnp.where(lane < 64, moved[0], pltpu.roll(moved[1], 64, 1))
-                out_ref[target, 8:16, :] = jnp.where(lane < 64, moved[2], tail)
-
-
-def final_kernel(p_ref, in_ref, rhs_ref, d_ref, q_ref, s_ref, wpart_ref, spot_ref, x_ref, r_ref):
+                out_ref[target, 0:8, 0, :] = pair
+                out_ref[target, 8:12, 0, :] = rest[0:4]
+
+
+def final_kernel(p_ref, in_ref, scale_ref, rhs_ref, d_ref, q_ref, s_ref, wpart_ref, spot_ref, x_ref, r_ref):
     p = p_ref[0]
     devices = in_ref.shape[0]
     lane = lax.broadcasted_iota(jnp.int32, (8, LANES), 1)
-    mine = jnp.broadcast_to(in_ref[p, 8:16, 68:69], (8, LANES))
+    case = lax.broadcasted_iota(jnp.int32, (8, LANES), 0)
+    mine = scale_ref[...]
     inv_mine = 1.0 / mine
-
-    def term(j):
-        tile = in_ref[j, 8:16, :]
-        ratio = pltpu.roll(tile, LANES - 4, 1) * inv_mine
-        return tile * jnp.where(lane == 66, ratio, jnp.where(lane == 67, ratio * ratio, 1.0))
-
-    def add_up(j, sums):
-        values = [term(8 * j + k) for k in range(8)]
-        while len(values) > 1:
-            values = [a + b for a, b in zip(values[::2], values[1::2])]
-        return sums + values[0]
-
-    sums = lax.fori_loop(0, devices // 8, add_up, jnp.zeros((8, LANES), F32), unroll=devices <= 64)
-    e0, d0, cross, square = (jnp.broadcast_to(sums[:, k : k + 1], (8, LANES)) for k in range(64, 68))
+    sums = None
+    for j in range(0, devices, 8):
+        rows = in_ref[j : j + 8, 12, 0, :]
+        ratio = pltpu.roll(rows, LANES - 32, 1) * inv_mine
+        rows = rows * jnp.where(lane < 16, 1.0, jnp.where(lane < 24, ratio, ratio * ratio))
+        sums = rows if j == 0 else sums + rows
+    sums = splat(jnp.sum(sums, axis=0, keepdims=True))
+    e0, d0, cross, square = (
+        splat(jnp.sum(jnp.where(lane == 8 * k + case, sums, 0.0), axis=1, keepdims=True)) for k in range(4)
+    )
     step = e0 / d0
     scaled = step * mine
     fresh = scaled * (step * cross) - e0
@@ -390,10 +415,11 @@
             source = p - sign * distance
             valid = (source >= 0) & (source < devices)
             source = jnp.clip(source, 0, devices - 1)
-            pair = in_ref[source, 0:8, :]
-            last = in_ref[source, 8:16, :]
-            ratio = jnp.broadcast_to(last[:, 68:69], (8, LANES)) * inv_mine
-            blocks = [pair, pltpu.roll(pair, 64, 1), last]
+            pair = in_ref[source, 0:8, 0, :]
+            rest = in_ref[source, 8:12, 0, :]
+            rest = jnp.concatenate([rest, pltpu.roll(rest, 64, 1)], axis=0)
+            ratio = splat(in_ref[source, 12, :, 32:33]) * inv_mine
+            blocks = [pair, pltpu.roll(pair, 64, 1), rest]
             inside = (lane >= shift) & (lane < shift + WIDTHS[distance]) & valid
             for i in range(3):
                 moved = blocks[i] if shift == 0 else pltpu.roll(blocks[i], shift, 1)
@@ -464,36 +490,39 @@
     )(pltpu.with_memory_space_constraint(p, pltpu.SMEM), *inputs)
     rhs, precond_blocks, bids, connectivity, grads, quad_weight, lame_moduli, mass_diag = held
     got = exchange(t0, t1, mixed)
-    hot, high, wide, spot = call(
+    row = shape(8, LANES)
+    hot, high, wide, spot, start, size = call(
         setup_kernel,
         [
-            shape(256, 10 * elems, dtype=BF16),
+            shape(10 * elems, 256, dtype=BF16),
             shape(10, elems, dtype=jnp.int32),
             shape(30, 4, elems),
             shape(own, ghosts, dtype=BF16),
+            row,
+            row,
         ],
-        [smem] + [vmem] * 3,
+        [smem] + [vmem] * 6,
         cost=pl.CostEstimate(flops=20_000_000, bytes_accessed=4_000_000, transcendentals=0),
-    )(elem_count, connectivity, bids, grads)
+    )(elem_count, connectivity, bids, grads, rhs, d, precond_blocks)
     mesh_args = (connectivity, high, wide, quad_weight, lame_moduli, hot, mass_diag)
     left = [pltpu.VMEM((192, 10 * elems), BF16)]
     tile = shape(48, LANES)
-    qpart, s0, s1, mixed, gprec, dot = call(
+    qpart, s0, s1, mixed, gprec, scale, dot = call(
         functools.partial(first_kernel, keys, devices),
-        [shape(24, own), tile, tile, tile, shape(16, 2 * LANES), shape(8, LANES)],
-        [smem] + [vmem] * (9 + len(keys)),
+        [shape(24, own), tile, tile, tile, shape(16, 2 * LANES), row, row],
+        [smem] + [vmem] * (10 + len(keys)),
         left,
-    )(p, d, bids, *mesh_args, *got)
+    )(p, d, bids, size, *mesh_args, *got)
     got = exchange(s0, s1, mixed)
     q, s, wpart, message = call(
         functools.partial(second_kernel, keys, devices),
-        [shape(24, own), shape(24, own), shape(24, own), shape(devices, 16, LANES)],
+        [shape(24, own), shape(24, own), shape(24, own), shape(devices, 13, 1, LANES)],
         [smem] + [vmem] * (16 + len(keys)),
         left,
-    )(p, rhs, d, qpart, s0, s1, precond_blocks, gprec, dot, spot, *mesh_args, *got)
+    )(p, qpart, s0, s1, precond_blocks, gprec, scale, start, dot, spot, *mesh_args, *got)
     message = lax.all_to_all(message, AXIS, 0, 0, tiled=True)
-    x, r = call(final_kernel, [shape(24, own), shape(24, own)], [smem] + [vmem] * 7)(
-        p, message, rhs, d, q, s, wpart, spot
+    x, r = call(final_kernel, [shape(24, own), shape(24, own)], [smem] + [vmem] * 8)(
+        p, message, scale, rhs, d, q, s, wpart, spot
     )
     return x.reshape(3, CASES, own), r.reshape(3, CASES, own)
 

time: 43.5 us -> 41 us (0.943)
  blocking collectives: 14.7 us -> 13.1 us
  Pallas kernels: 9.62 us -> 9 us
    all_to_all x1, blocking collectives: 14.7 us -> 13.1 us  [local(): message = lax.all_to_all(message, AXIS, 0, 0, tiled=True)]
    pallas_call x1, Pallas kernels: 2.9 us -> 2.32 us  [local(): call(functools.partial(first_kernel, keys, devices), [shape(24, own), til...]
  transfers between devices with their start and end apart: 10 -> 10, of which waited for: 3 -> 3; matrix products, arithmetic and copies ran while one was open for 0% -> 0% of each run, Pallas kernels for 2% -> 3%
where the time goes in v3:
time: 41 us; the launch traced here: 40.8 us
  starting transfers between devices  13.9 us (34%)
  blocking collectives  13.1 us (32%)
  Pallas kernels  9 us (22%)
  waiting for transfers between devices  3.48 us (8%)
  between operations  1.36 us (3%)
    ppermute x10, starting transfers between devices, exchange(): lax.ppermute(mixed if key == (4, 1) else tiles[key[0]], AXIS, sorted(move...  13.9 us
    all_to_all x1, blocking collectives, local(): message = lax.all_to_all(message, AXIS, 0, 0, tiled=True)  13.1 us
    ppermute x10, waiting for transfers between devices, exchange(): lax.ppermute(mixed if key == (4, 1) else tiles[key[0]], AXIS, sorted(move...  3.48 us
    pallas_call x1, Pallas kernels, local(): call(functools.partial(second_kernel, keys, devices), [shape(24, own), sh...  3.47 us
    pallas_call x1, Pallas kernels, local(): call(functools.partial(first_kernel, keys, devices), [shape(24, own), til...  2.32 us
    pallas_call x1, Pallas kernels, local(): call(functools.partial(begin_kernel, devices, len(inputs)), [shape(*value...  1.13 us
    pallas_call x1, Pallas kernels, local(): call(setup_kernel, [shape(10 * elems, 256, dtype=BF16), shape(10, elems,...  1.04 us
    pallas_call x1, Pallas kernels, local(): call(final_kernel, [shape(24, own), shape(24, own)], [smem] + [vmem] * 8)  1.03 us
  transfers between devices with their start and end apart: 10, of which 3 were waited for; matrix products, arithmetic and copies ran while one was open for 0% of the time, Pallas kernels for 3%

profile of v3, /device:TPU:0, one launch (start us, length us, event | category | flops | bytes accessed | tf_op | source)
XLA Modules:
  0.0 40.8 jit_solution(4547916486949175924)
XLA Ops:
  0.6 1.1 %shard_map.104 = (f32[24,768]{1,0:T(8,128)S(1)}, f32[3,3,768]{2,1,0:T(4,128)S(1)}, s32[1,256]{1,0:T(1,128)S(1)}, s32[10,512]{1,0:T(8,128)S(1)}, bf16[3,10,4,512]...) custom-call(s32[1]{0:T(128)} %bitcast.p_ref, ...), custom_call_target="tpu_custom_call" | custom-call | tf_op jit(solution)/shard_map/pallas_call | solution.py:485
  1.8 2.4 %collective-permute-start.3 = (f32[40,128]{1,0:T(8,128)S(1)}, f32[40,128]{1,0:T(8,128)S(1)}, u32[]{:S(2)}, u32[]{:S(2)}) collective-permute-start(f32[40,128]{1,0:T(8,128)S(1)} %get-tuple-element.48), channel_id=1, source_target_pairs={{0,3},{1,0},{2,1},{3,2},{4,8},{5,9},{6,10},{7,11},{8,4},{9,5},{10,... | collective-permute-start | bytes 61448 | tf_op jit(solution)/shard_map/ppermute | solution.py:477
  4.2 0.0 collective-permute-start.1
  4.2 0.7 %collective-permute-start = (f32[40,128]{1,0:T(8,128)S(1)}, f32[40,128]{1,0:T(8,128)S(1)}, u32[]{:S(2)}, u32[]{:S(2)}) collective-permute-start(f32[40,128]{1,0:T(8,128)S(1)} %get-tuple-element.46), channel_id=1, source_target_pairs={{0,1},{1,0},{2,3},{3,2},{4,5},{5,4},{6,7},{7,6},{8,9},{9,8},{10,11... | collective-permute-start | bytes 61448 | tf_op jit(solution)/shard_map/ppermute | solution.py:477
  4.9 3.9 %collective-permute-start.4 = (f32[40,128]{1,0:T(8,128)S(1)}, f32[40,128]{1,0:T(8,128)S(1)}, u32[]{:S(2)}, u32[]{:S(2)}) collective-permute-start(f32[40,128]{1,0:T(8,128)S(1)} %get-tuple-element.47), channel_id=1, source_target_pairs={{0,16},{1,17},{2,18},{3,19},{4,20},{5,21},{6,22},{7,23},{8,24},{9,... | collective-permute-start | bytes 61448 | tf_op jit(solution)/shard_map/ppermute | solution.py:477
  8.9 1.6 %collective-permute-start.2 = (f32[40,128]{1,0:T(8,128)S(1)}, f32[40,128]{1,0:T(8,128)S(1)}, u32[]{:S(2)}, u32[]{:S(2)}) collective-permute-start(f32[40,128]{1,0:T(8,128)S(1)} %get-tuple-element.47), channel_id=1, source_target_pairs={{0,4},{1,5},{2,6},{3,7},{4,0},{5,1},{6,2},{7,3},{8,12},{9,13},{10,... | collective-permute-start | bytes 61448 | tf_op jit(solution)/shard_map/ppermute | solution.py:477
  11.2 1.0 %shard_map.105 = (bf16[5120,256]{1,0:T(8,128)(2,1)S(1)}, s32[10,512]{1,0:T(8,128)S(1)}, f32[30,4,512]{2,1,0:T(4,128)S(1)}, bf16[768,256]{1,0:T(8,128)(2,1)S(1)},...) custom-call(s32[1]{0:T(128)S(6)} %copy.11.count_ref, s32[10,512]{1,0:T(8,128)S(1)} %get-tuple-element.35.conn_ref, ...), custom_call_target="tpu_custom_call" | custom-call | flops 20000000 | bytes 4000000 | tf_op jit(solution)/shard_map/pallas_call | solution.py:494
  12.2 0.0 collective-permute-done.3.rest_3_
  12.2 0.0 collective-permute-done.1.rest_1_
  12.2 0.0 collective-permute-done.rest_0_
  12.2 0.0 collective-permute-done.4.rest_4_
  12.2 0.4 collective-permute-done.2.rest_2_
  12.7 2.3 %shard_map.106 = (f32[24,768]{1,0:T(8,128)S(1)}, f32[48,128]{1,0:T(8,128)S(1)}, f32[48,128]{1,0:T(8,128)S(1)}, f32[48,128]{1,0:T(8,128)S(1)}, f32[16,256]{1,0:T(...) custom-call(s32[1]{0:T(128)} %bitcast.p_ref, f32[24,768]{1,0:T(8,128)S(1)} %get-tuple-element.33.d_ref, ...), custom_call_target="tpu_custom_call" | custom-call | tf_op jit(solution)/shard_map/pallas_call | solution.py:510
  15.0 0.1 collective-permute-start.8
  15.1 0.5 %collective-permute-start.6 = (f32[48,128]{1,0:T(8,128)S(1)}, f32[48,128]{1,0:T(8,128)S(1)}, u32[]{:S(2)}, u32[]{:S(2)}) collective-permute-start(f32[48,128]{1,0:T(8,128)S(1)} %get-tuple-element.50.s0_ref), channel_id=1, source_target_pairs={{0,1},{1,2},{2,0},{3,4},{4,3},{5,6},{6,5},{7,8},{8,7},{9,10},{10,9... | collective-permute-start | bytes 73736 | tf_op jit(solution)/shard_map/ppermute | solution.py:477
  15.5 1.3 %collective-permute-start.5 = (f32[48,128]{1,0:T(8,128)S(1)}, f32[48,128]{1,0:T(8,128)S(1)}, u32[]{:S(2)}, u32[]{:S(2)}) collective-permute-start(f32[48,128]{1,0:T(8,128)S(1)} %get-tuple-element.50.s0_ref), channel_id=1, source_target_pairs={{0,1},{1,0},{2,3},{3,2},{4,5},{5,4},{6,7},{7,6},{8,9},{9,8},{10,11... | collective-permute-start | bytes 73736 | tf_op jit(solution)/shard_map/ppermute | solution.py:477
  16.8 2.6 %collective-permute-start.9 = (f32[48,128]{1,0:T(8,128)S(1)}, f32[48,128]{1,0:T(8,128)S(1)}, u32[]{:S(2)}, u32[]{:S(2)}) collective-permute-start(f32[48,128]{1,0:T(8,128)S(1)} %get-tuple-element.51.s1_ref), channel_id=1, source_target_pairs={{0,16},{1,17},{2,18},{3,19},{4,20},{5,21},{6,22},{7,23},{8,24},{9,... | collective-permute-start | bytes 73736 | tf_op jit(solution)/shard_map/ppermute | solution.py:477
  19.4 0.8 %collective-permute-start.7 = (f32[48,128]{1,0:T(8,128)S(1)}, f32[48,128]{1,0:T(8,128)S(1)}, u32[]{:S(2)}, u32[]{:S(2)}) collective-permute-start(f32[48,128]{1,0:T(8,128)S(1)} %get-tuple-element.51.s1_ref), channel_id=1, source_target_pairs={{0,4},{1,5},{2,6},{3,7},{4,0},{5,1},{6,2},{7,3},{8,12},{9,13},{10,... | collective-permute-start | bytes 73736 | tf_op jit(solution)/shard_map/ppermute | solution.py:477
  20.1 0.0 collective-permute-done.8.rest_3_
  20.1 0.0 collective-permute-done.6.rest_1_
  20.1 0.0 collective-permute-done.5.rest_0_
  20.1 1.4 %collective-permute-done.9.rest_4_ = f32[48,128]{1,0:T(8,128)S(1)} collective-permute-done((f32[48,128]{1,0:T(8,128)S(1)}, f32[48,128]{1,0:T(8,128)S(1)}, u32[]{:S(2)}, u32[]{:S(2)}) %collective-permute-start.9) | collective-permute-done | bytes 24608 | tf_op jit(solution)/shard_map/ppermute | solution.py:477
  21.5 1.7 %collective-permute-done.7.rest_2_ = f32[48,128]{1,0:T(8,128)S(1)} collective-permute-done((f32[48,128]{1,0:T(8,128)S(1)}, f32[48,128]{1,0:T(8,128)S(1)}, u32[]{:S(2)}, u32[]{:S(2)}) %collective-permute-start.7) | collective-permute-done | bytes 24608 | tf_op jit(solution)/shard_map/ppermute | solution.py:477
  23.2 3.5 %shard_map.107 = (f32[24,768]{1,0:T(8,128)S(1)}, f32[24,768]{1,0:T(8,128)S(1)}, f32[24,768]{1,0:T(8,128)S(1)}, f32[32,13,1,128]{3,2,1,0:T(1,128)S(1)}) custom-call(s32[1]{0:T(128)} %bitcast.p_ref, f32[24,768]{1,0:T(8,128)S(1)} %get-tuple-element.49.qpart_ref, f32[48,128]{1,0:T(8,128)S(1)} %get-tuple-element.50.s0_ref, ...), custom_call_target="tpu_custom_call" | custom-call | tf_op jit(solution)/shard_map/pallas_call | solution.py:517
  26.7 13.1 %all_to_all.5.in_ref = f32[32,13,1,128]{3,2,1,0:T(1,128)S(1)} all-to-all(f32[32,13,1,128]{3,2,1,0:T(1,128)S(1)} %get-tuple-element.58), channel_id=1, replica_groups=mesh['dom'=32] {'dom'}, dimensions={0} | all-to-all | bytes 425984 | tf_op jit(solution)/shard_map/all_to_all | solution.py:523
  39.8 1.0 %shard_map.108 = (f32[24,768]{1,0:T(8,128)}, f32[24,768]{1,0:T(8,128)}) custom-call(s32[1]{0:T(128)} %bitcast.p_ref, f32[32,13,1,128]{3,2,1,0:T(1,128)S(1)} %all_to_all.5.in_ref, f32[8,128]{1,0:T(8,128)S(1)} %get-tuple-element.53.scale_ref, f32[24,768]{1,0:T(8,128)S(1)} %get-tuple-element.37.rhs_ref, f32[24,768]{1,0:T(8,128)S(1)} %get-tuple-element.33.d_ref, ...), custom_call_target="tpu_custom_call" | custom-call | tf_op jit(solution)/shard_map/pallas_call | solution.py:524
Async XLA Ops:
  1.8 10.4 %collective-permute-start.3 = (f32[40,128]{1,0:T(8,128)S(1)}, f32[40,128]{1,0:T(8,128)S(1)}, u32[]{:S(2)}, u32[]{:S(2)}) collective-permute-start(f32[40,128]{1,0:T(8,128)S(1)} %get-tuple-element.48), channel_id=1, source_target_pairs={{0,3},{1,0},{2,1},{3,2},{4,8},{5,9},{6,10},{7,11},{8,4},{9,5},{10,... | collective-permute-start | bytes 61448 | tf_op jit(solution)/shard_map/ppermute | solution.py:477
  4.2 8.0 %collective-permute-start.1 = (f32[40,128]{1,0:T(8,128)S(1)}, f32[40,128]{1,0:T(8,128)S(1)}, u32[]{:S(2)}, u32[]{:S(2)}) collective-permute-start(f32[40,128]{1,0:T(8,128)S(1)} %get-tuple-element.46), channel_id=1, source_target_pairs={{0,1},{1,2},{2,0},{3,4},{4,3},{5,6},{6,5},{7,8},{8,7},{9,10},{10,9... | collective-permute-start | bytes 61448 | tf_op jit(solution)/shard_map/ppermute | solution.py:477
  4.2 8.0 %collective-permute-start = (f32[40,128]{1,0:T(8,128)S(1)}, f32[40,128]{1,0:T(8,128)S(1)}, u32[]{:S(2)}, u32[]{:S(2)}) collective-permute-start(f32[40,128]{1,0:T(8,128)S(1)} %get-tuple-element.46), channel_id=1, source_target_pairs={{0,1},{1,0},{2,3},{3,2},{4,5},{5,4},{6,7},{7,6},{8,9},{9,8},{10,11... | collective-permute-start | bytes 61448 | tf_op jit(solution)/shard_map/ppermute | solution.py:477
  4.9 7.3 %collective-permute-start.4 = (f32[40,128]{1,0:T(8,128)S(1)}, f32[40,128]{1,0:T(8,128)S(1)}, u32[]{:S(2)}, u32[]{:S(2)}) collective-permute-start(f32[40,128]{1,0:T(8,128)S(1)} %get-tuple-element.47), channel_id=1, source_target_pairs={{0,16},{1,17},{2,18},{3,19},{4,20},{5,21},{6,22},{7,23},{8,24},{9,... | collective-permute-start | bytes 61448 | tf_op jit(solution)/shard_map/ppermute | solution.py:477
  8.9 3.8 %collective-permute-start.2 = (f32[40,128]{1,0:T(8,128)S(1)}, f32[40,128]{1,0:T(8,128)S(1)}, u32[]{:S(2)}, u32[]{:S(2)}) collective-permute-start(f32[40,128]{1,0:T(8,128)S(1)} %get-tuple-element.47), channel_id=1, source_target_pairs={{0,4},{1,5},{2,6},{3,7},{4,0},{5,1},{6,2},{7,3},{8,12},{9,13},{10,... | collective-permute-start | bytes 61448 | tf_op jit(solution)/shard_map/ppermute | solution.py:477
  15.0 5.1 %collective-permute-start.8 = (f32[48,128]{1,0:T(8,128)S(1)}, f32[48,128]{1,0:T(8,128)S(1)}, u32[]{:S(2)}, u32[]{:S(2)}) collective-permute-start(f32[48,128]{1,0:T(8,128)S(1)} %get-tuple-element.57), channel_id=1, source_target_pairs={{0,3},{1,0},{2,1},{3,2},{4,8},{5,9},{6,10},{7,11},{8,4},{9,5},{10,... | collective-permute-start | bytes 73736 | tf_op jit(solution)/shard_map/ppermute | solution.py:477
  15.1 5.1 %collective-permute-start.6 = (f32[48,128]{1,0:T(8,128)S(1)}, f32[48,128]{1,0:T(8,128)S(1)}, u32[]{:S(2)}, u32[]{:S(2)}) collective-permute-start(f32[48,128]{1,0:T(8,128)S(1)} %get-tuple-element.50.s0_ref), channel_id=1, source_target_pairs={{0,1},{1,2},{2,0},{3,4},{4,3},{5,6},{6,5},{7,8},{8,7},{9,10},{10,9... | collective-permute-start | bytes 73736 | tf_op jit(solution)/shard_map/ppermute | solution.py:477
  15.5 4.6 %collective-permute-start.5 = (f32[48,128]{1,0:T(8,128)S(1)}, f32[48,128]{1,0:T(8,128)S(1)}, u32[]{:S(2)}, u32[]{:S(2)}) collective-permute-start(f32[48,128]{1,0:T(8,128)S(1)} %get-tuple-element.50.s0_ref), channel_id=1, source_target_pairs={{0,1},{1,0},{2,3},{3,2},{4,5},{5,4},{6,7},{7,6},{8,9},{9,8},{10,11... | collective-permute-start | bytes 73736 | tf_op jit(solution)/shard_map/ppermute | solution.py:477
  16.8 4.7 %collective-permute-start.9 = (f32[48,128]{1,0:T(8,128)S(1)}, f32[48,128]{1,0:T(8,128)S(1)}, u32[]{:S(2)}, u32[]{:S(2)}) collective-permute-start(f32[48,128]{1,0:T(8,128)S(1)} %get-tuple-element.51.s1_ref), channel_id=1, source_target_pairs={{0,16},{1,17},{2,18},{3,19},{4,20},{5,21},{6,22},{7,23},{8,24},{9,... | collective-permute-start | bytes 73736 | tf_op jit(solution)/shard_map/ppermute | solution.py:477
  19.4 3.8 %collective-permute-start.7 = (f32[48,128]{1,0:T(8,128)S(1)}, f32[48,128]{1,0:T(8,128)S(1)}, u32[]{:S(2)}, u32[]{:S(2)}) collective-permute-start(f32[48,128]{1,0:T(8,128)S(1)} %get-tuple-element.51.s1_ref), channel_id=1, source_target_pairs={{0,4},{1,5},{2,6},{3,7},{4,0},{5,1},{6,2},{7,3},{8,12},{9,13},{10,... | collective-permute-start | bytes 73736 | tf_op jit(solution)/shard_map/ppermute | solution.py:477

commit v4 on v3

--- a/solution.py
+++ b/solution.py
@@ -91,12 +91,9 @@
     return jnp.where((p == 2) | (p == devices - 3), tile0, tile1)
 
 
-def spread(tiles, spot_ref):
-    stacked = jnp.concatenate([jnp.concatenate(t, axis=1) for t in tiles], axis=0)
-    head, tail = in_two(stacked)
-    left = jnp.concatenate([head, tail], axis=0)
-    out = lax.dot_general(left, spot_ref[...], (((1,), (1,)), ((), ())), preferred_element_type=F32)
-    return out[:24] + out[24:]
+def spread(tiles, place_ref, block):
+    place = jnp.broadcast_to(place_ref[0:1, block * LANES : (block + 1) * LANES], (8, LANES))
+    return [jnp.where(place >= 0, value, 0.0) for value in take_lanes(tiles, place)]
 
 
 def boundary_values(chunks, bids_ref):
@@ -181,7 +178,7 @@
 
 
 def setup_kernel(
-    count_ref, conn_ref, bids_ref, grads_ref, rhs_ref, d_ref, prec_ref, hot_ref, high_ref, wide_ref, spot_ref, start_ref, size_ref
+    count_ref, conn_ref, bids_ref, grads_ref, rhs_ref, d_ref, prec_ref, hot_ref, high_ref, wide_ref, place_ref, start_ref, size_ref
 ):
     elems = conn_ref.shape[1]
     element = lax.broadcasted_iota(jnp.int32, (10, elems), 1)
@@ -197,8 +194,13 @@
     for k in range(3):
         for a in range(10):
             wide_ref[k * 10 + a] = grads_ref[k, a].astype(F32)
-    nodes = lax.broadcasted_iota(jnp.int32, spot_ref.shape, 0)
-    spot_ref[...] = jnp.where(nodes == bids_ref[0:1, :], 1.0, 0.0).astype(BF16)
+    own, ghosts = rhs_ref.shape[1], bids_ref.shape[1]
+    listed = jnp.broadcast_to(bids_ref[0:1, :], (8, ghosts)).T[:, 0:1]
+    for first in range(0, own, LANES):
+        node = first + lax.broadcasted_iota(jnp.int32, (ghosts, LANES), 1)
+        entry = lax.broadcasted_iota(jnp.int32, (ghosts, LANES), 0)
+        found = jnp.max(jnp.where(listed == node, entry, -1), axis=0, keepdims=True)
+        place_ref[:, first : first + LANES] = found
     blocks = [slice(8 * i, 8 * i + 8) for i in range(3)]
     start_ref[...] = splat(lane_sum([p for b in blocks for p in split_lanes(rhs_ref[b, :] * d_ref[b, :])]))
     largest = jnp.abs(prec_ref[0])
@@ -303,7 +305,7 @@
     scale_ref,
     start_ref,
     dot_ref,
-    spot_ref,
+    place_ref,
     conn_ref,
     high_ref,
     wide_ref,
@@ -320,7 +322,10 @@
     lane = lax.broadcasted_iota(jnp.int32, (8, LANES), 1)
     case = lax.broadcasted_iota(jnp.int32, (8, LANES), 0)
     back = [joined(p, devices, received, slice(8 * i, 8 * i + 8), lane, True) for i in range(3)]
-    q_ref[...] = qpart_ref[...] + spread(back, spot_ref)
+    for c in range(own_chunks):
+        for i, value in enumerate(spread(back, place_ref, c)):
+            here = slice(8 * i, 8 * i + 8), slice(c * LANES, (c + 1) * LANES)
+            q_ref[here] = qpart_ref[here] + value
     scale = scale_ref[...]
     inverse = (1.0 / scale)[0:1, 0:1]
     ghost_q = []
@@ -381,7 +386,7 @@
                 out_ref[target, 8:12, 0, :] = rest[0:4]
 
 
-def final_kernel(p_ref, in_ref, scale_ref, rhs_ref, d_ref, q_ref, s_ref, wpart_ref, spot_ref, x_ref, r_ref):
+def final_kernel(p_ref, in_ref, scale_ref, rhs_ref, d_ref, q_ref, s_ref, wpart_ref, place_ref, x_ref, r_ref):
     p = p_ref[0]
     devices = in_ref.shape[0]
     lane = lax.broadcasted_iota(jnp.int32, (8, LANES), 1)
@@ -424,12 +429,11 @@
             for i in range(3):
                 moved = blocks[i] if shift == 0 else pltpu.roll(blocks[i], shift, 1)
                 back[i][tile] = jnp.where(inside, moved * ratio, back[i][tile])
-    w = spread(back, spot_ref)
-    for i in range(3):
-        for c in range(rhs_ref.shape[1] // LANES):
+    for c in range(rhs_ref.shape[1] // LANES):
+        for i, value in enumerate(spread(back, place_ref, c)):
             here = slice(8 * i, 8 * i + 8), slice(c * LANES, (c + 1) * LANES)
             x_ref[here] = for_d * d_ref[here] - for_s * s_ref[here]
-            r_ref[here] = rhs_ref[here] - for_d * q_ref[here] + for_s * (wpart_ref[here] + w[here])
+            r_ref[here] = rhs_ref[here] - for_d * q_ref[here] + for_s * (wpart_ref[here] + value)
 
 
 def local(
@@ -446,10 +450,9 @@
 ):
     own = right_side.shape[2]
     elems = connectivity.shape[1]
-    ghosts = boundary_ids.shape[0]
     p = lax.axis_index(AXIS).astype(jnp.int32).reshape(1)
     rhs = right_side.reshape(24, own)
-    bids = boundary_ids.reshape(1, ghosts)
+    bids = boundary_ids.reshape(1, boundary_ids.shape[0])
     grads = jnp.transpose(shape_grads, (1, 2, 0, 3))
     vmem = pl.BlockSpec(memory_space=pltpu.VMEM)
     smem = pl.BlockSpec(memory_space=pltpu.SMEM)
@@ -491,13 +494,13 @@
     rhs, precond_blocks, bids, connectivity, grads, quad_weight, lame_moduli, mass_diag = held
     got = exchange(t0, t1, mixed)
     row = shape(8, LANES)
-    hot, high, wide, spot, start, size = call(
+    hot, high, wide, place, start, size = call(
         setup_kernel,
         [
             shape(10 * elems, 256, dtype=BF16),
             shape(10, elems, dtype=jnp.int32),
             shape(30, 4, elems),
-            shape(own, ghosts, dtype=BF16),
+            shape(1, own, dtype=jnp.int32),
             row,
             row,
         ],
@@ -519,10 +522,10 @@
         [shape(24, own), shape(24, own), shape(24, own), shape(devices, 13, 1, LANES)],
         [smem] + [vmem] * (16 + len(keys)),
         left,
-    )(p, qpart, s0, s1, precond_blocks, gprec, scale, start, dot, spot, *mesh_args, *got)
+    )(p, qpart, s0, s1, precond_blocks, gprec, scale, start, dot, place, *mesh_args, *got)
     message = lax.all_to_all(message, AXIS, 0, 0, tiled=True)
     x, r = call(final_kernel, [shape(24, own), shape(24, own)], [smem] + [vmem] * 8)(
-        p, message, scale, rhs, d, q, s, wpart, spot
+        p, message, scale, rhs, d, q, s, wpart, place
     )
     return x.reshape(3, CASES, own), r.reshape(3, CASES, own)
 

time: 41 us -> 40.5 us (0.988)
  Pallas kernels: 9 us -> 8.51 us
where the time goes in v4:
time: 40.5 us; the launch traced here: 40.3 us
  starting transfers between devices  13.9 us (34%)
  blocking collectives  13.1 us (32%)
  Pallas kernels  8.51 us (21%)
  waiting for transfers between devices  3.45 us (9%)
  between operations  1.35 us (3%)
    ppermute x10, starting transfers between devices, exchange(): lax.ppermute(mixed if key == (4, 1) else tiles[key[0]], AXIS, sorted(move...  13.9 us
    all_to_all x1, blocking collectives, local(): message = lax.all_to_all(message, AXIS, 0, 0, tiled=True)  13.1 us
    ppermute x10, waiting for transfers between devices, exchange(): lax.ppermute(mixed if key == (4, 1) else tiles[key[0]], AXIS, sorted(move...  3.45 us
    pallas_call x1, Pallas kernels, local(): call(functools.partial(second_kernel, keys, devices), [shape(24, own), sh...  3.13 us
    pallas_call x1, Pallas kernels, local(): call(functools.partial(first_kernel, keys, devices), [shape(24, own), til...  2.25 us
    pallas_call x1, Pallas kernels, local(): call(functools.partial(begin_kernel, devices, len(inputs)), [shape(*value...  1.13 us
    pallas_call x1, Pallas kernels, local(): call(setup_kernel, [shape(10 * elems, 256, dtype=BF16), shape(10, elems,...  1.08 us
    pallas_call x1, Pallas kernels, local(): call(final_kernel, [shape(24, own), shape(24, own)], [smem] + [vmem] * 8)  0.93 us
  transfers between devices with their start and end apart: 10, of which 3 were waited for; matrix products, arithmetic and copies ran while one was open for 0% of the time, Pallas kernels for 3%

profile of v4, /device:TPU:0, one launch (start us, length us, event | category | flops | bytes accessed | tf_op | source)
XLA Modules:
  0.0 40.3 jit_solution(9514580708114156120)
XLA Ops:
  0.6 1.1 %shard_map.104 = (f32[24,768]{1,0:T(8,128)S(1)}, f32[3,3,768]{2,1,0:T(4,128)S(1)}, s32[1,256]{1,0:T(1,128)S(1)}, s32[10,512]{1,0:T(8,128)S(1)}, bf16[3,10,4,512]...) custom-call(s32[1]{0:T(128)} %bitcast.p_ref, ...), custom_call_target="tpu_custom_call" | custom-call | tf_op jit(solution)/shard_map/pallas_call | solution.py:488
  1.8 2.4 %collective-permute-start.3 = (f32[40,128]{1,0:T(8,128)S(1)}, f32[40,128]{1,0:T(8,128)S(1)}, u32[]{:S(2)}, u32[]{:S(2)}) collective-permute-start(f32[40,128]{1,0:T(8,128)S(1)} %get-tuple-element.48), channel_id=1, source_target_pairs={{0,3},{1,0},{2,1},{3,2},{4,8},{5,9},{6,10},{7,11},{8,4},{9,5},{10,... | collective-permute-start | bytes 61448 | tf_op jit(solution)/shard_map/ppermute | solution.py:480
  4.2 0.0 collective-permute-start.1
  4.2 0.7 %collective-permute-start = (f32[40,128]{1,0:T(8,128)S(1)}, f32[40,128]{1,0:T(8,128)S(1)}, u32[]{:S(2)}, u32[]{:S(2)}) collective-permute-start(f32[40,128]{1,0:T(8,128)S(1)} %get-tuple-element.46), channel_id=1, source_target_pairs={{0,1},{1,0},{2,3},{3,2},{4,5},{5,4},{6,7},{7,6},{8,9},{9,8},{10,11... | collective-permute-start | bytes 61448 | tf_op jit(solution)/shard_map/ppermute | solution.py:480
  4.9 3.9 %collective-permute-start.4 = (f32[40,128]{1,0:T(8,128)S(1)}, f32[40,128]{1,0:T(8,128)S(1)}, u32[]{:S(2)}, u32[]{:S(2)}) collective-permute-start(f32[40,128]{1,0:T(8,128)S(1)} %get-tuple-element.47), channel_id=1, source_target_pairs={{0,16},{1,17},{2,18},{3,19},{4,20},{5,21},{6,22},{7,23},{8,24},{9,... | collective-permute-start | bytes 61448 | tf_op jit(solution)/shard_map/ppermute | solution.py:480
  8.9 1.6 %collective-permute-start.2 = (f32[40,128]{1,0:T(8,128)S(1)}, f32[40,128]{1,0:T(8,128)S(1)}, u32[]{:S(2)}, u32[]{:S(2)}) collective-permute-start(f32[40,128]{1,0:T(8,128)S(1)} %get-tuple-element.47), channel_id=1, source_target_pairs={{0,4},{1,5},{2,6},{3,7},{4,0},{5,1},{6,2},{7,3},{8,12},{9,13},{10,... | collective-permute-start | bytes 61448 | tf_op jit(solution)/shard_map/ppermute | solution.py:480
  11.2 1.1 %shard_map.105 = (bf16[5120,256]{1,0:T(8,128)(2,1)S(1)}, s32[10,512]{1,0:T(8,128)S(1)}, f32[30,4,512]{2,1,0:T(4,128)S(1)}, s32[1,768]{1,0:T(1,128)S(1)}, f32[8,128]{1,0:T(8,128)S(1)}, /*index=5*/f32[8,128]{1,0:T(8,128)S(1)}) custom-call(s32[1]{0:T(128)S(6)} %copy.11.count_ref, s32[10,512]{1,0:T(8,128)S(1)} %get-tuple-element.35.conn_ref, ...), custom_call_target="tpu_custom_call" | custom-call | flops 20000000 | bytes 4000000 | tf_op jit(solution)/shard_map/pallas_call | solution.py:497
  12.2 0.0 collective-permute-done.3.rest_3_
  12.2 0.0 collective-permute-done.1.rest_1_
  12.3 0.0 collective-permute-done.rest_0_
  12.3 0.0 collective-permute-done.4.rest_4_
  12.3 0.4 collective-permute-done.2.rest_2_
  12.7 2.2 %shard_map.106 = (f32[24,768]{1,0:T(8,128)S(1)}, f32[48,128]{1,0:T(8,128)S(1)}, f32[48,128]{1,0:T(8,128)S(1)}, f32[48,128]{1,0:T(8,128)S(1)}, f32[16,256]{1,0:T(...) custom-call(s32[1]{0:T(128)} %bitcast.p_ref, f32[24,768]{1,0:T(8,128)S(1)} %get-tuple-element.33.d_ref, ...), custom_call_target="tpu_custom_call" | custom-call | tf_op jit(solution)/shard_map/pallas_call | solution.py:513
  14.9 0.1 collective-permute-start.8
  15.0 0.4 %collective-permute-start.6 = (f32[48,128]{1,0:T(8,128)S(1)}, f32[48,128]{1,0:T(8,128)S(1)}, u32[]{:S(2)}, u32[]{:S(2)}) collective-permute-start(f32[48,128]{1,0:T(8,128)S(1)} %get-tuple-element.50.s0_ref), channel_id=1, source_target_pairs={{0,1},{1,2},{2,0},{3,4},{4,3},{5,6},{6,5},{7,8},{8,7},{9,10},{10,9... | collective-permute-start | bytes 73736 | tf_op jit(solution)/shard_map/ppermute | solution.py:480
  15.5 1.3 %collective-permute-start.5 = (f32[48,128]{1,0:T(8,128)S(1)}, f32[48,128]{1,0:T(8,128)S(1)}, u32[]{:S(2)}, u32[]{:S(2)}) collective-permute-start(f32[48,128]{1,0:T(8,128)S(1)} %get-tuple-element.50.s0_ref), channel_id=1, source_target_pairs={{0,1},{1,0},{2,3},{3,2},{4,5},{5,4},{6,7},{7,6},{8,9},{9,8},{10,11... | collective-permute-start | bytes 73736 | tf_op jit(solution)/shard_map/ppermute | solution.py:480
  16.7 2.6 %collective-permute-start.9 = (f32[48,128]{1,0:T(8,128)S(1)}, f32[48,128]{1,0:T(8,128)S(1)}, u32[]{:S(2)}, u32[]{:S(2)}) collective-permute-start(f32[48,128]{1,0:T(8,128)S(1)} %get-tuple-element.51.s1_ref), channel_id=1, source_target_pairs={{0,16},{1,17},{2,18},{3,19},{4,20},{5,21},{6,22},{7,23},{8,24},{9,... | collective-permute-start | bytes 73736 | tf_op jit(solution)/shard_map/ppermute | solution.py:480
  19.3 0.8 %collective-permute-start.7 = (f32[48,128]{1,0:T(8,128)S(1)}, f32[48,128]{1,0:T(8,128)S(1)}, u32[]{:S(2)}, u32[]{:S(2)}) collective-permute-start(f32[48,128]{1,0:T(8,128)S(1)} %get-tuple-element.51.s1_ref), channel_id=1, source_target_pairs={{0,4},{1,5},{2,6},{3,7},{4,0},{5,1},{6,2},{7,3},{8,12},{9,13},{10,... | collective-permute-start | bytes 73736 | tf_op jit(solution)/shard_map/ppermute | solution.py:480
  20.0 0.0 collective-permute-done.8.rest_3_
  20.0 0.0 collective-permute-done.6.rest_1_
  20.1 0.0 collective-permute-done.5.rest_0_
  20.1 1.4 %collective-permute-done.9.rest_4_ = f32[48,128]{1,0:T(8,128)S(1)} collective-permute-done((f32[48,128]{1,0:T(8,128)S(1)}, f32[48,128]{1,0:T(8,128)S(1)}, u32[]{:S(2)}, u32[]{:S(2)}) %collective-permute-start.9) | collective-permute-done | bytes 24608 | tf_op jit(solution)/shard_map/ppermute | solution.py:480
  21.5 1.7 %collective-permute-done.7.rest_2_ = f32[48,128]{1,0:T(8,128)S(1)} collective-permute-done((f32[48,128]{1,0:T(8,128)S(1)}, f32[48,128]{1,0:T(8,128)S(1)}, u32[]{:S(2)}, u32[]{:S(2)}) %collective-permute-start.7) | collective-permute-done | bytes 24608 | tf_op jit(solution)/shard_map/ppermute | solution.py:480
  23.1 3.1 %shard_map.107 = (f32[24,768]{1,0:T(8,128)S(1)}, f32[24,768]{1,0:T(8,128)S(1)}, f32[24,768]{1,0:T(8,128)S(1)}, f32[32,13,1,128]{3,2,1,0:T(1,128)S(1)}) custom-call(s32[1]{0:T(128)} %bitcast.p_ref, f32[24,768]{1,0:T(8,128)S(1)} %get-tuple-element.49.qpart_ref, f32[48,128]{1,0:T(8,128)S(1)} %get-tuple-element.50.s0_ref, ...), custom_call_target="tpu_custom_call" | custom-call | tf_op jit(solution)/shard_map/pallas_call | solution.py:520
  26.2 13.1 %all_to_all.5.in_ref = f32[32,13,1,128]{3,2,1,0:T(1,128)S(1)} all-to-all(f32[32,13,1,128]{3,2,1,0:T(1,128)S(1)} %get-tuple-element.58), channel_id=1, replica_groups=mesh['dom'=32] {'dom'}, dimensions={0} | all-to-all | bytes 425984 | tf_op jit(solution)/shard_map/all_to_all | solution.py:526
  39.4 0.9 %shard_map.108 = (f32[24,768]{1,0:T(8,128)}, f32[24,768]{1,0:T(8,128)}) custom-call(s32[1]{0:T(128)} %bitcast.p_ref, f32[32,13,1,128]{3,2,1,0:T(1,128)S(1)} %all_to_all.5.in_ref, f32[8,128]{1,0:T(8,128)S(1)} %get-tuple-element.53.scale_ref, f32[24,768]{1,0:T(8,128)S(1)} %get-tuple-element.37.rhs_ref, f32[24,768]{1,0:T(8,128)S(1)} %get-tuple-element.33.d_ref, ...), custom_call_target="tpu_custom_call" | custom-call | tf_op jit(solution)/shard_map/pallas_call | solution.py:527
Async XLA Ops:
  1.8 10.5 %collective-permute-start.3 = (f32[40,128]{1,0:T(8,128)S(1)}, f32[40,128]{1,0:T(8,128)S(1)}, u32[]{:S(2)}, u32[]{:S(2)}) collective-permute-start(f32[40,128]{1,0:T(8,128)S(1)} %get-tuple-element.48), channel_id=1, source_target_pairs={{0,3},{1,0},{2,1},{3,2},{4,8},{5,9},{6,10},{7,11},{8,4},{9,5},{10,... | collective-permute-start | bytes 61448 | tf_op jit(solution)/shard_map/ppermute | solution.py:480
  4.2 8.1 %collective-permute-start.1 = (f32[40,128]{1,0:T(8,128)S(1)}, f32[40,128]{1,0:T(8,128)S(1)}, u32[]{:S(2)}, u32[]{:S(2)}) collective-permute-start(f32[40,128]{1,0:T(8,128)S(1)} %get-tuple-element.46), channel_id=1, source_target_pairs={{0,1},{1,2},{2,0},{3,4},{4,3},{5,6},{6,5},{7,8},{8,7},{9,10},{10,9... | collective-permute-start | bytes 61448 | tf_op jit(solution)/shard_map/ppermute | solution.py:480
  4.2 8.1 %collective-permute-start = (f32[40,128]{1,0:T(8,128)S(1)}, f32[40,128]{1,0:T(8,128)S(1)}, u32[]{:S(2)}, u32[]{:S(2)}) collective-permute-start(f32[40,128]{1,0:T(8,128)S(1)} %get-tuple-element.46), channel_id=1, source_target_pairs={{0,1},{1,0},{2,3},{3,2},{4,5},{5,4},{6,7},{7,6},{8,9},{9,8},{10,11... | collective-permute-start | bytes 61448 | tf_op jit(solution)/shard_map/ppermute | solution.py:480
  4.9 7.3 %collective-permute-start.4 = (f32[40,128]{1,0:T(8,128)S(1)}, f32[40,128]{1,0:T(8,128)S(1)}, u32[]{:S(2)}, u32[]{:S(2)}) collective-permute-start(f32[40,128]{1,0:T(8,128)S(1)} %get-tuple-element.47), channel_id=1, source_target_pairs={{0,16},{1,17},{2,18},{3,19},{4,20},{5,21},{6,22},{7,23},{8,24},{9,... | collective-permute-start | bytes 61448 | tf_op jit(solution)/shard_map/ppermute | solution.py:480
  8.9 3.8 %collective-permute-start.2 = (f32[40,128]{1,0:T(8,128)S(1)}, f32[40,128]{1,0:T(8,128)S(1)}, u32[]{:S(2)}, u32[]{:S(2)}) collective-permute-start(f32[40,128]{1,0:T(8,128)S(1)} %get-tuple-element.47), channel_id=1, source_target_pairs={{0,4},{1,5},{2,6},{3,7},{4,0},{5,1},{6,2},{7,3},{8,12},{9,13},{10,... | collective-permute-start | bytes 61448 | tf_op jit(solution)/shard_map/ppermute | solution.py:480
  14.9 5.1 %collective-permute-start.8 = (f32[48,128]{1,0:T(8,128)S(1)}, f32[48,128]{1,0:T(8,128)S(1)}, u32[]{:S(2)}, u32[]{:S(2)}) collective-permute-start(f32[48,128]{1,0:T(8,128)S(1)} %get-tuple-element.57), channel_id=1, source_target_pairs={{0,3},{1,0},{2,1},{3,2},{4,8},{5,9},{6,10},{7,11},{8,4},{9,5},{10,... | collective-permute-start | bytes 73736 | tf_op jit(solution)/shard_map/ppermute | solution.py:480
  15.0 5.0 %collective-permute-start.6 = (f32[48,128]{1,0:T(8,128)S(1)}, f32[48,128]{1,0:T(8,128)S(1)}, u32[]{:S(2)}, u32[]{:S(2)}) collective-permute-start(f32[48,128]{1,0:T(8,128)S(1)} %get-tuple-element.50.s0_ref), channel_id=1, source_target_pairs={{0,1},{1,2},{2,0},{3,4},{4,3},{5,6},{6,5},{7,8},{8,7},{9,10},{10,9... | collective-permute-start | bytes 73736 | tf_op jit(solution)/shard_map/ppermute | solution.py:480
  15.5 4.6 %collective-permute-start.5 = (f32[48,128]{1,0:T(8,128)S(1)}, f32[48,128]{1,0:T(8,128)S(1)}, u32[]{:S(2)}, u32[]{:S(2)}) collective-permute-start(f32[48,128]{1,0:T(8,128)S(1)} %get-tuple-element.50.s0_ref), channel_id=1, source_target_pairs={{0,1},{1,0},{2,3},{3,2},{4,5},{5,4},{6,7},{7,6},{8,9},{9,8},{10,11... | collective-permute-start | bytes 73736 | tf_op jit(solution)/shard_map/ppermute | solution.py:480
  16.7 4.7 %collective-permute-start.9 = (f32[48,128]{1,0:T(8,128)S(1)}, f32[48,128]{1,0:T(8,128)S(1)}, u32[]{:S(2)}, u32[]{:S(2)}) collective-permute-start(f32[48,128]{1,0:T(8,128)S(1)} %get-tuple-element.51.s1_ref), channel_id=1, source_target_pairs={{0,16},{1,17},{2,18},{3,19},{4,20},{5,21},{6,22},{7,23},{8,24},{9,... | collective-permute-start | bytes 73736 | tf_op jit(solution)/shard_map/ppermute | solution.py:480
  19.3 3.8 %collective-permute-start.7 = (f32[48,128]{1,0:T(8,128)S(1)}, f32[48,128]{1,0:T(8,128)S(1)}, u32[]{:S(2)}, u32[]{:S(2)}) collective-permute-start(f32[48,128]{1,0:T(8,128)S(1)} %get-tuple-element.51.s1_ref), channel_id=1, source_target_pairs={{0,4},{1,5},{2,6},{3,7},{4,0},{5,1},{6,2},{7,3},{8,12},{9,13},{10,... | collective-permute-start | bytes 73736 | tf_op jit(solution)/shard_map/ppermute | solution.py:480

commit v5 on v4

--- a/solution.py
+++ b/solution.py
@@ -289,8 +289,14 @@
     return [jnp.broadcast_to(mass_ref[c * LANES : (c + 1) * LANES].reshape(1, LANES), (8, LANES)) for c in range(count)]
 
 
-WINDOWS = ((1, 0, 64, 0), (4, 0, 48, 1), (16, 96, 112, 1))
-WIDTHS = {1: 64, 4: 48, 16: 16}
+WINDOWS = (
+    (1, 1, 0, 0, 64),
+    (1, -1, 0, 64, 64),
+    (4, 1, 1, 0, 48),
+    (4, -1, 1, 48, 48),
+    (16, 1, 1, 96, 16),
+    (16, -1, 1, 112, 16),
+)
 
 
 def second_kernel(
@@ -320,7 +326,6 @@
     p = p_ref[0]
     own_chunks = q_ref.shape[1] // LANES
     lane = lax.broadcasted_iota(jnp.int32, (8, LANES), 1)
-    case = lax.broadcasted_iota(jnp.int32, (8, LANES), 0)
     back = [joined(p, devices, received, slice(8 * i, 8 * i + 8), lane, True) for i in range(3)]
     for c in range(own_chunks):
         for i, value in enumerate(spread(back, place_ref, c)):
@@ -360,49 +365,85 @@
             w_ref[here] = acc[i][c] + heavy
             cross.append(q_ref[here] * chunks[i][c])
             square.append(heavy * chunks[i][c])
-    tail = jnp.zeros((8, LANES), F32)
+    tail = jnp.where(lane < 120, 0.0, scale)
     for k, value in enumerate((start_ref[...], dot_ref[...], splat(lane_sum(cross)), splat(lane_sum(square)))):
-        tail = jnp.where(lane == 8 * k + case, value, tail)
-    tail = jnp.where(lane[0:1] < 32, jnp.sum(tail, axis=0, keepdims=True), scale[0:1])
+        tail = jnp.where(lane == 120 + k, value, tail)
 
     def fill(j, unused):
         for k in range(8):
-            out_ref[8 * j + k, 12, :, :] = tail
+            out_ref[8 * j + k] = tail
         return unused
 
     lax.fori_loop(0, devices // 8, fill, 0)
-    for distance, shift_plus, shift_minus, tile in WINDOWS:
-        for sign, shift in ((1, shift_plus), (-1, shift_minus)):
-            moved = [ghost[i][tile] for i in range(3)]
-            if shift:
-                moved = [pltpu.roll(m, LANES - shift, 1) for m in moved]
-            pair = jnp.where(lane < 64, moved[0], pltpu.roll(moved[1], 64, 1))
-            rest = jnp.where(lane < 64, moved[2], pltpu.roll(pltpu.roll(moved[2], 4, 0), 64, 1))
-            target = p + sign * distance
-
-            @pl.when((target >= 0) & (target < devices))
-            def _():
-                out_ref[target, 0:8, 0, :] = pair
-                out_ref[target, 8:12, 0, :] = rest[0:4]
-
-
-def final_kernel(p_ref, in_ref, scale_ref, rhs_ref, d_ref, q_ref, s_ref, wpart_ref, place_ref, x_ref, r_ref):
-    p = p_ref[0]
+
+    def pack(tile, column):
+        packed = tail
+        for i in range(3):
+            shift = (40 * i - column) % LANES
+            moved = pltpu.roll(ghost[i][tile], shift, 1) if shift else ghost[i][tile]
+            packed = jnp.where((lane >= 40 * i) & (lane < 40 * i + 40), moved, packed)
+        return packed
+
+    for distance, sign, tile, column, width in WINDOWS:
+        target = p + sign * distance
+        direct = pack(tile, column)
+        beyond = pack(tile, column + 40) if width > 40 else None
+
+        @pl.when((target >= 0) & (target < devices))
+        def _():
+            out_ref[target] = direct
+            if beyond is not None:
+                out_ref[jnp.bitwise_xor(target, 1)] = beyond
+
+
+def unpacked(in_ref, owner, devices, lane, inverse, direct):
+    back = [[jnp.zeros((8, LANES), F32) for _ in range(2)] for _ in range(3)]
+    for distance, sign, tile, column, width in WINDOWS:
+        first, size = (column, min(width, 40)) if direct else (column + 40, width - 40)
+        if size <= 0:
+            continue
+        source = owner - sign * distance
+        valid = (source >= 0) & (source < devices)
+        block = in_ref[jnp.clip(source, 0, devices - 1)]
+        ratio = splat(block[:, 124:125]) * inverse
+        inside = (lane >= first) & (lane < first + size) & valid
+        for i in range(3):
+            shift = (first - 40 * i) % LANES
+            moved = pltpu.roll(block, shift, 1) if shift else block
+            back[i][tile] = jnp.where(inside, moved * ratio, back[i][tile])
+    return [back[i][t] for t in range(2) for i in range(3)]
+
+
+def relay_kernel(p_ref, in_ref, out_ref):
     devices = in_ref.shape[0]
     lane = lax.broadcasted_iota(jnp.int32, (8, LANES), 1)
-    case = lax.broadcasted_iota(jnp.int32, (8, LANES), 0)
+    owner = jnp.bitwise_xor(p_ref[0], 1)
+    inverse = 1.0 / splat(in_ref[owner][:, 124:125])
+    for k, block in enumerate(unpacked(in_ref, owner, devices, lane, inverse, False)):
+        out_ref[8 * k : 8 * k + 8, :] = block
+
+
+def scalar_kernel(p_ref, in_ref, scale_ref, out_ref):
+    devices = in_ref.shape[0]
+    lane = lax.broadcasted_iota(jnp.int32, (8, LANES), 1)
     mine = scale_ref[...]
     inv_mine = 1.0 / mine
-    sums = None
-    for j in range(0, devices, 8):
-        rows = in_ref[j : j + 8, 12, 0, :]
-        ratio = pltpu.roll(rows, LANES - 32, 1) * inv_mine
-        rows = rows * jnp.where(lane < 16, 1.0, jnp.where(lane < 24, ratio, ratio * ratio))
-        sums = rows if j == 0 else sums + rows
-    sums = splat(jnp.sum(sums, axis=0, keepdims=True))
-    e0, d0, cross, square = (
-        splat(jnp.sum(jnp.where(lane == 8 * k + case, sums, 0.0), axis=1, keepdims=True)) for k in range(4)
-    )
+    for k, block in enumerate(unpacked(in_ref, p_ref[0], devices, lane, inv_mine, True)):
+        out_ref[8 * k : 8 * k + 8, :] = block
+
+    def term(j):
+        tile = in_ref[j]
+        ratio = pltpu.roll(tile, LANES - 4, 1) * inv_mine
+        return tile * jnp.where(lane == 122, ratio, jnp.where(lane == 123, ratio * ratio, 1.0))
+
+    def add_up(j, sums):
+        values = [term(8 * j + k) for k in range(8)]
+        while len(values) > 1:
+            values = [a + b for a, b in zip(values[::2], values[1::2])]
+        return sums + values[0]
+
+    sums = lax.fori_loop(0, devices // 8, add_up, jnp.zeros((8, LANES), F32), unroll=devices <= 64)
+    e0, d0, cross, square = (splat(sums[:, k : k + 1]) for k in range(120, 124))
     step = e0 / d0
     scaled = step * mine
     fresh = scaled * (step * cross) - e0
@@ -410,25 +451,23 @@
     more = 1.0 + beta
     bend = more * more * d0 - 2.0 * more * (scaled * cross) + scaled * (scaled * square)
     step1 = fresh / bend
-    for_d = step + step1 * more
-    for_s = step1 * scaled
-
-    zero = jnp.zeros((8, LANES), F32)
-    back = [[zero, zero] for _ in range(3)]
-    for distance, shift_plus, shift_minus, tile in WINDOWS:
-        for sign, shift in ((1, shift_plus), (-1, shift_minus)):
-            source = p - sign * distance
-            valid = (source >= 0) & (source < devices)
-            source = jnp.clip(source, 0, devices - 1)
-            pair = in_ref[source, 0:8, 0, :]
-            rest = in_ref[source, 8:12, 0, :]
-            rest = jnp.concatenate([rest, pltpu.roll(rest, 64, 1)], axis=0)
-            ratio = splat(in_ref[source, 12, :, 32:33]) * inv_mine
-            blocks = [pair, pltpu.roll(pair, 64, 1), rest]
-            inside = (lane >= shift) & (lane < shift + WIDTHS[distance]) & valid
-            for i in range(3):
-                moved = blocks[i] if shift == 0 else pltpu.roll(blocks[i], shift, 1)
-                back[i][tile] = jnp.where(inside, moved * ratio, back[i][tile])
+    out_ref[48:56, :] = step + step1 * more
+    out_ref[56:64, :] = step1 * scaled
+
+
+def final_kernel(direct_ref, relayed_ref, rhs_ref, d_ref, q_ref, s_ref, wpart_ref, place_ref, x_ref, r_ref):
+    lane = lax.broadcasted_iota(jnp.int32, (8, LANES), 1)
+    for_d = direct_ref[48:56, :]
+    for_s = direct_ref[56:64, :]
+    back = [[None, None] for _ in range(3)]
+    for t in range(2):
+        far = lane < 0
+        for _, _, tile, column, width in WINDOWS:
+            if tile == t:
+                far = far | ((lane >= column + 40) & (lane < column + width))
+        for i in range(3):
+            here = slice(24 * t + 8 * i, 24 * t + 8 * i + 8)
+            back[i][t] = jnp.where(far, relayed_ref[here, :], direct_ref[here, :])
     for c in range(rhs_ref.shape[1] // LANES):
         for i, value in enumerate(spread(back, place_ref, c)):
             here = slice(8 * i, 8 * i + 8), slice(c * LANES, (c + 1) * LANES)
@@ -519,13 +558,21 @@
     got = exchange(s0, s1, mixed)
     q, s, wpart, message = call(
         functools.partial(second_kernel, keys, devices),
-        [shape(24, own), shape(24, own), shape(24, own), shape(devices, 13, 1, LANES)],
+        [shape(24, own), shape(24, own), shape(24, own), shape(devices, 8, LANES)],
         [smem] + [vmem] * (16 + len(keys)),
         left,
     )(p, qpart, s0, s1, precond_blocks, gprec, scale, start, dot, place, *mesh_args, *got)
     message = lax.all_to_all(message, AXIS, 0, 0, tiled=True)
-    x, r = call(final_kernel, [shape(24, own), shape(24, own)], [smem] + [vmem] * 8)(
-        p, message, scale, rhs, d, q, s, wpart, place
+    (relay,) = call(relay_kernel, [tile], [smem, vmem])(p, message)
+    relayed = lax.ppermute(relay, AXIS, [(i, i ^ 1) for i in range(devices)])
+    (direct,) = call(
+        scalar_kernel,
+        [shape(64, LANES)],
+        [smem] + [vmem] * 2,
+        cost=pl.CostEstimate(flops=20_000_000, bytes_accessed=2_000_000, transcendentals=0),
+    )(p, message, scale)
+    x, r = call(final_kernel, [shape(24, own), shape(24, own)], [vmem] * 8)(
+        direct, relayed, rhs, d, q, s, wpart, place
     )
     return x.reshape(3, CASES, own), r.reshape(3, CASES, own)
 

time: 40.5 us -> 40.3 us (level)
  blocking collectives: 13.1 us -> 12 us
  waiting for transfers between devices: 3.45 us -> 4.22 us
    all_to_all x1, blocking collectives: 13.1 us -> 12 us  [local(): message = lax.all_to_all(message, AXIS, 0, 0, tiled=True)]
    ppermute x0 -> x1, waiting for transfers between devices: none -> 0.77 us  [local(): relayed = lax.ppermute(relay, AXIS, [(i, i ^ 1) for i in range(devices)])]
    pallas_call x1 -> x3, Pallas kernels: 0.93 us -> 1.05 us  [the longest x1 0.76 us: local(): call(final_kernel, [shape(24, own), shape(24, own)], [vmem] * 8)]
  transfers between devices with their start and end apart: 10 -> 11, of which waited for: 3 -> 4; matrix products, arithmetic and copies ran while one was open for 0% -> 0% of each run, Pallas kernels for 3% -> 3%
where the time goes in v5:
time: 40.3 us; the launch traced here: 40.1 us
  starting transfers between devices  14.1 us (35%)
  blocking collectives  12 us (30%)
  Pallas kernels  8.41 us (21%)
  waiting for transfers between devices  4.22 us (10%)
  between operations  1.37 us (3%)
    ppermute x10, starting transfers between devices, exchange(): lax.ppermute(mixed if key == (4, 1) else tiles[key[0]], AXIS, sorted(move...  13.9 us
    all_to_all x1, blocking collectives, local(): message = lax.all_to_all(message, AXIS, 0, 0, tiled=True)  12 us
    ppermute x10, waiting for transfers between devices, exchange(): lax.ppermute(mixed if key == (4, 1) else tiles[key[0]], AXIS, sorted(move...  3.45 us
    pallas_call x1, Pallas kernels, local(): call(functools.partial(second_kernel, keys, devices), [shape(24, own), sh...  2.91 us
    pallas_call x1, Pallas kernels, local(): call(functools.partial(first_kernel, keys, devices), [shape(24, own), til...  2.25 us
    pallas_call x1, Pallas kernels, local(): call(functools.partial(begin_kernel, devices, len(inputs)), [shape(*value...  1.13 us
    pallas_call x1, Pallas kernels, local(): call(setup_kernel, [shape(10 * elems, 256, dtype=BF16), shape(10, elems,...  1.08 us
  transfers between devices with their start and end apart: 11, of which 4 were waited for; matrix products, arithmetic and copies ran while one was open for 0% of the time, Pallas kernels for 3%

profile of v5, /device:TPU:0, one launch (start us, length us, event | category | flops | bytes accessed | tf_op | source)
XLA Modules:
  0.0 40.1 jit_solution(9097464924932752253)
XLA Ops:
  0.6 1.1 %shard_map.104 = (f32[24,768]{1,0:T(8,128)S(1)}, f32[3,3,768]{2,1,0:T(4,128)S(1)}, s32[1,256]{1,0:T(1,128)S(1)}, s32[10,512]{1,0:T(8,128)S(1)}, bf16[3,10,4,512]...) custom-call(s32[1]{0:T(128)} %bitcast.p_ref, ...), custom_call_target="tpu_custom_call" | custom-call | tf_op jit(solution)/shard_map/pallas_call | solution.py:527
  1.8 2.4 %collective-permute-start.3 = (f32[40,128]{1,0:T(8,128)S(1)}, f32[40,128]{1,0:T(8,128)S(1)}, u32[]{:S(2)}, u32[]{:S(2)}) collective-permute-start(f32[40,128]{1,0:T(8,128)S(1)} %get-tuple-element.48), channel_id=1, source_target_pairs={{0,3},{1,0},{2,1},{3,2},{4,8},{5,9},{6,10},{7,11},{8,4},{9,5},{10,... | collective-permute-start | bytes 61448 | tf_op jit(solution)/shard_map/ppermute | solution.py:519
  4.2 0.0 collective-permute-start.1
  4.2 0.7 %collective-permute-start = (f32[40,128]{1,0:T(8,128)S(1)}, f32[40,128]{1,0:T(8,128)S(1)}, u32[]{:S(2)}, u32[]{:S(2)}) collective-permute-start(f32[40,128]{1,0:T(8,128)S(1)} %get-tuple-element.46), channel_id=1, source_target_pairs={{0,1},{1,0},{2,3},{3,2},{4,5},{5,4},{6,7},{7,6},{8,9},{9,8},{10,11... | collective-permute-start | bytes 61448 | tf_op jit(solution)/shard_map/ppermute | solution.py:519
  4.9 3.9 %collective-permute-start.4 = (f32[40,128]{1,0:T(8,128)S(1)}, f32[40,128]{1,0:T(8,128)S(1)}, u32[]{:S(2)}, u32[]{:S(2)}) collective-permute-start(f32[40,128]{1,0:T(8,128)S(1)} %get-tuple-element.47), channel_id=1, source_target_pairs={{0,16},{1,17},{2,18},{3,19},{4,20},{5,21},{6,22},{7,23},{8,24},{9,... | collective-permute-start | bytes 61448 | tf_op jit(solution)/shard_map/ppermute | solution.py:519
  8.9 1.6 %collective-permute-start.2 = (f32[40,128]{1,0:T(8,128)S(1)}, f32[40,128]{1,0:T(8,128)S(1)}, u32[]{:S(2)}, u32[]{:S(2)}) collective-permute-start(f32[40,128]{1,0:T(8,128)S(1)} %get-tuple-element.47), channel_id=1, source_target_pairs={{0,4},{1,5},{2,6},{3,7},{4,0},{5,1},{6,2},{7,3},{8,12},{9,13},{10,... | collective-permute-start | bytes 61448 | tf_op jit(solution)/shard_map/ppermute | solution.py:519
  11.2 1.1 %shard_map.105 = (bf16[5120,256]{1,0:T(8,128)(2,1)S(1)}, s32[10,512]{1,0:T(8,128)S(1)}, f32[30,4,512]{2,1,0:T(4,128)S(1)}, s32[1,768]{1,0:T(1,128)S(1)}, f32[8,128]{1,0:T(8,128)S(1)}, /*index=5*/f32[8,128]{1,0:T(8,128)S(1)}) custom-call(s32[1]{0:T(128)S(6)} %copy.11.count_ref, s32[10,512]{1,0:T(8,128)S(1)} %get-tuple-element.35.conn_ref, ...), custom_call_target="tpu_custom_call" | custom-call | flops 20000000 | bytes 4000000 | tf_op jit(solution)/shard_map/pallas_call | solution.py:536
  12.2 0.0 collective-permute-done.3.rest_3_
  12.2 0.0 collective-permute-done.1.rest_1_
  12.3 0.0 collective-permute-done.rest_0_
  12.3 0.0 collective-permute-done.4.rest_4_
  12.3 0.4 collective-permute-done.2.rest_2_
  12.7 2.2 %shard_map.106 = (f32[24,768]{1,0:T(8,128)S(1)}, f32[48,128]{1,0:T(8,128)S(1)}, f32[48,128]{1,0:T(8,128)S(1)}, f32[48,128]{1,0:T(8,128)S(1)}, f32[16,256]{1,0:T(...) custom-call(s32[1]{0:T(128)} %bitcast.p_ref, f32[24,768]{1,0:T(8,128)S(1)} %get-tuple-element.33.d_ref, ...), custom_call_target="tpu_custom_call" | custom-call | tf_op jit(solution)/shard_map/pallas_call | solution.py:552
  14.9 0.1 collective-permute-start.8
  15.0 0.4 %collective-permute-start.6 = (f32[48,128]{1,0:T(8,128)S(1)}, f32[48,128]{1,0:T(8,128)S(1)}, u32[]{:S(2)}, u32[]{:S(2)}) collective-permute-start(f32[48,128]{1,0:T(8,128)S(1)} %get-tuple-element.50.s0_ref), channel_id=1, source_target_pairs={{0,1},{1,2},{2,0},{3,4},{4,3},{5,6},{6,5},{7,8},{8,7},{9,10},{10,9... | collective-permute-start | bytes 73736 | tf_op jit(solution)/shard_map/ppermute | solution.py:519
  15.5 1.3 %collective-permute-start.5 = (f32[48,128]{1,0:T(8,128)S(1)}, f32[48,128]{1,0:T(8,128)S(1)}, u32[]{:S(2)}, u32[]{:S(2)}) collective-permute-start(f32[48,128]{1,0:T(8,128)S(1)} %get-tuple-element.50.s0_ref), channel_id=1, source_target_pairs={{0,1},{1,0},{2,3},{3,2},{4,5},{5,4},{6,7},{7,6},{8,9},{9,8},{10,11... | collective-permute-start | bytes 73736 | tf_op jit(solution)/shard_map/ppermute | solution.py:519
  16.7 2.6 %collective-permute-start.9 = (f32[48,128]{1,0:T(8,128)S(1)}, f32[48,128]{1,0:T(8,128)S(1)}, u32[]{:S(2)}, u32[]{:S(2)}) collective-permute-start(f32[48,128]{1,0:T(8,128)S(1)} %get-tuple-element.51.s1_ref), channel_id=1, source_target_pairs={{0,16},{1,17},{2,18},{3,19},{4,20},{5,21},{6,22},{7,23},{8,24},{9,... | collective-permute-start | bytes 73736 | tf_op jit(solution)/shard_map/ppermute | solution.py:519
  19.3 0.8 %collective-permute-start.7 = (f32[48,128]{1,0:T(8,128)S(1)}, f32[48,128]{1,0:T(8,128)S(1)}, u32[]{:S(2)}, u32[]{:S(2)}) collective-permute-start(f32[48,128]{1,0:T(8,128)S(1)} %get-tuple-element.51.s1_ref), channel_id=1, source_target_pairs={{0,4},{1,5},{2,6},{3,7},{4,0},{5,1},{6,2},{7,3},{8,12},{9,13},{10,... | collective-permute-start | bytes 73736 | tf_op jit(solution)/shard_map/ppermute | solution.py:519
  20.0 0.0 collective-permute-done.8.rest_3_
  20.1 0.0 collective-permute-done.6.rest_1_
  20.1 0.0 collective-permute-done.5.rest_0_
  20.1 1.4 %collective-permute-done.9.rest_4_ = f32[48,128]{1,0:T(8,128)S(1)} collective-permute-done((f32[48,128]{1,0:T(8,128)S(1)}, f32[48,128]{1,0:T(8,128)S(1)}, u32[]{:S(2)}, u32[]{:S(2)}) %collective-permute-start.9) | collective-permute-done | bytes 24608 | tf_op jit(solution)/shard_map/ppermute | solution.py:519
  21.5 1.7 %collective-permute-done.7.rest_2_ = f32[48,128]{1,0:T(8,128)S(1)} collective-permute-done((f32[48,128]{1,0:T(8,128)S(1)}, f32[48,128]{1,0:T(8,128)S(1)}, u32[]{:S(2)}, u32[]{:S(2)}) %collective-permute-start.7) | collective-permute-done | bytes 24608 | tf_op jit(solution)/shard_map/ppermute | solution.py:519
  23.1 2.9 %shard_map.107 = (f32[24,768]{1,0:T(8,128)S(1)}, f32[24,768]{1,0:T(8,128)S(1)}, f32[24,768]{1,0:T(8,128)S(1)}, f32[32,8,128]{2,1,0:T(8,128)S(1)}) custom-call(s32[1]{0:T(128)} %bitcast.p_ref, f32[24,768]{1,0:T(8,128)S(1)} %get-tuple-element.49.qpart_ref, f32[48,128]{1,0:T(8,128)S(1)} %get-tuple-element.50.s0_ref, f32[48,128]{1,0:T(8,128)S(1)} %get-tuple-element.51.s1_ref, ...), custom_call_target="tpu_custom_call" | custom-call | tf_op jit(solution)/shard_map/pallas_call | solution.py:559
  26.0 12.0 %all_to_all.5.in_ref = f32[32,8,128]{2,1,0:T(8,128)S(1)} all-to-all(f32[32,8,128]{2,1,0:T(8,128)S(1)} %get-tuple-element.58), channel_id=1, replica_groups=mesh['dom'=32] {'dom'}, dimensions={0} | all-to-all | bytes 262144 | tf_op jit(solution)/shard_map/all_to_all | solution.py:565
  38.0 0.1 shard_map.109
  38.1 0.3 collective-permute-start.10
  38.4 0.2 shard_map.108.direct_ref
  38.6 0.8 %collective-permute-done.10.relayed_ref = f32[48,128]{1,0:T(8,128)S(1)} collective-permute-done((f32[48,128]{1,0:T(8,128)S(1)}, f32[48,128]{1,0:T(8,128)S(1)}, u32[]{:S(2)}, u32[]{:S(2)}) %collective-permute-start.10) | collective-permute-done | bytes 24608 | tf_op jit(solution)/shard_map/ppermute | solution.py:567
  39.4 0.8 %shard_map.110 = (f32[24,768]{1,0:T(8,128)}, f32[24,768]{1,0:T(8,128)}) custom-call(f32[64,128]{1,0:T(8,128)S(1)} %shard_map.108.direct_ref, f32[48,128]{1,0:T(8,128)S(1)} %collective-permute-done.10.relayed_ref, f32[24,768]{1,0:T(8,128)S(1)} %get-tuple-element.37.rhs_ref, f32[24,768]{1,0:T(8,128)S(1)} %get-tuple-element.33.d_ref, ...), custom_call_target="tpu_custom_call" | custom-call | tf_op jit(solution)/shard_map/pallas_call | solution.py:574
Async XLA Ops:
  1.8 10.5 %collective-permute-start.3 = (f32[40,128]{1,0:T(8,128)S(1)}, f32[40,128]{1,0:T(8,128)S(1)}, u32[]{:S(2)}, u32[]{:S(2)}) collective-permute-start(f32[40,128]{1,0:T(8,128)S(1)} %get-tuple-element.48), channel_id=1, source_target_pairs={{0,3},{1,0},{2,1},{3,2},{4,8},{5,9},{6,10},{7,11},{8,4},{9,5},{10,... | collective-permute-start | bytes 61448 | tf_op jit(solution)/shard_map/ppermute | solution.py:519
  4.2 8.1 %collective-permute-start.1 = (f32[40,128]{1,0:T(8,128)S(1)}, f32[40,128]{1,0:T(8,128)S(1)}, u32[]{:S(2)}, u32[]{:S(2)}) collective-permute-start(f32[40,128]{1,0:T(8,128)S(1)} %get-tuple-element.46), channel_id=1, source_target_pairs={{0,1},{1,2},{2,0},{3,4},{4,3},{5,6},{6,5},{7,8},{8,7},{9,10},{10,9... | collective-permute-start | bytes 61448 | tf_op jit(solution)/shard_map/ppermute | solution.py:519
  4.2 8.1 %collective-permute-start = (f32[40,128]{1,0:T(8,128)S(1)}, f32[40,128]{1,0:T(8,128)S(1)}, u32[]{:S(2)}, u32[]{:S(2)}) collective-permute-start(f32[40,128]{1,0:T(8,128)S(1)} %get-tuple-element.46), channel_id=1, source_target_pairs={{0,1},{1,0},{2,3},{3,2},{4,5},{5,4},{6,7},{7,6},{8,9},{9,8},{10,11... | collective-permute-start | bytes 61448 | tf_op jit(solution)/shard_map/ppermute | solution.py:519
  4.9 7.3 %collective-permute-start.4 = (f32[40,128]{1,0:T(8,128)S(1)}, f32[40,128]{1,0:T(8,128)S(1)}, u32[]{:S(2)}, u32[]{:S(2)}) collective-permute-start(f32[40,128]{1,0:T(8,128)S(1)} %get-tuple-element.47), channel_id=1, source_target_pairs={{0,16},{1,17},{2,18},{3,19},{4,20},{5,21},{6,22},{7,23},{8,24},{9,... | collective-permute-start | bytes 61448 | tf_op jit(solution)/shard_map/ppermute | solution.py:519
  8.9 3.8 %collective-permute-start.2 = (f32[40,128]{1,0:T(8,128)S(1)}, f32[40,128]{1,0:T(8,128)S(1)}, u32[]{:S(2)}, u32[]{:S(2)}) collective-permute-start(f32[40,128]{1,0:T(8,128)S(1)} %get-tuple-element.47), channel_id=1, source_target_pairs={{0,4},{1,5},{2,6},{3,7},{4,0},{5,1},{6,2},{7,3},{8,12},{9,13},{10,... | collective-permute-start | bytes 61448 | tf_op jit(solution)/shard_map/ppermute | solution.py:519
  14.9 5.1 %collective-permute-start.8 = (f32[48,128]{1,0:T(8,128)S(1)}, f32[48,128]{1,0:T(8,128)S(1)}, u32[]{:S(2)}, u32[]{:S(2)}) collective-permute-start(f32[48,128]{1,0:T(8,128)S(1)} %get-tuple-element.57), channel_id=1, source_target_pairs={{0,3},{1,0},{2,1},{3,2},{4,8},{5,9},{6,10},{7,11},{8,4},{9,5},{10,... | collective-permute-start | bytes 73736 | tf_op jit(solution)/shard_map/ppermute | solution.py:519
  15.0 5.0 %collective-permute-start.6 = (f32[48,128]{1,0:T(8,128)S(1)}, f32[48,128]{1,0:T(8,128)S(1)}, u32[]{:S(2)}, u32[]{:S(2)}) collective-permute-start(f32[48,128]{1,0:T(8,128)S(1)} %get-tuple-element.50.s0_ref), channel_id=1, source_target_pairs={{0,1},{1,2},{2,0},{3,4},{4,3},{5,6},{6,5},{7,8},{8,7},{9,10},{10,9... | collective-permute-start | bytes 73736 | tf_op jit(solution)/shard_map/ppermute | solution.py:519
  15.5 4.6 %collective-permute-start.5 = (f32[48,128]{1,0:T(8,128)S(1)}, f32[48,128]{1,0:T(8,128)S(1)}, u32[]{:S(2)}, u32[]{:S(2)}) collective-permute-start(f32[48,128]{1,0:T(8,128)S(1)} %get-tuple-element.50.s0_ref), channel_id=1, source_target_pairs={{0,1},{1,0},{2,3},{3,2},{4,5},{5,4},{6,7},{7,6},{8,9},{9,8},{10,11... | collective-permute-start | bytes 73736 | tf_op jit(solution)/shard_map/ppermute | solution.py:519
  16.7 4.7 %collective-permute-start.9 = (f32[48,128]{1,0:T(8,128)S(1)}, f32[48,128]{1,0:T(8,128)S(1)}, u32[]{:S(2)}, u32[]{:S(2)}) collective-permute-start(f32[48,128]{1,0:T(8,128)S(1)} %get-tuple-element.51.s1_ref), channel_id=1, source_target_pairs={{0,16},{1,17},{2,18},{3,19},{4,20},{5,21},{6,22},{7,23},{8,24},{9,... | collective-permute-start | bytes 73736 | tf_op jit(solution)/shard_map/ppermute | solution.py:519
  19.3 3.8 %collective-permute-start.7 = (f32[48,128]{1,0:T(8,128)S(1)}, f32[48,128]{1,0:T(8,128)S(1)}, u32[]{:S(2)}, u32[]{:S(2)}) collective-permute-start(f32[48,128]{1,0:T(8,128)S(1)} %get-tuple-element.51.s1_ref), channel_id=1, source_target_pairs={{0,4},{1,5},{2,6},{3,7},{4,0},{5,1},{6,2},{7,3},{8,12},{9,13},{10,... | collective-permute-start | bytes 73736 | tf_op jit(solution)/shard_map/ppermute | solution.py:519
  38.1 1.3 %collective-permute-start.10 = (f32[48,128]{1,0:T(8,128)S(1)}, f32[48,128]{1,0:T(8,128)S(1)}, u32[]{:S(2)}, u32[]{:S(2)}) collective-permute-start(f32[48,128]{1,0:T(8,128)S(1)} %shard_map.109), channel_id=1, source_target_pairs={{0,1},{1,0},{2,3},{3,2},{4,5},{5,4},{6,7},{7,6},{8,9},{9,8},{10,11... | collective-permute-start | bytes 73736 | tf_op jit(solution)/shard_map/ppermute | solution.py:567

commit v6 on v5

--- a/solution.py
+++ b/solution.py
@@ -63,28 +63,48 @@
     return head, tail
 
 
-def joined(p, devices, received, rows, lane, opposite):
+def plus_lanes(lane):
+    return [lane < 64, (lane < 48) | ((lane >= 96) & (lane < 112))]
+
+
+def pack_far(blocks, lane):
+    packed = jnp.zeros((8, LANES), F32)
+    for r, block in enumerate(blocks):
+        moved = pltpu.roll(block, (32 * r - 96) % LANES, 1)
+        packed = jnp.where((lane >= 32 * r) & (lane < 32 * r + 32), moved, packed)
+    return packed
+
+
+def joined(p, devices, received, block, lane):
+    def arrived(key):
+        if key[0] == 16:
+            shift = (96 - 32 * block) % LANES
+            return pltpu.roll(received[key][0:8, :], shift, 1) if shift else received[key][0:8, :]
+        return received[key][8 * block : 8 * block + 8, :]
+
     sides = {}
     detour = (p == 1) | (p == devices - 2)
     for distance in DISTANCES:
-        even = received[distance, 0][rows, :]
+        even = arrived((distance, 0))
         first = lax.rem(lax.div(p, distance), 2) == 0
         if (distance, 1) in received:
-            odd = received[distance, 1][rows, :]
+            odd = arrived((distance, 1))
             if distance == 1:
-                odd = jnp.where(detour, received[4, 1][rows, :], odd)
+                odd = jnp.where(detour, arrived((4, 1)), odd)
         else:
             odd = jnp.zeros_like(even)
         plus = jnp.where(p + distance < devices, jnp.where(first, even, odd), 0.0)
         minus = jnp.where(p - distance >= 0, jnp.where(first, odd, even), 0.0)
-        sides[distance] = (minus, plus) if opposite else (plus, minus)
-    tile0 = jnp.where(lane < 64, sides[1][0], sides[1][1])
-    tile1 = jnp.where(
-        lane < 48,
-        sides[4][0],
-        jnp.where(lane < 96, sides[4][1], jnp.where(lane < 112, sides[16][0], sides[16][1])),
-    )
-    return [tile0, tile1]
+        sides[distance] = plus, minus
+    tiles = []
+    for a, b in ((0, 1), (1, 0)):
+        tile1 = jnp.where(
+            lane < 48,
+            sides[4][a],
+            jnp.where(lane < 96, sides[4][b], jnp.where(lane < 112, sides[16][a], sides[16][b])),
+        )
+        tiles.append([jnp.where(lane < 64, sides[1][a], sides[1][b]), tile1])
+    return tiles
 
 
 def send_mixed(p, devices, tile0, tile1):
@@ -100,15 +120,18 @@
     return [take_lanes(chunks, row8(bids_ref, 0, t * LANES)) for t in range(2)]
 
 
-def elements(chunks, conn_ref, high_ref, wide_ref, qw_ref, lame_ref, left_ref):
+def elements(chunks, count, conn_ref, high_ref, wide_ref, qw_ref, lame_ref, hot_ref, held_ref, left_ref, sum_ref, work_ref):
     elems = conn_ref.shape[1]
-    work = jnp.zeros((8, LANES), F32)
+    for i in range(3):
+        for c, value in enumerate(chunks[i]):
+            held_ref[8 * i : 8 * i + 8, c * LANES : (c + 1) * LANES] = value
 
     def wide(k, a, q, e0):
         return jnp.broadcast_to(wide_ref[k * 10 + a, q : q + 1, e0 : e0 + LANES], (8, LANES))
 
-    for e0 in range(0, elems, LANES):
-        nodal = [take_lanes(chunks, row8(conn_ref, a, e0)) for a in range(10)]
+    def block(e0):
+        held = [split_lanes(held_ref[8 * i : 8 * i + 8, :]) for i in range(3)] if e0 else chunks
+        nodal = [take_lanes(held, row8(conn_ref, a, e0)) for a in range(10)]
         forces = [[None] * 10 for _ in range(3)]
         lam = lame_ref[0:1, e0 : e0 + LANES]
         mu = lame_ref[1:2, e0 : e0 + LANES]
@@ -141,26 +164,36 @@
             for i in range(3):
                 if a + i > 0:
                     done = done + forces[i][a] * nodal[a][i]
-        work = work + jnp.where(row8(high_ref, 0, e0) >= 0, done, 0.0)
+        done = jnp.where(row8(high_ref, 0, e0) >= 0, done, 0.0)
         for a in range(10):
             high = row8(high_ref, a, e0)
             parts = [in_two(forces[i][a]) for i in range(3)]
             for h in range(4):
                 mask = high == h
                 kept = [jnp.where(mask, parts[i][s].astype(F32), 0.0) for s in range(2) for i in range(3)]
-                at = e0 * 10 + a * LANES
-                left_ref[h * 48 : h * 48 + 48, at : at + LANES] = jnp.concatenate(kept, axis=0).astype(BF16)
-    return work
-
-
-def scatter(left_ref, hot_ref, first, last):
-    out = lax.dot_general(
-        left_ref[48 * first : 48 * last, :], hot_ref[...], (((1,), (0,)), ((), ())), preferred_element_type=F32
-    )
+                left_ref[h * 48 : h * 48 + 48, a * LANES : (a + 1) * LANES] = jnp.concatenate(kept, axis=0).astype(
+                    BF16
+                )
+        added = lax.dot_general(
+            left_ref[...],
+            hot_ref[e0 * 10 : (e0 + LANES) * 10, :],
+            (((1,), (0,)), ((), ())),
+            preferred_element_type=F32,
+        )
+        sum_ref[...] = sum_ref[...] + added if e0 else added
+        work_ref[...] = work_ref[...] + done if e0 else done
+
+    block(0)
+    for e0 in range(LANES, elems, LANES):
+        pl.when(e0 < count)(functools.partial(block, e0))
+
+
+def node_sums(sum_ref):
+    out = sum_ref[...]
     blocks = []
     for i in range(3):
         blocks.append([])
-        for h in range(last - first):
+        for h in range(4):
             at = h * 48 + i * 8
             blocks[i] += split_lanes(out[at : at + 8] + out[at + 24 : at + 32])
     return blocks
@@ -209,10 +242,14 @@
     size_ref[...] = splat(jnp.max(jnp.max(largest, axis=1, keepdims=True), axis=0, keepdims=True))
 
 
+def entry(i, j):
+    return (0, 1, 2, 1, 3, 4, 2, 4, 5)[3 * i + j]
+
+
 def begin_kernel(devices, inputs, p_ref, *rest):
     hbm = rest[:inputs]
     held = rest[inputs : 2 * inputs]
-    d_ref, t0_ref, t1_ref, mixed_ref, blocks_ref, sems = rest[2 * inputs :]
+    d_ref, t0_ref, t1_ref, mixed_ref, far_ref, blocks_ref, sems = rest[2 * inputs :]
     copies = [pltpu.make_async_copy(hbm[k], held[k], sems.at[k]) for k in range(inputs)]
     for copy in copies:
         copy.start()
@@ -227,12 +264,15 @@
             + prec_ref[i, 1:2, :] * rhs_ref[8:16, :]
             + prec_ref[i, 2:3, :] * rhs_ref[16:24, :]
         )
-        for j in range(3):
-            blocks_ref[3 * i + j : 3 * i + j + 1, :] = prec_ref[i, j : j + 1, :]
+        for j in range(i, 3):
+            k = entry(i, j)
+            blocks_ref[k : k + 1, :] = prec_ref[i, j : j + 1, :]
     rows = [split_lanes(d_ref[8 * i : 8 * i + 8, :]) for i in range(3)]
-    rows += [split_lanes(blocks_ref[8 * i : 8 * i + 8, :]) for i in range(2)]
+    rows.append(split_lanes(blocks_ref[...]))
     tiles = boundary_values(rows, bids_ref)
-    for r in range(5):
+    far_ref[...] = jnp.zeros_like(far_ref)
+    far_ref[0:8, :] = pack_far(tiles[1], lax.broadcasted_iota(jnp.int32, (8, LANES), 1))
+    for r in range(4):
         here = slice(8 * r, 8 * r + 8)
         t0_ref[here, :] = tiles[0][r]
         t1_ref[here, :] = tiles[1][r]
@@ -242,25 +282,25 @@
 
 
 def first_kernel(
-    keys, devices, p_ref, d_ref, bids_ref, size_ref, conn_ref, high_ref, wide_ref, qw_ref, lame_ref, hot_ref, mass_ref, *rest
+    keys, devices, p_ref, count_ref, d_ref, bids_ref, size_ref, conn_ref, high_ref, wide_ref, qw_ref, lame_ref, hot_ref, mass_ref, *rest
 ):
     received = dict(zip(keys, rest[: len(keys)]))
-    q_ref, s0_ref, s1_ref, mixed_ref, gprec_ref, scale_ref, dot_ref, left_ref = rest[len(keys) :]
+    q_ref, ghost_ref, gprec_ref, scale_ref, dot_ref, *send = rest[len(keys) : -4]
+    scratch = rest[-4:]
+    send = dict(zip(keys, send))
     p = p_ref[0]
     lane = lax.broadcasted_iota(jnp.int32, (8, LANES), 1)
     chunks = []
     for i in range(3):
-        ghost = joined(p, devices, received, slice(8 * i, 8 * i + 8), lane, False)
-        chunks.append(split_lanes(d_ref[8 * i : 8 * i + 8, :]) + ghost)
+        chunks.append(split_lanes(d_ref[8 * i : 8 * i + 8, :]) + joined(p, devices, received, i, lane)[0])
     largest = size_ref[...]
-    for r in range(2):
-        tiles = joined(p, devices, received, slice(24 + 8 * r, 32 + 8 * r), lane, False)
-        for t in range(2):
-            gprec_ref[8 * r : 8 * r + 8, t * LANES : (t + 1) * LANES] = tiles[t]
-            largest = jnp.maximum(largest, jnp.abs(tiles[t]))
+    for t, tile in enumerate(joined(p, devices, received, 3, lane)[0]):
+        gprec_ref[:, t * LANES : (t + 1) * LANES] = tile
+        largest = jnp.maximum(largest, jnp.abs(tile))
     scale_ref[...] = splat(jnp.max(jnp.max(largest, axis=1, keepdims=True), axis=0, keepdims=True))
-    work = elements(chunks, conn_ref, high_ref, wide_ref, qw_ref, lame_ref, left_ref)
-    acc = scatter(left_ref, hot_ref, 0, 4)
+    elements(chunks, count_ref[0], conn_ref, high_ref, wide_ref, qw_ref, lame_ref, hot_ref, *scratch)
+    acc = node_sums(scratch[2])
+    work = scratch[3][...]
     own_chunks = d_ref.shape[1] // LANES
     mass = mass_rows(mass_ref)
     dots = [work]
@@ -272,13 +312,30 @@
             partial[i].append(acc[i][c] + heavy)
             dots.append(heavy * chunks[i][c])
     tiles = boundary_values(partial, bids_ref)
-    for i in range(3):
-        send = [acc[i][own_chunks], acc[i][own_chunks + 1]], [tiles[0][i], tiles[1][i]]
-        for part, (tile0, tile1) in enumerate(send):
-            here = slice(24 * part + 8 * i, 24 * part + 8 * i + 8)
-            s0_ref[here, :] = tile0
-            s1_ref[here, :] = tile1
-            mixed_ref[here, :] = send_mixed(p, devices, tile0, tile1)
+    higher = plus_lanes(lane)
+    message = {}
+    for key in keys:
+        distance, parity = key
+        t = 0 if distance == 1 else 1
+        first = lax.rem(lax.div(p, distance), 2) == parity
+        message[key] = []
+        for i in range(3):
+            mine, theirs = acc[i][own_chunks + t], tiles[t][i]
+            upward = jnp.where(higher[t], mine, theirs)
+            downward = jnp.where(higher[t], theirs, mine)
+            message[key].append(jnp.where(first, upward, downward))
+    message[4, 1] = [send_mixed(p, devices, a, b) for a, b in zip(message[1, 1], message[4, 1])]
+    for key in keys:
+        if key[0] == 16:
+            send[key][...] = jnp.zeros_like(send[key])
+            send[key][0:8, :] = pack_far(message[key], lane)
+            continue
+        for i in range(3):
+            send[key][8 * i : 8 * i + 8, :] = message[key][i]
+    for i in range(3):
+        for t in range(2):
+            here = slice(24 * t + 8 * i, 24 * t + 8 * i + 8)
+            ghost_ref[here, :] = acc[i][own_chunks + t]
         for c in range(own_chunks):
             q_ref[8 * i : 8 * i + 8, c * LANES : (c + 1) * LANES] = partial[i][c]
     dot_ref[...] = splat(lane_sum(dots))
@@ -303,9 +360,9 @@
     keys,
     devices,
     p_ref,
+    count_ref,
     qpart_ref,
-    s0_ref,
-    s1_ref,
+    ghost_ref,
     prec_ref,
     gprec_ref,
     scale_ref,
@@ -322,11 +379,12 @@
     *rest,
 ):
     received = dict(zip(keys, rest[: len(keys)]))
-    q_ref, s_ref, w_ref, out_ref, left_ref = rest[len(keys) :]
+    q_ref, s_ref, w_ref, out_ref, *scratch = rest[len(keys) :]
     p = p_ref[0]
     own_chunks = q_ref.shape[1] // LANES
     lane = lax.broadcasted_iota(jnp.int32, (8, LANES), 1)
-    back = [joined(p, devices, received, slice(8 * i, 8 * i + 8), lane, True) for i in range(3)]
+    swapped = [joined(p, devices, received, i, lane) for i in range(3)]
+    back = [both[1] for both in swapped]
     for c in range(own_chunks):
         for i, value in enumerate(spread(back, place_ref, c)):
             here = slice(8 * i, 8 * i + 8), slice(c * LANES, (c + 1) * LANES)
@@ -335,8 +393,9 @@
     inverse = (1.0 / scale)[0:1, 0:1]
     ghost_q = []
     for i in range(3):
-        tiles = joined(p, devices, received, slice(24 + 8 * i, 32 + 8 * i), lane, False)
-        ghost_q.append([s0_ref[8 * i : 8 * i + 8, :] + tiles[0], s1_ref[8 * i : 8 * i + 8, :] + tiles[1]])
+        ghost_q.append(
+            [ghost_ref[24 * t + 8 * i : 24 * t + 8 * i + 8, :] + swapped[i][0][t] for t in range(2)]
+        )
     chunks = []
     for i in range(3):
         value = (
@@ -349,11 +408,13 @@
         for t in range(2):
             total = None
             for j in range(3):
-                term = (gprec_ref[3 * i + j : 3 * i + j + 1, t * LANES : (t + 1) * LANES] * inverse) * ghost_q[j][t]
+                k = entry(i, j)
+                term = (gprec_ref[k : k + 1, t * LANES : (t + 1) * LANES] * inverse) * ghost_q[j][t]
                 total = term if j == 0 else total + term
             chunks[i].append(total)
-    work = elements(chunks, conn_ref, high_ref, wide_ref, qw_ref, lame_ref, left_ref)
-    acc = scatter(left_ref, hot_ref, 0, 4)
+    elements(chunks, count_ref[0], conn_ref, high_ref, wide_ref, qw_ref, lame_ref, hot_ref, *scratch)
+    acc = node_sums(scratch[2])
+    work = scratch[3][...]
     ghost = [acc[i][own_chunks:] for i in range(3)]
     mass = mass_rows(mass_ref)
     cross = []
@@ -513,26 +574,24 @@
             compiler_params=pltpu.CompilerParams(vmem_limit_bytes=24 << 20),
         )
 
-    def exchange(tile0, tile1, mixed):
-        tiles = {1: tile0, 4: tile1, 16: tile1}
-        return [
-            lax.ppermute(mixed if key == (4, 1) else tiles[key[0]], AXIS, sorted(moves[key].items())) for key in keys
-        ]
-
-    tile = shape(40, LANES)
+    def exchange(tiles):
+        return [lax.ppermute(tiles[key], AXIS, sorted(moves[key].items())) for key in keys]
+
+    tile = shape(32, LANES)
+    row = shape(8, LANES)
     inputs = [
         pltpu.with_memory_space_constraint(value, pltpu.HBM)
         for value in (rhs, precond_blocks, bids, connectivity, grads, quad_weight, lame_moduli, mass_diag)
     ]
-    *held, d, t0, t1, mixed = call(
+    *held, d, t0, t1, mixed, far = call(
         functools.partial(begin_kernel, devices, len(inputs)),
-        [shape(*value.shape, dtype=value.dtype) for value in inputs] + [shape(24, own), tile, tile, tile],
+        [shape(*value.shape, dtype=value.dtype) for value in inputs] + [shape(24, own), tile, tile, tile, shape(32, LANES)],
         [smem] + [hbm] * len(inputs),
-        [pltpu.VMEM((16, own), F32), pltpu.SemaphoreType.DMA((len(inputs),))],
+        [pltpu.VMEM((8, own), F32), pltpu.SemaphoreType.DMA((len(inputs),))],
     )(pltpu.with_memory_space_constraint(p, pltpu.SMEM), *inputs)
     rhs, precond_blocks, bids, connectivity, grads, quad_weight, lame_moduli, mass_diag = held
-    got = exchange(t0, t1, mixed)
-    row = shape(8, LANES)
+    kind = {1: t0, 4: t1, 16: far}
+    got = exchange({key: mixed if key == (4, 1) else kind[key[0]] for key in keys})
     hot, high, wide, place, start, size = call(
         setup_kernel,
         [
@@ -547,21 +606,27 @@
         cost=pl.CostEstimate(flops=20_000_000, bytes_accessed=4_000_000, transcendentals=0),
     )(elem_count, connectivity, bids, grads, rhs, d, precond_blocks)
     mesh_args = (connectivity, high, wide, quad_weight, lame_moduli, hot, mass_diag)
-    left = [pltpu.VMEM((192, 10 * elems), BF16)]
+    left = [
+        pltpu.VMEM((24, own + boundary_ids.shape[0]), F32),
+        pltpu.VMEM((192, 10 * LANES), BF16),
+        pltpu.VMEM((192, 256), F32),
+        pltpu.VMEM((8, LANES), F32),
+    ]
     tile = shape(48, LANES)
-    qpart, s0, s1, mixed, gprec, scale, dot = call(
+    qpart, ghost, gprec, scale, dot, *send = call(
         functools.partial(first_kernel, keys, devices),
-        [shape(24, own), tile, tile, tile, shape(16, 2 * LANES), row, row],
-        [smem] + [vmem] * (10 + len(keys)),
+        [shape(24, own), tile, shape(8, 2 * LANES), row, row]
+        + [shape(8 if key[0] == 16 else 24, LANES) for key in keys],
+        [smem, smem] + [vmem] * (10 + len(keys)),
         left,
-    )(p, d, bids, size, *mesh_args, *got)
-    got = exchange(s0, s1, mixed)
+    )(p, elem_count, d, bids, size, *mesh_args, *got)
+    got = exchange(dict(zip(keys, send)))
     q, s, wpart, message = call(
         functools.partial(second_kernel, keys, devices),
         [shape(24, own), shape(24, own), shape(24, own), shape(devices, 8, LANES)],
-        [smem] + [vmem] * (16 + len(keys)),
+        [smem, smem] + [vmem] * (15 + len(keys)),
         left,
-    )(p, qpart, s0, s1, precond_blocks, gprec, scale, start, dot, place, *mesh_args, *got)
+    )(p, elem_count, qpart, ghost, precond_blocks, gprec, scale, start, dot, place, *mesh_args, *got)
     message = lax.all_to_all(message, AXIS, 0, 0, tiled=True)
     (relay,) = call(relay_kernel, [tile], [smem, vmem])(p, message)
     relayed = lax.ppermute(relay, AXIS, [(i, i ^ 1) for i in range(devices)])

time: 40.3 us -> 39.4 us (0.978)
  starting transfers between devices: 14.1 us -> 16.7 us
  Pallas kernels: 8.41 us -> 5.98 us
  waiting for transfers between devices: 4.22 us -> 2.87 us
  blocking collectives: 12 us -> 12.5 us
    ppermute x10, starting transfers between devices: 13.9 us -> 16.4 us  [exchange(): lax.ppermute(tiles[key], AXIS, sorted(moves[key].items()))]
    ppermute x10, waiting for transfers between devices: 3.45 us -> 2.1 us  [exchange(): lax.ppermute(tiles[key], AXIS, sorted(moves[key].items()))]
    pallas_call x1, Pallas kernels: 2.91 us -> 1.59 us  [local(): call(functools.partial(second_kernel, keys, devices), [shape(24, own), sh...]
    pallas_call x1, Pallas kernels: 2.25 us -> 1.1 us  [local(): call(functools.partial(first_kernel, keys, devices), [shape(24, own), til...]
    all_to_all x1, blocking collectives: 12 us -> 12.5 us  [local(): message = lax.all_to_all(message, AXIS, 0, 0, tiled=True)]
  transfers between devices with their start and end apart: 11 -> 11, of which waited for: 4 -> 3; matrix products, arithmetic and copies ran while one was open for 0% -> 0% of each run, Pallas kernels for 3% -> 3%
where the time goes in v6:
time: 39.4 us
  starting transfers between devices  16.7 us (42%)
  blocking collectives  12.5 us (32%)
  Pallas kernels  5.98 us (15%)
  waiting for transfers between devices  2.87 us (7%)
  between operations  1.37 us (3%)
    ppermute x10, starting transfers between devices, exchange(): lax.ppermute(tiles[key], AXIS, sorted(moves[key].items()))  16.4 us
    all_to_all x1, blocking collectives, local(): message = lax.all_to_all(message, AXIS, 0, 0, tiled=True)  12.5 us
    ppermute x10, waiting for transfers between devices, exchange(): lax.ppermute(tiles[key], AXIS, sorted(moves[key].items()))  2.1 us
    pallas_call x1, Pallas kernels, local(): call(functools.partial(second_kernel, keys, devices), [shape(24, own), sh...  1.59 us
    pallas_call x1, Pallas kernels, local(): call(functools.partial(begin_kernel, devices, len(inputs)), [shape(*value...  1.16 us
    pallas_call x1, Pallas kernels, local(): call(functools.partial(first_kernel, keys, devices), [shape(24, own), til...  1.1 us
    pallas_call x1, Pallas kernels, local(): call(setup_kernel, [shape(10 * elems, 256, dtype=BF16), shape(10, elems,...  1.08 us
  transfers between devices with their start and end apart: 11, of which 3 were waited for; matrix products, arithmetic and copies ran while one was open for 0% of the time, Pallas kernels for 3%

profile of v6, /device:TPU:0, one launch (start us, length us, event | category | flops | bytes accessed | tf_op | source)
XLA Modules:
  0.0 39.4 jit_solution(1093070051516188515)
XLA Ops:
  0.6 1.2 %shard_map.104 = (f32[24,768]{1,0:T(8,128)S(1)}, f32[3,3,768]{2,1,0:T(4,128)S(1)}, s32[1,256]{1,0:T(1,128)S(1)}, s32[10,512]{1,0:T(8,128)S(1)}, bf16[3,10,4,512]...) custom-call(s32[1]{0:T(128)} %bitcast.p_ref, ...), custom_call_target="tpu_custom_call" | custom-call | tf_op jit(solution)/shard_map/pallas_call | solution.py:586
  1.8 3.0 %collective-permute-start.2 = (f32[32,128]{1,0:T(8,128)S(1)}, f32[32,128]{1,0:T(8,128)S(1)}, u32[]{:S(2)}, u32[]{:S(2)}) collective-permute-start(f32[32,128]{1,0:T(8,128)S(1)} %get-tuple-element.51), channel_id=1, source_target_pairs={{0,4},{1,5},{2,6},{3,7},{4,0},{5,1},{6,2},{7,3},{8,12},{9,13},{10,... | collective-permute-start | bytes 49160 | tf_op jit(solution)/shard_map/ppermute | solution.py:578
  4.8 0.7 %collective-permute-start.3 = (f32[32,128]{1,0:T(8,128)S(1)}, f32[32,128]{1,0:T(8,128)S(1)}, u32[]{:S(2)}, u32[]{:S(2)}) collective-permute-start(f32[32,128]{1,0:T(8,128)S(1)} %get-tuple-element.52), channel_id=1, source_target_pairs={{0,3},{1,0},{2,1},{3,2},{4,8},{5,9},{6,10},{7,11},{8,4},{9,5},{10,... | collective-permute-start | bytes 49160 | tf_op jit(solution)/shard_map/ppermute | solution.py:578
  5.5 2.3 %collective-permute-start.4 = (f32[32,128]{1,0:T(8,128)S(1)}, f32[32,128]{1,0:T(8,128)S(1)}, u32[]{:S(2)}, u32[]{:S(2)}) collective-permute-start(f32[32,128]{1,0:T(8,128)S(1)} %get-tuple-element.53), channel_id=1, source_target_pairs={{0,16},{1,17},{2,18},{3,19},{4,20},{5,21},{6,22},{7,23},{8,24},{9,... | collective-permute-start | bytes 49160 | tf_op jit(solution)/shard_map/ppermute | solution.py:578
  7.8 0.0 collective-permute-start.1
  7.8 1.6 %collective-permute-start = (f32[32,128]{1,0:T(8,128)S(1)}, f32[32,128]{1,0:T(8,128)S(1)}, u32[]{:S(2)}, u32[]{:S(2)}) collective-permute-start(f32[32,128]{1,0:T(8,128)S(1)} %get-tuple-element.50), channel_id=1, source_target_pairs={{0,1},{1,0},{2,3},{3,2},{4,5},{5,4},{6,7},{7,6},{8,9},{9,8},{10,11... | collective-permute-start | bytes 49160 | tf_op jit(solution)/shard_map/ppermute | solution.py:578
  10.1 1.1 %shard_map.105 = (bf16[5120,256]{1,0:T(8,128)(2,1)S(1)}, s32[10,512]{1,0:T(8,128)S(1)}, f32[30,4,512]{2,1,0:T(4,128)S(1)}, s32[1,768]{1,0:T(1,128)S(1)}, f32[8,128]{1,0:T(8,128)S(1)}, /*index=5*/f32[8,128]{1,0:T(8,128)S(1)}) custom-call(s32[1]{0:T(128)S(6)} %copy.11.count_ref, s32[10,512]{1,0:T(8,128)S(1)} %get-tuple-element.39.conn_ref, ...), custom_call_target="tpu_custom_call" | custom-call | flops 20000000 | bytes 4000000 | tf_op jit(solution)/shard_map/pallas_call | solution.py:595
  11.2 0.0 collective-permute-done.2.rest_2_
  11.2 0.0 collective-permute-done.3.rest_3_
  11.2 0.0 collective-permute-done.4.rest_4_
  11.2 0.4 collective-permute-done.1.rest_1_
  11.6 0.0 collective-permute-done.rest_0_
  11.6 1.1 %shard_map.106 = (f32[24,768]{1,0:T(8,128)S(1)}, f32[48,128]{1,0:T(8,128)S(1)}, f32[8,256]{1,0:T(8,128)S(1)}, f32[8,128]{1,0:T(8,128)S(1)}, f32[8,128]{1,0:T(8,1...) custom-call(s32[1]{0:T(128)} %bitcast.p_ref, ...), custom_call_target="tpu_custom_call" | custom-call | tf_op jit(solution)/shard_map/pallas_call | solution.py:616
  12.7 0.1 collective-permute-start.5
  12.7 0.5 %collective-permute-start.6 = (f32[24,128]{1,0:T(8,128)S(1)}, f32[24,128]{1,0:T(8,128)S(1)}, u32[]{:S(2)}, u32[]{:S(2)}) collective-permute-start(f32[24,128]{1,0:T(8,128)S(1)} %get-tuple-element.62), channel_id=1, source_target_pairs={{0,1},{1,2},{2,0},{3,4},{4,3},{5,6},{6,5},{7,8},{8,7},{9,10},{10,9... | collective-permute-start | bytes 36872 | tf_op jit(solution)/shard_map/ppermute | solution.py:578
  13.2 4.2 %collective-permute-start.7 = (f32[24,128]{1,0:T(8,128)S(1)}, f32[24,128]{1,0:T(8,128)S(1)}, u32[]{:S(2)}, u32[]{:S(2)}) collective-permute-start(f32[24,128]{1,0:T(8,128)S(1)} %get-tuple-element.63), channel_id=1, source_target_pairs={{0,4},{1,5},{2,6},{3,7},{4,0},{5,1},{6,2},{7,3},{8,12},{9,13},{10,... | collective-permute-start | bytes 36872 | tf_op jit(solution)/shard_map/ppermute | solution.py:578
  17.5 0.7 %collective-permute-start.8 = (f32[24,128]{1,0:T(8,128)S(1)}, f32[24,128]{1,0:T(8,128)S(1)}, u32[]{:S(2)}, u32[]{:S(2)}) collective-permute-start(f32[24,128]{1,0:T(8,128)S(1)} %get-tuple-element.64), channel_id=1, source_target_pairs={{0,3},{1,0},{2,1},{3,2},{4,8},{5,9},{6,10},{7,11},{8,4},{9,5},{10,... | collective-permute-start | bytes 36872 | tf_op jit(solution)/shard_map/ppermute | solution.py:578
  18.2 3.3 %collective-permute-start.9 = (f32[8,128]{1,0:T(8,128)S(1)}, f32[8,128]{1,0:T(8,128)S(1)}, u32[]{:S(2)}, u32[]{:S(2)}) collective-permute-start(f32[8,128]{1,0:T(8,128)S(1)} %get-tuple-element.65), channel_id=1, source_target_pairs={{0,16},{1,17},{2,18},{3,19},{4,20},{5,21},{6,22},{7,23},{8,24},{9,... | collective-permute-start | bytes 12296 | tf_op jit(solution)/shard_map/ppermute | solution.py:578
  21.5 1.7 %collective-permute-done.9.rest_4_ = f32[8,128]{1,0:T(8,128)S(1)} collective-permute-done((f32[8,128]{1,0:T(8,128)S(1)}, f32[8,128]{1,0:T(8,128)S(1)}, u32[]{:S(2)}, u32[]{:S(2)}) %collective-permute-start.9) | collective-permute-done | bytes 4128 | tf_op jit(solution)/shard_map/ppermute | solution.py:578
  23.2 0.0 collective-permute-done.5.rest_0_
  23.2 0.0 collective-permute-done.6.rest_1_
  23.2 0.0 collective-permute-done.7.rest_2_
  23.2 0.0 collective-permute-done.8.rest_3_
  23.2 1.6 %shard_map.107 = (f32[24,768]{1,0:T(8,128)S(1)}, f32[24,768]{1,0:T(8,128)S(1)}, f32[24,768]{1,0:T(8,128)S(1)}, f32[32,8,128]{2,1,0:T(8,128)S(1)}) custom-call(s32[1]{0:T(128)} %bitcast.p_ref, s32[1]{0:T(128)S(6)} %copy.11.count_ref, f32[24,768]{1,0:T(8,128)S(1)} %get-tuple-element.54.qpart_ref, f32[48,128]{1,0:T(8,128)S(1)} %get-tuple-element.55.ghost_ref, ...), custom_call_target="tpu_custom_call" | custom-call | tf_op jit(solution)/shard_map/pallas_call | solution.py:624
  24.8 12.5 %all_to_all.5.in_ref = f32[32,8,128]{2,1,0:T(8,128)S(1)} all-to-all(f32[32,8,128]{2,1,0:T(8,128)S(1)} %get-tuple-element.66), channel_id=1, replica_groups=mesh['dom'=32] {'dom'}, dimensions={0} | all-to-all | bytes 262144 | tf_op jit(solution)/shard_map/all_to_all | solution.py:630
  37.3 0.1 shard_map.109
  37.4 0.3 collective-permute-start.10
  37.7 0.2 shard_map.108.direct_ref
  37.9 0.8 %collective-permute-done.10.relayed_ref = f32[48,128]{1,0:T(8,128)S(1)} collective-permute-done((f32[48,128]{1,0:T(8,128)S(1)}, f32[48,128]{1,0:T(8,128)S(1)}, u32[]{:S(2)}, u32[]{:S(2)}) %collective-permute-start.10) | collective-permute-done | bytes 24608 | tf_op jit(solution)/shard_map/ppermute | solution.py:632
  38.7 0.8 %shard_map.110 = (f32[24,768]{1,0:T(8,128)}, f32[24,768]{1,0:T(8,128)}) custom-call(f32[64,128]{1,0:T(8,128)S(1)} %shard_map.108.direct_ref, f32[48,128]{1,0:T(8,128)S(1)} %collective-permute-done.10.relayed_ref, f32[24,768]{1,0:T(8,128)S(1)} %get-tuple-element.41.rhs_ref, f32[24,768]{1,0:T(8,128)S(1)} %get-tuple-element.37.d_ref, ...), custom_call_target="tpu_custom_call" | custom-call | tf_op jit(solution)/shard_map/pallas_call | solution.py:639
Async XLA Ops:
  1.8 9.4 %collective-permute-start.2 = (f32[32,128]{1,0:T(8,128)S(1)}, f32[32,128]{1,0:T(8,128)S(1)}, u32[]{:S(2)}, u32[]{:S(2)}) collective-permute-start(f32[32,128]{1,0:T(8,128)S(1)} %get-tuple-element.51), channel_id=1, source_target_pairs={{0,4},{1,5},{2,6},{3,7},{4,0},{5,1},{6,2},{7,3},{8,12},{9,13},{10,... | collective-permute-start | bytes 49160 | tf_op jit(solution)/shard_map/ppermute | solution.py:578
  4.8 6.3 %collective-permute-start.3 = (f32[32,128]{1,0:T(8,128)S(1)}, f32[32,128]{1,0:T(8,128)S(1)}, u32[]{:S(2)}, u32[]{:S(2)}) collective-permute-start(f32[32,128]{1,0:T(8,128)S(1)} %get-tuple-element.52), channel_id=1, source_target_pairs={{0,3},{1,0},{2,1},{3,2},{4,8},{5,9},{6,10},{7,11},{8,4},{9,5},{10,... | collective-permute-start | bytes 49160 | tf_op jit(solution)/shard_map/ppermute | solution.py:578
  5.5 5.7 %collective-permute-start.4 = (f32[32,128]{1,0:T(8,128)S(1)}, f32[32,128]{1,0:T(8,128)S(1)}, u32[]{:S(2)}, u32[]{:S(2)}) collective-permute-start(f32[32,128]{1,0:T(8,128)S(1)} %get-tuple-element.53), channel_id=1, source_target_pairs={{0,16},{1,17},{2,18},{3,19},{4,20},{5,21},{6,22},{7,23},{8,24},{9,... | collective-permute-start | bytes 49160 | tf_op jit(solution)/shard_map/ppermute | solution.py:578
  7.8 3.7 %collective-permute-start.1 = (f32[32,128]{1,0:T(8,128)S(1)}, f32[32,128]{1,0:T(8,128)S(1)}, u32[]{:S(2)}, u32[]{:S(2)}) collective-permute-start(f32[32,128]{1,0:T(8,128)S(1)} %get-tuple-element.50), channel_id=1, source_target_pairs={{0,1},{1,2},{2,0},{3,4},{4,3},{5,6},{6,5},{7,8},{8,7},{9,10},{10,9... | collective-permute-start | bytes 49160 | tf_op jit(solution)/shard_map/ppermute | solution.py:578
  7.8 3.7 %collective-permute-start = (f32[32,128]{1,0:T(8,128)S(1)}, f32[32,128]{1,0:T(8,128)S(1)}, u32[]{:S(2)}, u32[]{:S(2)}) collective-permute-start(f32[32,128]{1,0:T(8,128)S(1)} %get-tuple-element.50), channel_id=1, source_target_pairs={{0,1},{1,0},{2,3},{3,2},{4,5},{5,4},{6,7},{7,6},{8,9},{9,8},{10,11... | collective-permute-start | bytes 49160 | tf_op jit(solution)/shard_map/ppermute | solution.py:578
  12.7 10.5 %collective-permute-start.5 = (f32[24,128]{1,0:T(8,128)S(1)}, f32[24,128]{1,0:T(8,128)S(1)}, u32[]{:S(2)}, u32[]{:S(2)}) collective-permute-start(f32[24,128]{1,0:T(8,128)S(1)} %get-tuple-element.61), channel_id=1, source_target_pairs={{0,1},{1,0},{2,3},{3,2},{4,5},{5,4},{6,7},{7,6},{8,9},{9,8},{10,11... | collective-permute-start | bytes 36872 | tf_op jit(solution)/shard_map/ppermute | solution.py:578
  12.7 10.4 %collective-permute-start.6 = (f32[24,128]{1,0:T(8,128)S(1)}, f32[24,128]{1,0:T(8,128)S(1)}, u32[]{:S(2)}, u32[]{:S(2)}) collective-permute-start(f32[24,128]{1,0:T(8,128)S(1)} %get-tuple-element.62), channel_id=1, source_target_pairs={{0,1},{1,2},{2,0},{3,4},{4,3},{5,6},{6,5},{7,8},{8,7},{9,10},{10,9... | collective-permute-start | bytes 36872 | tf_op jit(solution)/shard_map/ppermute | solution.py:578
  13.2 10.0 %collective-permute-start.7 = (f32[24,128]{1,0:T(8,128)S(1)}, f32[24,128]{1,0:T(8,128)S(1)}, u32[]{:S(2)}, u32[]{:S(2)}) collective-permute-start(f32[24,128]{1,0:T(8,128)S(1)} %get-tuple-element.63), channel_id=1, source_target_pairs={{0,4},{1,5},{2,6},{3,7},{4,0},{5,1},{6,2},{7,3},{8,12},{9,13},{10,... | collective-permute-start | bytes 36872 | tf_op jit(solution)/shard_map/ppermute | solution.py:578
  17.5 5.7 %collective-permute-start.8 = (f32[24,128]{1,0:T(8,128)S(1)}, f32[24,128]{1,0:T(8,128)S(1)}, u32[]{:S(2)}, u32[]{:S(2)}) collective-permute-start(f32[24,128]{1,0:T(8,128)S(1)} %get-tuple-element.64), channel_id=1, source_target_pairs={{0,3},{1,0},{2,1},{3,2},{4,8},{5,9},{6,10},{7,11},{8,4},{9,5},{10,... | collective-permute-start | bytes 36872 | tf_op jit(solution)/shard_map/ppermute | solution.py:578
  18.2 5.0 %collective-permute-start.9 = (f32[8,128]{1,0:T(8,128)S(1)}, f32[8,128]{1,0:T(8,128)S(1)}, u32[]{:S(2)}, u32[]{:S(2)}) collective-permute-start(f32[8,128]{1,0:T(8,128)S(1)} %get-tuple-element.65), channel_id=1, source_target_pairs={{0,16},{1,17},{2,18},{3,19},{4,20},{5,21},{6,22},{7,23},{8,24},{9,... | collective-permute-start | bytes 12296 | tf_op jit(solution)/shard_map/ppermute | solution.py:578
  37.4 1.3 %collective-permute-start.10 = (f32[48,128]{1,0:T(8,128)S(1)}, f32[48,128]{1,0:T(8,128)S(1)}, u32[]{:S(2)}, u32[]{:S(2)}) collective-permute-start(f32[48,128]{1,0:T(8,128)S(1)} %shard_map.109), channel_id=1, source_target_pairs={{0,1},{1,0},{2,3},{3,2},{4,5},{5,4},{6,7},{7,6},{8,9},{9,8},{10,11... | collective-permute-start | bytes 73736 | tf_op jit(solution)/shard_map/ppermute | solution.py:632

commit v7 on v6

--- a/solution.py
+++ b/solution.py
@@ -616,7 +616,7 @@
     qpart, ghost, gprec, scale, dot, *send = call(
         functools.partial(first_kernel, keys, devices),
         [shape(24, own), tile, shape(8, 2 * LANES), row, row]
-        + [shape(8 if key[0] == 16 else 24, LANES) for key in keys],
+        + [shape(32 if key[0] == 16 else 24, LANES) for key in keys],
         [smem, smem] + [vmem] * (10 + len(keys)),
         left,
     )(p, elem_count, d, bids, size, *mesh_args, *got)

time: 39.4 us -> 39 us (0.990)
  starting transfers between devices: 16.7 us -> 14.2 us
  blocking collectives: 12.5 us -> 14.8 us
    ppermute x10, starting transfers between devices: 16.4 us -> 13.9 us  [exchange(): lax.ppermute(tiles[key], AXIS, sorted(moves[key].items()))]
    all_to_all x1, blocking collectives: 12.5 us -> 14.8 us  [local(): message = lax.all_to_all(message, AXIS, 0, 0, tiled=True)]
  transfers between devices with their start and end apart: 11 -> 11, of which waited for: 3 -> 5; matrix products, arithmetic and copies ran while one was open for 0% -> 0% of each run, Pallas kernels for 3% -> 3%
where the time goes in v7:
time: 39 us; the launch traced here: 38.8 us
  blocking collectives  14.8 us (38%)
  starting transfers between devices  14.2 us (36%)
  Pallas kernels  5.97 us (15%)
  waiting for transfers between devices  2.55 us (7%)
  between operations  1.35 us (3%)
    all_to_all x1, blocking collectives, local(): message = lax.all_to_all(message, AXIS, 0, 0, tiled=True)  14.8 us
    ppermute x10, starting transfers between devices, exchange(): lax.ppermute(tiles[key], AXIS, sorted(moves[key].items()))  13.9 us
    ppermute x10, waiting for transfers between devices, exchange(): lax.ppermute(tiles[key], AXIS, sorted(moves[key].items()))  1.78 us
    pallas_call x1, Pallas kernels, local(): call(functools.partial(second_kernel, keys, devices), [shape(24, own), sh...  1.58 us
    pallas_call x1, Pallas kernels, local(): call(functools.partial(begin_kernel, devices, len(inputs)), [shape(*value...  1.16 us
    pallas_call x1, Pallas kernels, local(): call(functools.partial(first_kernel, keys, devices), [shape(24, own), til...  1.1 us
    pallas_call x1, Pallas kernels, local(): call(setup_kernel, [shape(10 * elems, 256, dtype=BF16), shape(10, elems,...  1.08 us
  transfers between devices with their start and end apart: 11, of which 5 were waited for; matrix products, arithmetic and copies ran while one was open for 0% of the time, Pallas kernels for 3%

profile of v7, /device:TPU:0, one launch (start us, length us, event | category | flops | bytes accessed | tf_op | source)
XLA Modules:
  0.0 38.8 jit_solution(13202422723539357642)
XLA Ops:
  0.6 1.2 %shard_map.104 = (f32[24,768]{1,0:T(8,128)S(1)}, f32[3,3,768]{2,1,0:T(4,128)S(1)}, s32[1,256]{1,0:T(1,128)S(1)}, s32[10,512]{1,0:T(8,128)S(1)}, bf16[3,10,4,512]...) custom-call(s32[1]{0:T(128)} %bitcast.p_ref, ...), custom_call_target="tpu_custom_call" | custom-call | tf_op jit(solution)/shard_map/pallas_call | solution.py:586
  1.8 3.0 %collective-permute-start.2 = (f32[32,128]{1,0:T(8,128)S(1)}, f32[32,128]{1,0:T(8,128)S(1)}, u32[]{:S(2)}, u32[]{:S(2)}) collective-permute-start(f32[32,128]{1,0:T(8,128)S(1)} %get-tuple-element.51), channel_id=1, source_target_pairs={{0,4},{1,5},{2,6},{3,7},{4,0},{5,1},{6,2},{7,3},{8,12},{9,13},{10,... | collective-permute-start | bytes 49160 | tf_op jit(solution)/shard_map/ppermute | solution.py:578
  4.8 0.7 %collective-permute-start.3 = (f32[32,128]{1,0:T(8,128)S(1)}, f32[32,128]{1,0:T(8,128)S(1)}, u32[]{:S(2)}, u32[]{:S(2)}) collective-permute-start(f32[32,128]{1,0:T(8,128)S(1)} %get-tuple-element.52), channel_id=1, source_target_pairs={{0,3},{1,0},{2,1},{3,2},{4,8},{5,9},{6,10},{7,11},{8,4},{9,5},{10,... | collective-permute-start | bytes 49160 | tf_op jit(solution)/shard_map/ppermute | solution.py:578
  5.5 2.3 %collective-permute-start.4 = (f32[32,128]{1,0:T(8,128)S(1)}, f32[32,128]{1,0:T(8,128)S(1)}, u32[]{:S(2)}, u32[]{:S(2)}) collective-permute-start(f32[32,128]{1,0:T(8,128)S(1)} %get-tuple-element.53), channel_id=1, source_target_pairs={{0,16},{1,17},{2,18},{3,19},{4,20},{5,21},{6,22},{7,23},{8,24},{9,... | collective-permute-start | bytes 49160 | tf_op jit(solution)/shard_map/ppermute | solution.py:578
  7.8 0.0 collective-permute-start.1
  7.8 1.6 %collective-permute-start = (f32[32,128]{1,0:T(8,128)S(1)}, f32[32,128]{1,0:T(8,128)S(1)}, u32[]{:S(2)}, u32[]{:S(2)}) collective-permute-start(f32[32,128]{1,0:T(8,128)S(1)} %get-tuple-element.50), channel_id=1, source_target_pairs={{0,1},{1,0},{2,3},{3,2},{4,5},{5,4},{6,7},{7,6},{8,9},{9,8},{10,11... | collective-permute-start | bytes 49160 | tf_op jit(solution)/shard_map/ppermute | solution.py:578
  10.1 1.1 %shard_map.105 = (bf16[5120,256]{1,0:T(8,128)(2,1)S(1)}, s32[10,512]{1,0:T(8,128)S(1)}, f32[30,4,512]{2,1,0:T(4,128)S(1)}, s32[1,768]{1,0:T(1,128)S(1)}, f32[8,128]{1,0:T(8,128)S(1)}, /*index=5*/f32[8,128]{1,0:T(8,128)S(1)}) custom-call(s32[1]{0:T(128)S(6)} %copy.11.count_ref, s32[10,512]{1,0:T(8,128)S(1)} %get-tuple-element.39.conn_ref, ...), custom_call_target="tpu_custom_call" | custom-call | flops 20000000 | bytes 4000000 | tf_op jit(solution)/shard_map/pallas_call | solution.py:595
  11.2 0.0 collective-permute-done.2.rest_2_
  11.2 0.0 collective-permute-done.3.rest_3_
  11.2 0.0 collective-permute-done.4.rest_4_
  11.2 0.4 collective-permute-done.1.rest_1_
  11.6 0.0 collective-permute-done.rest_0_
  11.6 1.1 %shard_map.106 = (f32[24,768]{1,0:T(8,128)S(1)}, f32[48,128]{1,0:T(8,128)S(1)}, f32[8,256]{1,0:T(8,128)S(1)}, f32[8,128]{1,0:T(8,128)S(1)}, f32[8,128]{1,0:T(8,1...) custom-call(s32[1]{0:T(128)} %bitcast.p_ref, ...), custom_call_target="tpu_custom_call" | custom-call | tf_op jit(solution)/shard_map/pallas_call | solution.py:616
  12.7 2.8 %collective-permute-start.9 = (f32[32,128]{1,0:T(8,128)S(1)}, f32[32,128]{1,0:T(8,128)S(1)}, u32[]{:S(2)}, u32[]{:S(2)}) collective-permute-start(f32[32,128]{1,0:T(8,128)S(1)} %get-tuple-element.65), channel_id=1, source_target_pairs={{0,16},{1,17},{2,18},{3,19},{4,20},{5,21},{6,22},{7,23},{8,24},{9,... | collective-permute-start | bytes 49160 | tf_op jit(solution)/shard_map/ppermute | solution.py:578
  15.4 0.0 collective-permute-start.5
  15.4 0.5 %collective-permute-start.6 = (f32[24,128]{1,0:T(8,128)S(1)}, f32[24,128]{1,0:T(8,128)S(1)}, u32[]{:S(2)}, u32[]{:S(2)}) collective-permute-start(f32[24,128]{1,0:T(8,128)S(1)} %get-tuple-element.62), channel_id=1, source_target_pairs={{0,1},{1,2},{2,0},{3,4},{4,3},{5,6},{6,5},{7,8},{8,7},{9,10},{10,9... | collective-permute-start | bytes 36872 | tf_op jit(solution)/shard_map/ppermute | solution.py:578
  16.0 1.9 %collective-permute-start.7 = (f32[24,128]{1,0:T(8,128)S(1)}, f32[24,128]{1,0:T(8,128)S(1)}, u32[]{:S(2)}, u32[]{:S(2)}) collective-permute-start(f32[24,128]{1,0:T(8,128)S(1)} %get-tuple-element.63), channel_id=1, source_target_pairs={{0,4},{1,5},{2,6},{3,7},{4,0},{5,1},{6,2},{7,3},{8,12},{9,13},{10,... | collective-permute-start | bytes 36872 | tf_op jit(solution)/shard_map/ppermute | solution.py:578
  17.8 1.1 %collective-permute-start.8 = (f32[24,128]{1,0:T(8,128)S(1)}, f32[24,128]{1,0:T(8,128)S(1)}, u32[]{:S(2)}, u32[]{:S(2)}) collective-permute-start(f32[24,128]{1,0:T(8,128)S(1)} %get-tuple-element.64), channel_id=1, source_target_pairs={{0,3},{1,0},{2,1},{3,2},{4,8},{5,9},{6,10},{7,11},{8,4},{9,5},{10,... | collective-permute-start | bytes 36872 | tf_op jit(solution)/shard_map/ppermute | solution.py:578
  18.9 0.0 collective-permute-done.5.rest_0_
  18.9 0.2 collective-permute-done.6.rest_1_
  19.1 0.5 %collective-permute-done.7.rest_2_ = f32[24,128]{1,0:T(8,128)S(1)} collective-permute-done((f32[24,128]{1,0:T(8,128)S(1)}, f32[24,128]{1,0:T(8,128)S(1)}, u32[]{:S(2)}, u32[]{:S(2)}) %collective-permute-start.7) | collective-permute-done | bytes 12320 | tf_op jit(solution)/shard_map/ppermute | solution.py:578
  19.7 0.7 %collective-permute-done.8.rest_3_ = f32[24,128]{1,0:T(8,128)S(1)} collective-permute-done((f32[24,128]{1,0:T(8,128)S(1)}, f32[24,128]{1,0:T(8,128)S(1)}, u32[]{:S(2)}, u32[]{:S(2)}) %collective-permute-start.8) | collective-permute-done | bytes 12320 | tf_op jit(solution)/shard_map/ppermute | solution.py:578
  20.3 0.0 collective-permute-done.9.rest_4_
  20.3 1.6 %shard_map.107 = (f32[24,768]{1,0:T(8,128)S(1)}, f32[24,768]{1,0:T(8,128)S(1)}, f32[24,768]{1,0:T(8,128)S(1)}, f32[32,8,128]{2,1,0:T(8,128)S(1)}) custom-call(s32[1]{0:T(128)} %bitcast.p_ref, s32[1]{0:T(128)S(6)} %copy.11.count_ref, f32[24,768]{1,0:T(8,128)S(1)} %get-tuple-element.54.qpart_ref, f32[48,128]{1,0:T(8,128)S(1)} %get-tuple-element.55.ghost_ref, ...), custom_call_target="tpu_custom_call" | custom-call | tf_op jit(solution)/shard_map/pallas_call | solution.py:624
  21.9 14.8 %all_to_all.5.in_ref = f32[32,8,128]{2,1,0:T(8,128)S(1)} all-to-all(f32[32,8,128]{2,1,0:T(8,128)S(1)} %get-tuple-element.66), channel_id=1, replica_groups=mesh['dom'=32] {'dom'}, dimensions={0} | all-to-all | bytes 262144 | tf_op jit(solution)/shard_map/all_to_all | solution.py:630
  36.7 0.1 shard_map.109
  36.8 0.3 collective-permute-start.10
  37.1 0.2 shard_map.108.direct_ref
  37.3 0.8 %collective-permute-done.10.relayed_ref = f32[48,128]{1,0:T(8,128)S(1)} collective-permute-done((f32[48,128]{1,0:T(8,128)S(1)}, f32[48,128]{1,0:T(8,128)S(1)}, u32[]{:S(2)}, u32[]{:S(2)}) %collective-permute-start.10) | collective-permute-done | bytes 24608 | tf_op jit(solution)/shard_map/ppermute | solution.py:632
  38.1 0.8 %shard_map.110 = (f32[24,768]{1,0:T(8,128)}, f32[24,768]{1,0:T(8,128)}) custom-call(f32[64,128]{1,0:T(8,128)S(1)} %shard_map.108.direct_ref, f32[48,128]{1,0:T(8,128)S(1)} %collective-permute-done.10.relayed_ref, f32[24,768]{1,0:T(8,128)S(1)} %get-tuple-element.41.rhs_ref, f32[24,768]{1,0:T(8,128)S(1)} %get-tuple-element.37.d_ref, ...), custom_call_target="tpu_custom_call" | custom-call | tf_op jit(solution)/shard_map/pallas_call | solution.py:639
Async XLA Ops:
  1.8 9.4 %collective-permute-start.2 = (f32[32,128]{1,0:T(8,128)S(1)}, f32[32,128]{1,0:T(8,128)S(1)}, u32[]{:S(2)}, u32[]{:S(2)}) collective-permute-start(f32[32,128]{1,0:T(8,128)S(1)} %get-tuple-element.51), channel_id=1, source_target_pairs={{0,4},{1,5},{2,6},{3,7},{4,0},{5,1},{6,2},{7,3},{8,12},{9,13},{10,... | collective-permute-start | bytes 49160 | tf_op jit(solution)/shard_map/ppermute | solution.py:578
  4.8 6.3 %collective-permute-start.3 = (f32[32,128]{1,0:T(8,128)S(1)}, f32[32,128]{1,0:T(8,128)S(1)}, u32[]{:S(2)}, u32[]{:S(2)}) collective-permute-start(f32[32,128]{1,0:T(8,128)S(1)} %get-tuple-element.52), channel_id=1, source_target_pairs={{0,3},{1,0},{2,1},{3,2},{4,8},{5,9},{6,10},{7,11},{8,4},{9,5},{10,... | collective-permute-start | bytes 49160 | tf_op jit(solution)/shard_map/ppermute | solution.py:578
  5.5 5.7 %collective-permute-start.4 = (f32[32,128]{1,0:T(8,128)S(1)}, f32[32,128]{1,0:T(8,128)S(1)}, u32[]{:S(2)}, u32[]{:S(2)}) collective-permute-start(f32[32,128]{1,0:T(8,128)S(1)} %get-tuple-element.53), channel_id=1, source_target_pairs={{0,16},{1,17},{2,18},{3,19},{4,20},{5,21},{6,22},{7,23},{8,24},{9,... | collective-permute-start | bytes 49160 | tf_op jit(solution)/shard_map/ppermute | solution.py:578
  7.8 3.7 %collective-permute-start.1 = (f32[32,128]{1,0:T(8,128)S(1)}, f32[32,128]{1,0:T(8,128)S(1)}, u32[]{:S(2)}, u32[]{:S(2)}) collective-permute-start(f32[32,128]{1,0:T(8,128)S(1)} %get-tuple-element.50), channel_id=1, source_target_pairs={{0,1},{1,2},{2,0},{3,4},{4,3},{5,6},{6,5},{7,8},{8,7},{9,10},{10,9... | collective-permute-start | bytes 49160 | tf_op jit(solution)/shard_map/ppermute | solution.py:578
  7.8 3.7 %collective-permute-start = (f32[32,128]{1,0:T(8,128)S(1)}, f32[32,128]{1,0:T(8,128)S(1)}, u32[]{:S(2)}, u32[]{:S(2)}) collective-permute-start(f32[32,128]{1,0:T(8,128)S(1)} %get-tuple-element.50), channel_id=1, source_target_pairs={{0,1},{1,0},{2,3},{3,2},{4,5},{5,4},{6,7},{7,6},{8,9},{9,8},{10,11... | collective-permute-start | bytes 49160 | tf_op jit(solution)/shard_map/ppermute | solution.py:578
  12.7 7.7 %collective-permute-start.9 = (f32[32,128]{1,0:T(8,128)S(1)}, f32[32,128]{1,0:T(8,128)S(1)}, u32[]{:S(2)}, u32[]{:S(2)}) collective-permute-start(f32[32,128]{1,0:T(8,128)S(1)} %get-tuple-element.65), channel_id=1, source_target_pairs={{0,16},{1,17},{2,18},{3,19},{4,20},{5,21},{6,22},{7,23},{8,24},{9,... | collective-permute-start | bytes 49160 | tf_op jit(solution)/shard_map/ppermute | solution.py:578
  15.4 3.5 %collective-permute-start.5 = (f32[24,128]{1,0:T(8,128)S(1)}, f32[24,128]{1,0:T(8,128)S(1)}, u32[]{:S(2)}, u32[]{:S(2)}) collective-permute-start(f32[24,128]{1,0:T(8,128)S(1)} %get-tuple-element.61), channel_id=1, source_target_pairs={{0,1},{1,0},{2,3},{3,2},{4,5},{5,4},{6,7},{7,6},{8,9},{9,8},{10,11... | collective-permute-start | bytes 36872 | tf_op jit(solution)/shard_map/ppermute | solution.py:578
  15.4 3.7 %collective-permute-start.6 = (f32[24,128]{1,0:T(8,128)S(1)}, f32[24,128]{1,0:T(8,128)S(1)}, u32[]{:S(2)}, u32[]{:S(2)}) collective-permute-start(f32[24,128]{1,0:T(8,128)S(1)} %get-tuple-element.62), channel_id=1, source_target_pairs={{0,1},{1,2},{2,0},{3,4},{4,3},{5,6},{6,5},{7,8},{8,7},{9,10},{10,9... | collective-permute-start | bytes 36872 | tf_op jit(solution)/shard_map/ppermute | solution.py:578
  16.0 3.7 %collective-permute-start.7 = (f32[24,128]{1,0:T(8,128)S(1)}, f32[24,128]{1,0:T(8,128)S(1)}, u32[]{:S(2)}, u32[]{:S(2)}) collective-permute-start(f32[24,128]{1,0:T(8,128)S(1)} %get-tuple-element.63), channel_id=1, source_target_pairs={{0,4},{1,5},{2,6},{3,7},{4,0},{5,1},{6,2},{7,3},{8,12},{9,13},{10,... | collective-permute-start | bytes 36872 | tf_op jit(solution)/shard_map/ppermute | solution.py:578
  17.8 2.5 %collective-permute-start.8 = (f32[24,128]{1,0:T(8,128)S(1)}, f32[24,128]{1,0:T(8,128)S(1)}, u32[]{:S(2)}, u32[]{:S(2)}) collective-permute-start(f32[24,128]{1,0:T(8,128)S(1)} %get-tuple-element.64), channel_id=1, source_target_pairs={{0,3},{1,0},{2,1},{3,2},{4,8},{5,9},{6,10},{7,11},{8,4},{9,5},{10,... | collective-permute-start | bytes 36872 | tf_op jit(solution)/shard_map/ppermute | solution.py:578
  36.8 1.3 %collective-permute-start.10 = (f32[48,128]{1,0:T(8,128)S(1)}, f32[48,128]{1,0:T(8,128)S(1)}, u32[]{:S(2)}, u32[]{:S(2)}) collective-permute-start(f32[48,128]{1,0:T(8,128)S(1)} %shard_map.109), channel_id=1, source_target_pairs={{0,1},{1,0},{2,3},{3,2},{4,5},{5,4},{6,7},{7,6},{8,9},{9,8},{10,11... | collective-permute-start | bytes 73736 | tf_op jit(solution)/shard_map/ppermute | solution.py:632

commit v8 on v6

--- a/solution.py
+++ b/solution.py
@@ -219,11 +219,16 @@
     high_ref[...] = jnp.where(is_live, conn_ref[...] >> 8, -1)
     lows = lax.broadcasted_iota(jnp.int32, (LANES, 256), 1)
     padding = jnp.zeros((6, LANES), jnp.int32)
-    for e0 in range(0, elems, LANES):
+
+    def one_hot(e0):
         index = jnp.concatenate([conn_ref[:, e0 : e0 + LANES] & 255, padding], axis=0).T
         for a in range(10):
             at = e0 * 10 + a * LANES
             hot_ref[at : at + LANES, :] = jnp.where(lows == index[:, a : a + 1], 1.0, 0.0).astype(BF16)
+
+    one_hot(0)
+    for e0 in range(LANES, elems, LANES):
+        pl.when(e0 < count_ref[0])(functools.partial(one_hot, e0))
     for k in range(3):
         for a in range(10):
             wide_ref[k * 10 + a] = grads_ref[k, a].astype(F32)

time: 39.4 us -> 39.6 us (level)
  waiting for transfers between devices: 2.87 us -> 4.25 us
  blocking collectives: 12.5 us -> 11.5 us
    ppermute x10, waiting for transfers between devices: 2.1 us -> 3.48 us  [exchange(): lax.ppermute(tiles[key], AXIS, sorted(moves[key].items()))]
    all_to_all x1, blocking collectives: 12.5 us -> 11.5 us  [local(): message = lax.all_to_all(message, AXIS, 0, 0, tiled=True)]
  transfers between devices with their start and end apart: 11 -> 11, of which waited for: 3 -> 3; matrix products, arithmetic and copies ran while one was open for 0% -> 0% of each run, Pallas kernels for 3% -> 2%
where the time goes in v8:
time: 39.6 us; the launch traced here: 39.4 us
  starting transfers between devices  16.7 us (42%)
  blocking collectives  11.5 us (29%)
  Pallas kernels  5.61 us (14%)
  waiting for transfers between devices  4.25 us (11%)
  between operations  1.36 us (3%)
    ppermute x10, starting transfers between devices, exchange(): lax.ppermute(tiles[key], AXIS, sorted(moves[key].items()))  16.4 us
    all_to_all x1, blocking collectives, local(): message = lax.all_to_all(message, AXIS, 0, 0, tiled=True)  11.5 us
    ppermute x10, waiting for transfers between devices, exchange(): lax.ppermute(tiles[key], AXIS, sorted(moves[key].items()))  3.48 us
    pallas_call x1, Pallas kernels, local(): call(functools.partial(second_kernel, keys, devices), [shape(24, own), sh...  1.58 us
    pallas_call x1, Pallas kernels, local(): call(functools.partial(begin_kernel, devices, len(inputs)), [shape(*value...  1.16 us
    pallas_call x1, Pallas kernels, local(): call(functools.partial(first_kernel, keys, devices), [shape(24, own), til...  1.1 us
  transfers between devices with their start and end apart: 11, of which 3 were waited for; matrix products, arithmetic and copies ran while one was open for 0% of the time, Pallas kernels for 2%

profile of v8, /device:TPU:0, one launch (start us, length us, event | category | flops | bytes accessed | tf_op | source)
XLA Modules:
  0.0 39.4 jit_solution(14457546522367462315)
XLA Ops:
  0.6 1.2 %shard_map.104 = (f32[24,768]{1,0:T(8,128)S(1)}, f32[3,3,768]{2,1,0:T(4,128)S(1)}, s32[1,256]{1,0:T(1,128)S(1)}, s32[10,512]{1,0:T(8,128)S(1)}, bf16[3,10,4,512]...) custom-call(s32[1]{0:T(128)} %bitcast.p_ref, ...), custom_call_target="tpu_custom_call" | custom-call | tf_op jit(solution)/shard_map/pallas_call | solution.py:591
  1.8 3.0 %collective-permute-start.2 = (f32[32,128]{1,0:T(8,128)S(1)}, f32[32,128]{1,0:T(8,128)S(1)}, u32[]{:S(2)}, u32[]{:S(2)}) collective-permute-start(f32[32,128]{1,0:T(8,128)S(1)} %get-tuple-element.51), channel_id=1, source_target_pairs={{0,4},{1,5},{2,6},{3,7},{4,0},{5,1},{6,2},{7,3},{8,12},{9,13},{10,... | collective-permute-start | bytes 49160 | tf_op jit(solution)/shard_map/ppermute | solution.py:583
  4.8 0.7 %collective-permute-start.3 = (f32[32,128]{1,0:T(8,128)S(1)}, f32[32,128]{1,0:T(8,128)S(1)}, u32[]{:S(2)}, u32[]{:S(2)}) collective-permute-start(f32[32,128]{1,0:T(8,128)S(1)} %get-tuple-element.52), channel_id=1, source_target_pairs={{0,3},{1,0},{2,1},{3,2},{4,8},{5,9},{6,10},{7,11},{8,4},{9,5},{10,... | collective-permute-start | bytes 49160 | tf_op jit(solution)/shard_map/ppermute | solution.py:583
  5.5 2.3 %collective-permute-start.4 = (f32[32,128]{1,0:T(8,128)S(1)}, f32[32,128]{1,0:T(8,128)S(1)}, u32[]{:S(2)}, u32[]{:S(2)}) collective-permute-start(f32[32,128]{1,0:T(8,128)S(1)} %get-tuple-element.53), channel_id=1, source_target_pairs={{0,16},{1,17},{2,18},{3,19},{4,20},{5,21},{6,22},{7,23},{8,24},{9,... | collective-permute-start | bytes 49160 | tf_op jit(solution)/shard_map/ppermute | solution.py:583
  7.8 0.0 collective-permute-start.1
  7.8 1.6 %collective-permute-start = (f32[32,128]{1,0:T(8,128)S(1)}, f32[32,128]{1,0:T(8,128)S(1)}, u32[]{:S(2)}, u32[]{:S(2)}) collective-permute-start(f32[32,128]{1,0:T(8,128)S(1)} %get-tuple-element.50), channel_id=1, source_target_pairs={{0,1},{1,0},{2,3},{3,2},{4,5},{5,4},{6,7},{7,6},{8,9},{9,8},{10,11... | collective-permute-start | bytes 49160 | tf_op jit(solution)/shard_map/ppermute | solution.py:583
  10.1 0.7 %shard_map.105 = (bf16[5120,256]{1,0:T(8,128)(2,1)S(1)}, s32[10,512]{1,0:T(8,128)S(1)}, f32[30,4,512]{2,1,0:T(4,128)S(1)}, s32[1,768]{1,0:T(1,128)S(1)}, f32[8,128]{1,0:T(8,128)S(1)}, /*index=5*/f32[8,128]{1,0:T(8,128)S(1)}) custom-call(s32[1]{0:T(128)S(6)} %copy.11.count_ref, s32[10,512]{1,0:T(8,128)S(1)} %get-tuple-element.39.conn_ref, ...), custom_call_target="tpu_custom_call" | custom-call | flops 20000000 | bytes 4000000 | tf_op jit(solution)/shard_map/pallas_call | solution.py:600
  10.8 0.0 collective-permute-done.2.rest_2_
  10.8 0.0 collective-permute-done.3.rest_3_
  10.8 0.0 collective-permute-done.4.rest_4_
  10.8 0.7 %collective-permute-done.1.rest_1_ = f32[32,128]{1,0:T(8,128)S(1)} collective-permute-done((f32[32,128]{1,0:T(8,128)S(1)}, f32[32,128]{1,0:T(8,128)S(1)}, u32[]{:S(2)}, u32[]{:S(2)}) %collective-permute-start.1) | collective-permute-done | bytes 16416 | tf_op jit(solution)/shard_map/ppermute | solution.py:583
  11.6 0.0 collective-permute-done.rest_0_
  11.6 1.1 %shard_map.106 = (f32[24,768]{1,0:T(8,128)S(1)}, f32[48,128]{1,0:T(8,128)S(1)}, f32[8,256]{1,0:T(8,128)S(1)}, f32[8,128]{1,0:T(8,128)S(1)}, f32[8,128]{1,0:T(8,1...) custom-call(s32[1]{0:T(128)} %bitcast.p_ref, ...), custom_call_target="tpu_custom_call" | custom-call | tf_op jit(solution)/shard_map/pallas_call | solution.py:621
  12.7 0.6 %collective-permute-start.5 = (f32[24,128]{1,0:T(8,128)S(1)}, f32[24,128]{1,0:T(8,128)S(1)}, u32[]{:S(2)}, u32[]{:S(2)}) collective-permute-start(f32[24,128]{1,0:T(8,128)S(1)} %get-tuple-element.61), channel_id=1, source_target_pairs={{0,1},{1,0},{2,3},{3,2},{4,5},{5,4},{6,7},{7,6},{8,9},{9,8},{10,11... | collective-permute-start | bytes 36872 | tf_op jit(solution)/shard_map/ppermute | solution.py:583
  13.3 0.1 collective-permute-start.6
  13.3 5.2 %collective-permute-start.7 = (f32[24,128]{1,0:T(8,128)S(1)}, f32[24,128]{1,0:T(8,128)S(1)}, u32[]{:S(2)}, u32[]{:S(2)}) collective-permute-start(f32[24,128]{1,0:T(8,128)S(1)} %get-tuple-element.63), channel_id=1, source_target_pairs={{0,4},{1,5},{2,6},{3,7},{4,0},{5,1},{6,2},{7,3},{8,12},{9,13},{10,... | collective-permute-start | bytes 36872 | tf_op jit(solution)/shard_map/ppermute | solution.py:583
  18.6 1.1 %collective-permute-start.8 = (f32[24,128]{1,0:T(8,128)S(1)}, f32[24,128]{1,0:T(8,128)S(1)}, u32[]{:S(2)}, u32[]{:S(2)}) collective-permute-start(f32[24,128]{1,0:T(8,128)S(1)} %get-tuple-element.64), channel_id=1, source_target_pairs={{0,3},{1,0},{2,1},{3,2},{4,8},{5,9},{6,10},{7,11},{8,4},{9,5},{10,... | collective-permute-start | bytes 36872 | tf_op jit(solution)/shard_map/ppermute | solution.py:583
  19.7 1.8 %collective-permute-start.9 = (f32[8,128]{1,0:T(8,128)S(1)}, f32[8,128]{1,0:T(8,128)S(1)}, u32[]{:S(2)}, u32[]{:S(2)}) collective-permute-start(f32[8,128]{1,0:T(8,128)S(1)} %get-tuple-element.65), channel_id=1, source_target_pairs={{0,16},{1,17},{2,18},{3,19},{4,20},{5,21},{6,22},{7,23},{8,24},{9,... | collective-permute-start | bytes 12296 | tf_op jit(solution)/shard_map/ppermute | solution.py:583
  21.5 2.7 %collective-permute-done.9.rest_4_ = f32[8,128]{1,0:T(8,128)S(1)} collective-permute-done((f32[8,128]{1,0:T(8,128)S(1)}, f32[8,128]{1,0:T(8,128)S(1)}, u32[]{:S(2)}, u32[]{:S(2)}) %collective-permute-start.9) | collective-permute-done | bytes 4128 | tf_op jit(solution)/shard_map/ppermute | solution.py:583
  24.2 0.0 collective-permute-done.5.rest_0_
  24.2 0.0 collective-permute-done.6.rest_1_
  24.2 0.0 collective-permute-done.7.rest_2_
  24.2 0.0 collective-permute-done.8.rest_3_
  24.2 1.6 %shard_map.107 = (f32[24,768]{1,0:T(8,128)S(1)}, f32[24,768]{1,0:T(8,128)S(1)}, f32[24,768]{1,0:T(8,128)S(1)}, f32[32,8,128]{2,1,0:T(8,128)S(1)}) custom-call(s32[1]{0:T(128)} %bitcast.p_ref, s32[1]{0:T(128)S(6)} %copy.11.count_ref, f32[24,768]{1,0:T(8,128)S(1)} %get-tuple-element.54.qpart_ref, f32[48,128]{1,0:T(8,128)S(1)} %get-tuple-element.55.ghost_ref, ...), custom_call_target="tpu_custom_call" | custom-call | tf_op jit(solution)/shard_map/pallas_call | solution.py:629
  25.8 11.5 %all_to_all.5.in_ref = f32[32,8,128]{2,1,0:T(8,128)S(1)} all-to-all(f32[32,8,128]{2,1,0:T(8,128)S(1)} %get-tuple-element.66), channel_id=1, replica_groups=mesh['dom'=32] {'dom'}, dimensions={0} | all-to-all | bytes 262144 | tf_op jit(solution)/shard_map/all_to_all | solution.py:635
  37.3 0.1 shard_map.109
  37.4 0.3 collective-permute-start.10
  37.6 0.2 shard_map.108.direct_ref
  37.8 0.8 %collective-permute-done.10.relayed_ref = f32[48,128]{1,0:T(8,128)S(1)} collective-permute-done((f32[48,128]{1,0:T(8,128)S(1)}, f32[48,128]{1,0:T(8,128)S(1)}, u32[]{:S(2)}, u32[]{:S(2)}) %collective-permute-start.10) | collective-permute-done | bytes 24608 | tf_op jit(solution)/shard_map/ppermute | solution.py:637
  38.6 0.8 %shard_map.110 = (f32[24,768]{1,0:T(8,128)}, f32[24,768]{1,0:T(8,128)}) custom-call(f32[64,128]{1,0:T(8,128)S(1)} %shard_map.108.direct_ref, f32[48,128]{1,0:T(8,128)S(1)} %collective-permute-done.10.relayed_ref, f32[24,768]{1,0:T(8,128)S(1)} %get-tuple-element.41.rhs_ref, f32[24,768]{1,0:T(8,128)S(1)} %get-tuple-element.37.d_ref, ...), custom_call_target="tpu_custom_call" | custom-call | tf_op jit(solution)/shard_map/pallas_call | solution.py:644
Async XLA Ops:
  1.8 9.0 %collective-permute-start.2 = (f32[32,128]{1,0:T(8,128)S(1)}, f32[32,128]{1,0:T(8,128)S(1)}, u32[]{:S(2)}, u32[]{:S(2)}) collective-permute-start(f32[32,128]{1,0:T(8,128)S(1)} %get-tuple-element.51), channel_id=1, source_target_pairs={{0,4},{1,5},{2,6},{3,7},{4,0},{5,1},{6,2},{7,3},{8,12},{9,13},{10,... | collective-permute-start | bytes 49160 | tf_op jit(solution)/shard_map/ppermute | solution.py:583
  4.8 6.0 %collective-permute-start.3 = (f32[32,128]{1,0:T(8,128)S(1)}, f32[32,128]{1,0:T(8,128)S(1)}, u32[]{:S(2)}, u32[]{:S(2)}) collective-permute-start(f32[32,128]{1,0:T(8,128)S(1)} %get-tuple-element.52), channel_id=1, source_target_pairs={{0,3},{1,0},{2,1},{3,2},{4,8},{5,9},{6,10},{7,11},{8,4},{9,5},{10,... | collective-permute-start | bytes 49160 | tf_op jit(solution)/shard_map/ppermute | solution.py:583
  5.5 5.3 %collective-permute-start.4 = (f32[32,128]{1,0:T(8,128)S(1)}, f32[32,128]{1,0:T(8,128)S(1)}, u32[]{:S(2)}, u32[]{:S(2)}) collective-permute-start(f32[32,128]{1,0:T(8,128)S(1)} %get-tuple-element.53), channel_id=1, source_target_pairs={{0,16},{1,17},{2,18},{3,19},{4,20},{5,21},{6,22},{7,23},{8,24},{9,... | collective-permute-start | bytes 49160 | tf_op jit(solution)/shard_map/ppermute | solution.py:583
  7.8 3.7 %collective-permute-start.1 = (f32[32,128]{1,0:T(8,128)S(1)}, f32[32,128]{1,0:T(8,128)S(1)}, u32[]{:S(2)}, u32[]{:S(2)}) collective-permute-start(f32[32,128]{1,0:T(8,128)S(1)} %get-tuple-element.50), channel_id=1, source_target_pairs={{0,1},{1,2},{2,0},{3,4},{4,3},{5,6},{6,5},{7,8},{8,7},{9,10},{10,9... | collective-permute-start | bytes 49160 | tf_op jit(solution)/shard_map/ppermute | solution.py:583
  7.8 3.7 %collective-permute-start = (f32[32,128]{1,0:T(8,128)S(1)}, f32[32,128]{1,0:T(8,128)S(1)}, u32[]{:S(2)}, u32[]{:S(2)}) collective-permute-start(f32[32,128]{1,0:T(8,128)S(1)} %get-tuple-element.50), channel_id=1, source_target_pairs={{0,1},{1,0},{2,3},{3,2},{4,5},{5,4},{6,7},{7,6},{8,9},{9,8},{10,11... | collective-permute-start | bytes 49160 | tf_op jit(solution)/shard_map/ppermute | solution.py:583
  12.7 11.5 %collective-permute-start.5 = (f32[24,128]{1,0:T(8,128)S(1)}, f32[24,128]{1,0:T(8,128)S(1)}, u32[]{:S(2)}, u32[]{:S(2)}) collective-permute-start(f32[24,128]{1,0:T(8,128)S(1)} %get-tuple-element.61), channel_id=1, source_target_pairs={{0,1},{1,0},{2,3},{3,2},{4,5},{5,4},{6,7},{7,6},{8,9},{9,8},{10,11... | collective-permute-start | bytes 36872 | tf_op jit(solution)/shard_map/ppermute | solution.py:583
  13.3 10.9 %collective-permute-start.6 = (f32[24,128]{1,0:T(8,128)S(1)}, f32[24,128]{1,0:T(8,128)S(1)}, u32[]{:S(2)}, u32[]{:S(2)}) collective-permute-start(f32[24,128]{1,0:T(8,128)S(1)} %get-tuple-element.62), channel_id=1, source_target_pairs={{0,1},{1,2},{2,0},{3,4},{4,3},{5,6},{6,5},{7,8},{8,7},{9,10},{10,9... | collective-permute-start | bytes 36872 | tf_op jit(solution)/shard_map/ppermute | solution.py:583
  13.3 10.9 %collective-permute-start.7 = (f32[24,128]{1,0:T(8,128)S(1)}, f32[24,128]{1,0:T(8,128)S(1)}, u32[]{:S(2)}, u32[]{:S(2)}) collective-permute-start(f32[24,128]{1,0:T(8,128)S(1)} %get-tuple-element.63), channel_id=1, source_target_pairs={{0,4},{1,5},{2,6},{3,7},{4,0},{5,1},{6,2},{7,3},{8,12},{9,13},{10,... | collective-permute-start | bytes 36872 | tf_op jit(solution)/shard_map/ppermute | solution.py:583
  18.6 5.6 %collective-permute-start.8 = (f32[24,128]{1,0:T(8,128)S(1)}, f32[24,128]{1,0:T(8,128)S(1)}, u32[]{:S(2)}, u32[]{:S(2)}) collective-permute-start(f32[24,128]{1,0:T(8,128)S(1)} %get-tuple-element.64), channel_id=1, source_target_pairs={{0,3},{1,0},{2,1},{3,2},{4,8},{5,9},{6,10},{7,11},{8,4},{9,5},{10,... | collective-permute-start | bytes 36872 | tf_op jit(solution)/shard_map/ppermute | solution.py:583
  19.7 4.5 %collective-permute-start.9 = (f32[8,128]{1,0:T(8,128)S(1)}, f32[8,128]{1,0:T(8,128)S(1)}, u32[]{:S(2)}, u32[]{:S(2)}) collective-permute-start(f32[8,128]{1,0:T(8,128)S(1)} %get-tuple-element.65), channel_id=1, source_target_pairs={{0,16},{1,17},{2,18},{3,19},{4,20},{5,21},{6,22},{7,23},{8,24},{9,... | collective-permute-start | bytes 12296 | tf_op jit(solution)/shard_map/ppermute | solution.py:583
  37.4 1.3 %collective-permute-start.10 = (f32[48,128]{1,0:T(8,128)S(1)}, f32[48,128]{1,0:T(8,128)S(1)}, u32[]{:S(2)}, u32[]{:S(2)}) collective-permute-start(f32[48,128]{1,0:T(8,128)S(1)} %shard_map.109), channel_id=1, source_target_pairs={{0,1},{1,0},{2,3},{3,2},{4,5},{5,4},{6,7},{7,6},{8,9},{9,8},{10,11... | collective-permute-start | bytes 73736 | tf_op jit(solution)/shard_map/ppermute | solution.py:637
